TPU v7x, 32 devices: a whole 2x2x4 slice. The times are simulated.
32 devices in a mesh: fsdp: 4 (over z), ctx: 2 (over y), tp: 4 (over x, core).
Axes of the slice: x: 2, y: 2, z: 4, core: 2. Of those that a mesh axis runs over, the one named last changes fastest.
Arguments:
- inputs: bfloat16 [8, 2048, 512], P('fsdp', ('ctx', 'tp')), may hold values from -6 to 6
- memory: bfloat16 [8, 512, 512], P('fsdp', ('ctx', 'tp')), may hold values from -6 to 6
- cotangent: bfloat16 [8, 2048, 512], P('fsdp', ('ctx', 'tp')), may hold values from -6 to 6
- positions: int32 [8, 2048], P('fsdp'), may hold values from 0 to 2047, each once within a row
- lengths: int32 [8], P('fsdp'), may hold values from 1024 to 2048, as said below
- memory_lengths: int32 [8], P('fsdp'), may hold values from 128 to 512, as said below
- query_weight: bfloat16 [512, 512], P(('fsdp', 'ctx'), 'tp'), may hold values from -0.375 to 0.375
- key_weight: bfloat16 [512, 512], P(('fsdp', 'ctx'), 'tp'), may hold values from -0.375 to 0.375
- value_weight: bfloat16 [512, 512], P(('fsdp', 'ctx'), 'tp'), may hold values from -0.25 to 0.25
- output_weight: bfloat16 [512, 512], P('tp', ('fsdp', 'ctx')), may hold values from -1 to 1
- cross_query_weight: bfloat16 [512, 512], P(('fsdp', 'ctx'), 'tp'), may hold values from -0.375 to 0.375
- cross_key_weight: bfloat16 [512, 512], P(('fsdp', 'ctx'), 'tp'), may hold values from -0.375 to 0.375
- cross_value_weight: bfloat16 [512, 512], P(('fsdp', 'ctx'), 'tp'), may hold values from -0.25 to 0.25
- cross_output_weight: bfloat16 [512, 512], P('tp', ('fsdp', 'ctx')), may hold values from -1 to 1
- expand_weight: bfloat16 [512, 2048], P(('fsdp', 'ctx'), 'tp'), may hold values from -0.25 to 0.25
- reduce_weight: bfloat16 [2048, 512], P('tp', ('fsdp', 'ctx')), may hold values from -0.1875 to 0.1875
- query_bias: float32 [512], replicated, may hold values from -1.5 to 1.5
- value_bias: float32 [512], replicated, may hold values from -1.5 to 1.5
- output_bias: float32 [512], replicated, may hold values from -1.5 to 1.5
- first_gain: float32 [512], replicated, may hold values from 0.5 to 1.5
- first_shift: float32 [512], replicated, may hold values from -1.5 to 1.5
- cross_query_bias: float32 [512], replicated, may hold values from -1.5 to 1.5
- cross_value_bias: float32 [512], replicated, may hold values from -1.5 to 1.5
- cross_output_bias: float32 [512], replicated, may hold values from -1.5 to 1.5
- second_gain: float32 [512], replicated, may hold values from 0.5 to 1.5
- second_shift: float32 [512], replicated, may hold values from -1.5 to 1.5
- expand_bias: float32 [2048], replicated, may hold values from -2.5 to 2.5
- reduce_bias: float32 [512], replicated, may hold values from -1.5 to 1.5
- third_gain: float32 [512], replicated, may hold values from 0.5 to 1.5
- third_shift: float32 [512], replicated, may hold values from -1.5 to 1.5
Outputs:
- outputs: float32 [8, 2048, 512], P('fsdp', ('ctx', 'tp'))
- input_grad: float32 [8, 2048, 512], P('fsdp', ('ctx', 'tp'))
- memory_grad: float32 [8, 512, 512], P('fsdp', ('ctx', 'tp'))
- query_weight_grad: float32 [512, 512], P(('fsdp', 'ctx'), 'tp')
- key_weight_grad: float32 [512, 512], P(('fsdp', 'ctx'), 'tp')
- value_weight_grad: float32 [512, 512], P(('fsdp', 'ctx'), 'tp')
- output_weight_grad: float32 [512, 512], P('tp', ('fsdp', 'ctx'))
- cross_query_weight_grad: float32 [512, 512], P(('fsdp', 'ctx'), 'tp')
- cross_key_weight_grad: float32 [512, 512], P(('fsdp', 'ctx'), 'tp')
- cross_value_weight_grad: float32 [512, 512], P(('fsdp', 'ctx'), 'tp')
- cross_output_weight_grad: float32 [512, 512], P('tp', ('fsdp', 'ctx'))
- expand_weight_grad: float32 [512, 2048], P(('fsdp', 'ctx'), 'tp')
- reduce_weight_grad: float32 [2048, 512], P('tp', ('fsdp', 'ctx'))
- query_bias_grad: float32 [512], replicated
- value_bias_grad: float32 [512], replicated
- output_bias_grad: float32 [512], replicated
- first_gain_grad: float32 [512], replicated
- first_shift_grad: float32 [512], replicated
- cross_query_bias_grad: float32 [512], replicated
- cross_value_bias_grad: float32 [512], replicated
- cross_output_bias_grad: float32 [512], replicated
- second_gain_grad: float32 [512], replicated
- second_shift_grad: float32 [512], replicated
- expand_bias_grad: float32 [2048], replicated
- reduce_bias_grad: float32 [512], replicated
- third_gain_grad: float32 [512], replicated
- third_shift_grad: float32 [512], replicated
Inputs may be any that keep to these rules, and one draw needn't show every extreme that they name: `lengths`: some sequence has 2048 tokens in every draw. `memory_lengths`: some memory has 512 tokens in every draw. Each row is a permutation of the positions 0 to 2047.
All inputs are finite; a program needn't handle non-finite values.
Results may differ from a plain program's by a relative error of at most 0.025.
The roundings to bfloat16 on the way count: a program that leaves them out, or rounds other values in their place, can miss the bound.
Values may be sent and summed in bfloat16 or wider, within the bound.
No kernel may reach another device: no remote copies, remote signals or barrier semaphores. Data moves between devices by JAX's collectives and lax.ppermute only.
A program may use at most 192 MiB of HBM per device.

v0:
```python
import math

import jax
import jax.numpy as jnp
from jax import lax
from jax.sharding import PartitionSpec as P

HEAD_DIM = 64
MEM = 512


EPSILON = 1e-05
NEGATIVE = -1e30


def layer_norm(values, gain, shift):
    center = values - jnp.mean(values, axis=-1, keepdims=True)
    spread = jnp.mean(center * center, axis=-1, keepdims=True)
    return center * lax.rsqrt(spread + EPSILON) * gain + shift


def norm_back(values, gain, shift, grad):
    unused, pullback = jax.vjp(layer_norm, values, gain, shift)
    return pullback(grad)


def product(left, right):
    return jnp.dot(left, right, preferred_element_type=jnp.float32)


def product_left(left, right):
    return lax.dot_general(
        left, right, (((0,), (0,)), ((), ())), preferred_element_type=jnp.float32
    )


def product_right(left, right):
    return lax.dot_general(
        left, right, (((1,), (1,)), ((), ())), preferred_element_type=jnp.float32
    )


def split_heads(values):
    return values.reshape(values.shape[0], values.shape[1] // HEAD_DIM, HEAD_DIM)


def merge_heads(values):
    return values.reshape(values.shape[0], values.shape[1] * values.shape[2])


def masked_scores(query, keys, allowed):
    scores = jnp.einsum(
        "qhd,khd->hqk", split_heads(query), split_heads(keys), preferred_element_type=jnp.float32
    )
    scores = scores / math.sqrt(HEAD_DIM)
    return jnp.where(allowed[None], scores, NEGATIVE)


def attend(query, keys, values, allowed):
    scores = masked_scores(query, keys, allowed)
    largest = jnp.max(scores, axis=-1, keepdims=True)
    total = jnp.sum(jnp.exp(scores - largest), axis=-1, keepdims=True)
    log_total = largest + jnp.log(total)
    probs = jnp.exp(scores - log_total).astype(jnp.bfloat16)
    mixed = jnp.einsum(
        "hqk,khd->qhd", probs, split_heads(values), preferred_element_type=jnp.float32
    )
    return (merge_heads(mixed).astype(jnp.bfloat16), log_total)


def attend_back(query, keys, values, allowed, log_total, grad_mixed):
    probs = jnp.exp(masked_scores(query, keys, allowed) - log_total)
    grad_heads = split_heads(grad_mixed)
    grad_probs = jnp.einsum(
        "qhd,khd->hqk", grad_heads, split_heads(values), preferred_element_type=jnp.float32
    )
    inner = jnp.sum(grad_probs * probs, axis=-1, keepdims=True)
    grad_scores = (probs * (grad_probs - inner)).astype(jnp.bfloat16)
    grad_query = jnp.einsum(
        "hqk,khd->qhd", grad_scores, split_heads(keys), preferred_element_type=jnp.float32
    )
    grad_keys = jnp.einsum(
        "hqk,qhd->khd", grad_scores, split_heads(query), preferred_element_type=jnp.float32
    )
    grad_values = jnp.einsum(
        "hqk,qhd->khd", probs.astype(jnp.bfloat16), grad_heads, preferred_element_type=jnp.float32
    )
    scale = math.sqrt(HEAD_DIM)
    return (
        merge_heads(grad_query) / scale,
        merge_heads(grad_keys) / scale,
        merge_heads(grad_values),
    )


def gather_weights(parts):
    return (
        lax.all_gather(parts[0], ("fsdp", "ctx"), axis=0, tiled=True),
        lax.all_gather(parts[1], ("fsdp", "ctx"), axis=0, tiled=True),
        lax.all_gather(parts[2], ("fsdp", "ctx"), axis=0, tiled=True),
        lax.all_gather(parts[3], ("fsdp", "ctx"), axis=1, tiled=True),
        lax.all_gather(parts[4], ("fsdp", "ctx"), axis=0, tiled=True),
        lax.all_gather(parts[5], ("fsdp", "ctx"), axis=0, tiled=True),
        lax.all_gather(parts[6], ("fsdp", "ctx"), axis=0, tiled=True),
        lax.all_gather(parts[7], ("fsdp", "ctx"), axis=1, tiled=True),
        lax.all_gather(parts[8], ("fsdp", "ctx"), axis=0, tiled=True),
        lax.all_gather(parts[9], ("fsdp", "ctx"), axis=1, tiled=True),
    )


def reduce_weights(parts):
    return (
        lax.psum_scatter(parts[0], ("fsdp", "ctx"), scatter_dimension=0, tiled=True),
        lax.psum_scatter(parts[1], ("fsdp", "ctx"), scatter_dimension=0, tiled=True),
        lax.psum_scatter(parts[2], ("fsdp", "ctx"), scatter_dimension=0, tiled=True),
        lax.psum_scatter(parts[3], ("fsdp", "ctx"), scatter_dimension=1, tiled=True),
        lax.psum_scatter(parts[4], ("fsdp", "ctx"), scatter_dimension=0, tiled=True),
        lax.psum_scatter(parts[5], ("fsdp", "ctx"), scatter_dimension=0, tiled=True),
        lax.psum_scatter(parts[6], ("fsdp", "ctx"), scatter_dimension=0, tiled=True),
        lax.psum_scatter(parts[7], ("fsdp", "ctx"), scatter_dimension=1, tiled=True),
        lax.psum_scatter(parts[8], ("fsdp", "ctx"), scatter_dimension=0, tiled=True),
        lax.psum_scatter(parts[9], ("fsdp", "ctx"), scatter_dimension=1, tiled=True),
    )


def token_rows(values):
    return lax.all_gather(values, "tp", axis=0, tiled=True)


def row_sums(values):
    return lax.psum_scatter(values, "tp", scatter_dimension=0, tiled=True)


def mix_rows(values, local_weight):
    return row_sums(product(values, local_weight))


def mix_back(values, local_weight):
    return row_sums(product_right(values, local_weight))


def add_parts(first, second):
    return tuple((left + right for left, right in zip(first, second)))


def placed(part, offset, total):
    return lax.dynamic_update_slice_in_dim(jnp.zeros((total,), jnp.float32), part, offset, 0)


def per_device(
    inputs,
    memory,
    cotangent,
    positions,
    lengths,
    memory_lengths,
    query_weight,
    key_weight,
    value_weight,
    output_weight,
    cross_query_weight,
    cross_key_weight,
    cross_value_weight,
    cross_output_weight,
    expand_weight,
    reduce_weight,
    query_bias,
    value_bias,
    output_bias,
    first_gain,
    first_shift,
    cross_query_bias,
    cross_value_bias,
    cross_output_bias,
    second_gain,
    second_shift,
    expand_bias,
    reduce_bias,
    third_gain,
    third_shift,
):
    local_parts = (
        query_weight,
        key_weight,
        value_weight,
        output_weight,
        cross_query_weight,
        cross_key_weight,
        cross_value_weight,
        cross_output_weight,
        expand_weight,
        reduce_weight,
    )
    gathered = gather_weights(local_parts)
    (
        full_query,
        full_key,
        full_value,
        full_output,
        full_cross_query,
        full_cross_key,
        full_cross_value,
        full_cross_output,
        full_expand,
        full_reduce,
    ) = gathered
    head_width = query_weight.shape[1]
    hidden_width = expand_weight.shape[1]
    width = inputs.shape[2]
    head_start = lax.axis_index("tp") * head_width
    hidden_start = lax.axis_index("tp") * hidden_width
    own_rows = inputs.shape[1]
    group_rows = own_rows * lax.axis_size("tp")
    query_start = lax.axis_index("ctx") * group_rows
    row_start = query_start + lax.axis_index("tp") * own_rows
    memory_slots = jnp.arange(MEM)
    own_query_bias = lax.dynamic_slice_in_dim(query_bias, head_start, head_width)
    own_value_bias = lax.dynamic_slice_in_dim(value_bias, head_start, head_width)
    own_cross_query_bias = lax.dynamic_slice_in_dim(cross_query_bias, head_start, head_width)
    own_cross_value_bias = lax.dynamic_slice_in_dim(cross_value_bias, head_start, head_width)
    own_expand_bias = lax.dynamic_slice_in_dim(expand_bias, hidden_start, hidden_width)
    outputs_list = []
    input_list = []
    memory_list = []
    shard_sums = None
    vector_sums = None
    for micro_index in range(inputs.shape[0]):
        rows_in = inputs[micro_index]
        memory_in = memory[micro_index]
        grad_in = cotangent[micro_index]
        slot_positions = positions[micro_index]
        length = lengths[micro_index]
        memory_length = memory_lengths[micro_index]
        query_positions = lax.dynamic_slice_in_dim(slot_positions, query_start, group_rows)
        own_positions = lax.dynamic_slice_in_dim(slot_positions, row_start, own_rows)
        self_allowed = (slot_positions[None, :] <= query_positions[:, None]) & (
            slot_positions[None, :] < length
        )
        cross_allowed = jnp.broadcast_to((memory_slots < memory_length)[None, :], (group_rows, MEM))
        wide_rows, wide_memory = (
            lax.all_gather(rows_in, "tp", axis=0, tiled=True),
            lax.all_gather(memory_in, "tp", axis=0, tiled=True),
        )
        query_low = (product(wide_rows, full_query) + own_query_bias).astype(jnp.bfloat16)
        key_low = product(wide_rows, full_key).astype(jnp.bfloat16)
        value_low = (product(wide_rows, full_value) + own_value_bias).astype(jnp.bfloat16)
        memory_key = product(wide_memory, full_cross_key).astype(jnp.bfloat16)
        memory_value = (product(wide_memory, full_cross_value) + own_cross_value_bias).astype(
            jnp.bfloat16
        )
        all_keys, all_values, all_memory_keys, all_memory_values = (
            lax.all_gather(key_low, "ctx", axis=0, tiled=True),
            lax.all_gather(value_low, "ctx", axis=0, tiled=True),
            lax.all_gather(memory_key, "ctx", axis=0, tiled=True),
            lax.all_gather(memory_value, "ctx", axis=0, tiled=True),
        )
        attended, self_total = attend(query_low, all_keys, all_values, self_allowed)
        first_in = rows_in.astype(jnp.float32) + mix_rows(attended, full_output) + output_bias
        first_out = layer_norm(first_in, first_gain, first_shift)
        wide_first = token_rows(first_out.astype(jnp.bfloat16))
        cross_query = (product(wide_first, full_cross_query) + own_cross_query_bias).astype(
            jnp.bfloat16
        )
        cross_attended, cross_total = attend(
            cross_query, all_memory_keys, all_memory_values, cross_allowed
        )
        second_in = first_out + mix_rows(cross_attended, full_cross_output) + cross_output_bias
        second_out = layer_norm(second_in, second_gain, second_shift)
        wide_second = token_rows(second_out.astype(jnp.bfloat16))
        expanded = product(wide_second, full_expand) + own_expand_bias
        activated = jax.nn.silu(expanded).astype(jnp.bfloat16)
        third_in = second_out + mix_rows(activated, full_reduce) + reduce_bias
        outputs_list.append(layer_norm(third_in, third_gain, third_shift))
        masked_grad = jnp.where((own_positions < length)[:, None], grad_in.astype(jnp.float32), 0.0)
        third_grad, third_gain_part, third_shift_part = norm_back(
            third_in, third_gain, third_shift, masked_grad
        )
        wide_third = token_rows(third_grad.astype(jnp.bfloat16))
        reduce_part = product_left(activated, wide_third)
        activated_grad = product_right(wide_third, full_reduce)
        silu_grad = jax.vjp(jax.nn.silu, expanded)[1](activated_grad)[0]
        expanded_grad = silu_grad.astype(jnp.bfloat16)
        expand_bias_part = jnp.sum(expanded_grad.astype(jnp.float32), axis=0)
        expand_part = product_left(wide_second, expanded_grad)
        second_grad = third_grad + mix_back(expanded_grad, full_expand)
        second_in_grad, second_gain_part, second_shift_part = norm_back(
            second_in, second_gain, second_shift, second_grad
        )
        wide_second_grad = token_rows(second_in_grad.astype(jnp.bfloat16))
        cross_output_part = product_left(cross_attended, wide_second_grad)
        cross_attended_grad = product_right(wide_second_grad, full_cross_output).astype(
            jnp.bfloat16
        )
        cross_query_grad, memory_key_part, memory_value_part = attend_back(
            cross_query,
            all_memory_keys,
            all_memory_values,
            cross_allowed,
            cross_total,
            cross_attended_grad,
        )
        cross_query_low = cross_query_grad.astype(jnp.bfloat16)
        cross_query_bias_part = jnp.sum(cross_query_low.astype(jnp.float32), axis=0)
        cross_query_part = product_left(wide_first, cross_query_low)
        first_grad = second_in_grad + mix_back(cross_query_low, full_cross_query)
        first_in_grad, first_gain_part, first_shift_part = norm_back(
            first_in, first_gain, first_shift, first_grad
        )
        wide_first_grad = token_rows(first_in_grad.astype(jnp.bfloat16))
        output_part = product_left(attended, wide_first_grad)
        attended_grad = product_right(wide_first_grad, full_output).astype(jnp.bfloat16)
        query_grad, key_part, value_part = attend_back(
            query_low, all_keys, all_values, self_allowed, self_total, attended_grad
        )
        key_sum, value_sum, memory_key_sum, memory_value_sum = (
            lax.psum_scatter(key_part, "ctx", scatter_dimension=0, tiled=True),
            lax.psum_scatter(value_part, "ctx", scatter_dimension=0, tiled=True),
            lax.psum_scatter(memory_key_part, "ctx", scatter_dimension=0, tiled=True),
            lax.psum_scatter(memory_value_part, "ctx", scatter_dimension=0, tiled=True),
        )
        query_low_grad = query_grad.astype(jnp.bfloat16)
        key_low_grad = key_sum.astype(jnp.bfloat16)
        value_low_grad = value_sum.astype(jnp.bfloat16)
        memory_key_low = memory_key_sum.astype(jnp.bfloat16)
        memory_value_low = memory_value_sum.astype(jnp.bfloat16)
        query_part = product_left(wide_rows, query_low_grad)
        key_weight_part = product_left(wide_rows, key_low_grad)
        value_weight_part = product_left(wide_rows, value_low_grad)
        cross_key_part = product_left(wide_memory, memory_key_low)
        cross_value_part = product_left(wide_memory, memory_value_low)
        input_part = (
            product_right(query_low_grad, full_query)
            + product_right(key_low_grad, full_key)
            + product_right(value_low_grad, full_value)
        )
        memory_part = product_right(memory_key_low, full_cross_key) + product_right(
            memory_value_low, full_cross_value
        )
        input_sum, memory_sum = (
            lax.psum_scatter(input_part, "tp", scatter_dimension=0, tiled=True),
            lax.psum_scatter(memory_part, "tp", scatter_dimension=0, tiled=True),
        )
        input_list.append(first_in_grad + input_sum)
        memory_list.append(memory_sum)
        micro_parts = (
            query_part,
            key_weight_part,
            value_weight_part,
            output_part,
            cross_query_part,
            cross_key_part,
            cross_value_part,
            cross_output_part,
            expand_part,
            reduce_part,
        )
        reduced = reduce_weights(micro_parts)
        shard_sums = reduced if shard_sums is None else add_parts(shard_sums, reduced)
        vector_parts = (
            placed(jnp.sum(query_low_grad.astype(jnp.float32), axis=0), head_start, width),
            placed(jnp.sum(value_low_grad.astype(jnp.float32), axis=0), head_start, width),
            jnp.sum(first_in_grad, axis=0),
            first_gain_part,
            first_shift_part,
            placed(cross_query_bias_part, head_start, width),
            placed(jnp.sum(memory_value_low.astype(jnp.float32), axis=0), head_start, width),
            jnp.sum(second_in_grad, axis=0),
            second_gain_part,
            second_shift_part,
            placed(expand_bias_part, hidden_start, expand_bias.shape[0]),
            jnp.sum(third_grad, axis=0),
            third_gain_part,
            third_shift_part,
        )
        vector_sums = vector_parts if vector_sums is None else add_parts(vector_sums, vector_parts)
    vectors = lax.psum(
        (
            vector_sums[0],
            vector_sums[1],
            vector_sums[2],
            vector_sums[3],
            vector_sums[4],
            vector_sums[5],
            vector_sums[6],
            vector_sums[7],
            vector_sums[8],
            vector_sums[9],
            vector_sums[10],
            vector_sums[11],
            vector_sums[12],
            vector_sums[13],
        ),
        ("fsdp", "ctx", "tp"),
    )
    return (
        jnp.stack(outputs_list),
        jnp.stack(input_list),
        jnp.stack(memory_list),
        shard_sums[0],
        shard_sums[1],
        shard_sums[2],
        shard_sums[3],
        shard_sums[4],
        shard_sums[5],
        shard_sums[6],
        shard_sums[7],
        shard_sums[8],
        shard_sums[9],
        vectors[0],
        vectors[1],
        vectors[2],
        vectors[3],
        vectors[4],
        vectors[5],
        vectors[6],
        vectors[7],
        vectors[8],
        vectors[9],
        vectors[10],
        vectors[11],
        vectors[12],
        vectors[13],
    )


def solution(mesh):
    placed = (
        P("fsdp", ("ctx", "tp"), None),
        P("fsdp", ("ctx", "tp"), None),
        P("fsdp", ("ctx", "tp"), None),
        P("fsdp", None),
        P("fsdp"),
        P("fsdp"),
        P(("fsdp", "ctx"), "tp"),
        P(("fsdp", "ctx"), "tp"),
        P(("fsdp", "ctx"), "tp"),
        P("tp", ("fsdp", "ctx")),
        P(("fsdp", "ctx"), "tp"),
        P(("fsdp", "ctx"), "tp"),
        P(("fsdp", "ctx"), "tp"),
        P("tp", ("fsdp", "ctx")),
        P(("fsdp", "ctx"), "tp"),
        P("tp", ("fsdp", "ctx")),
        P(),
        P(),
        P(),
        P(),
        P(),
        P(),
        P(),
        P(),
        P(),
        P(),
        P(),
        P(),
        P(),
        P(),
    )
    return jax.shard_map(
        per_device,
        mesh=mesh,
        in_specs=placed,
        out_specs=(
            P("fsdp", ("ctx", "tp"), None),
            P("fsdp", ("ctx", "tp"), None),
            P("fsdp", ("ctx", "tp"), None),
            P(("fsdp", "ctx"), "tp"),
            P(("fsdp", "ctx"), "tp"),
            P(("fsdp", "ctx"), "tp"),
            P("tp", ("fsdp", "ctx")),
            P(("fsdp", "ctx"), "tp"),
            P(("fsdp", "ctx"), "tp"),
            P(("fsdp", "ctx"), "tp"),
            P("tp", ("fsdp", "ctx")),
            P(("fsdp", "ctx"), "tp"),
            P("tp", ("fsdp", "ctx")),
            P(),
            P(),
            P(),
            P(),
            P(),
            P(),
            P(),
            P(),
            P(),
            P(),
            P(),
            P(),
            P(),
            P(),
        ),
        check_vma=False,
    )
```

profile of v0, /device:TPU:0, one launch (start us, length us, event | category | flops | bytes accessed | tf_op | source)
XLA Modules:
  0.0 1848.8 jit_solution(1914845566361930478)
XLA Ops:
  13.6 32.6 %all_gather.99 = bf16[512,128]{1,0:T(8,128)(2,1)S(1)} all-gather(bf16[64,128]{1,0:T(8,128)(2,1)} %param.36), channel_id=1, replica_groups=mesh['fsdp'=4,'ctx'=2,'tp'=4] {'fsdp','ctx'}, dimensions={0}, use_global_device_ids=true | all-gather | bytes 147456 | tf_op jit(solution)/shard_map/all_gather | solution.py:98
  46.3 30.8 %all_gather.100 = bf16[512,128]{1,0:T(8,128)(2,1)S(1)} all-gather(bf16[64,128]{1,0:T(8,128)(2,1)} %param.37), channel_id=1, replica_groups=mesh['fsdp'=4,'ctx'=2,'tp'=4] {'fsdp','ctx'}, dimensions={0}, use_global_device_ids=true | all-gather | bytes 147456 | tf_op jit(solution)/shard_map/all_gather | solution.py:99
  77.0 30.7 %all_gather.97 = bf16[512,128]{1,0:T(8,128)(2,1)S(1)} all-gather(bf16[64,128]{1,0:T(8,128)(2,1)} %param.38), channel_id=1, replica_groups=mesh['fsdp'=4,'ctx'=2,'tp'=4] {'fsdp','ctx'}, dimensions={0}, use_global_device_ids=true | all-gather | bytes 147456 | tf_op jit(solution)/shard_map/all_gather | solution.py:100
  109.9 30.9 %all_gather.102 = bf16[128,512]{0,1:T(8,128)(2,1)S(1)} all-gather(bf16[128,64]{0,1:T(8,128)(2,1)} %param.39), channel_id=1, replica_groups=mesh['fsdp'=4,'ctx'=2,'tp'=4] {'fsdp','ctx'}, dimensions={1}, use_global_device_ids=true | all-gather | bytes 147456 | tf_op jit(solution)/shard_map/all_gather | solution.py:101
  229.3 33.6 %reduce-scatter.49.cloned.1.call-done = f32[256,512]{1,0:T(8,128)} async-done(((f32[1024,512]{1,0:T(8,128)}), f32[256,512]{1,0:T(8,128)}) %reduce-scatter.49.cloned.1.call-update) | async-done | bytes 524304 | tf_op jit(solution)/shard_map/reduce_scatter | solution.py:131
  269.2 30.6 %all_gather.108 = bf16[512,128]{1,0:T(8,128)(2,1)S(1)} all-gather(bf16[64,128]{1,0:T(8,128)(2,1)S(1)} %copy-done.121), channel_id=1, replica_groups=mesh['fsdp'=4,'ctx'=2,'tp'=4] {'fsdp','ctx'}, dimensions={0}, use_global_device_ids=true | all-gather | bytes 147456 | tf_op jit(solution)/shard_map/all_gather | solution.py:103
  313.2 30.7 %all_gather.104 = bf16[512,128]{1,0:T(8,128)(2,1)S(1)} all-gather(bf16[64,128]{1,0:T(8,128)(2,1)} %param.42), channel_id=1, replica_groups=mesh['fsdp'=4,'ctx'=2,'tp'=4] {'fsdp','ctx'}, dimensions={0}, use_global_device_ids=true | all-gather | bytes 147456 | tf_op jit(solution)/shard_map/all_gather | solution.py:104
  352.2 32.7 %all_gather.107 = bf16[512,128]{1,0:T(8,128)(2,1)} all-gather(bf16[64,128]{1,0:T(8,128)(2,1)} %param.40), channel_id=1, replica_groups=mesh['fsdp'=4,'ctx'=2,'tp'=4] {'fsdp','ctx'}, dimensions={0}, use_global_device_ids=true | all-gather | bytes 147456 | tf_op jit(solution)/shard_map/all_gather | solution.py:102
  384.9 32.8 %all_gather.110 = bf16[128,512]{0,1:T(8,128)(2,1)} all-gather(bf16[128,64]{0,1:T(8,128)(2,1)} %param.43), channel_id=1, replica_groups=mesh['fsdp'=4,'ctx'=2,'tp'=4] {'fsdp','ctx'}, dimensions={1}, use_global_device_ids=true | all-gather | bytes 147456 | tf_op jit(solution)/shard_map/all_gather | solution.py:105
  472.2 33.7 %reduce-scatter.51.cloned.1.call-done = f32[256,512]{1,0:T(8,128)} async-done(((f32[1024,512]{1,0:T(8,128)}), f32[256,512]{1,0:T(8,128)}) %reduce-scatter.51.cloned.1.call-update) | async-done | bytes 524304 | tf_op jit(solution)/shard_map/reduce_scatter | solution.py:131
  512.5 33.4 %all_gather.112 = bf16[512,512]{1,0:T(8,128)(2,1)} all-gather(bf16[64,512]{1,0:T(8,128)(2,1)S(1)} %copy-done.97), channel_id=1, replica_groups=mesh['fsdp'=4,'ctx'=2,'tp'=4] {'fsdp','ctx'}, dimensions={0}, use_global_device_ids=true | all-gather | bytes 589824 | tf_op jit(solution)/shard_map/all_gather | solution.py:106
  545.8 33.6 %all_gather.113 = bf16[512,512]{0,1:T(8,128)(2,1)} all-gather(bf16[512,64]{0,1:T(8,128)(2,1)S(1)} %copy-done.98), channel_id=1, replica_groups=mesh['fsdp'=4,'ctx'=2,'tp'=4] {'fsdp','ctx'}, dimensions={1}, use_global_device_ids=true | all-gather | bytes 589824 | tf_op jit(solution)/shard_map/all_gather | solution.py:107
  595.6 22.0 %reduce-scatter.53.cloned.1.call-done = f32[256,512]{1,0:T(8,128)} async-done(((f32[1024,512]{1,0:T(8,128)}), f32[256,512]{1,0:T(8,128)}) %reduce-scatter.53.cloned.1.call-update) | async-done | bytes 524304 | tf_op jit(solution)/shard_map/reduce_scatter | solution.py:131
  617.7 33.6 %reduce-scatter.47.cloned.1.call-done = f32[256,512]{1,0:T(8,128)} async-done(((f32[1024,512]{1,0:T(8,128)}), f32[256,512]{1,0:T(8,128)}) %reduce-scatter.47.cloned.1.call-update) | async-done | bytes 524304 | tf_op jit(solution)/shard_map/reduce_scatter | solution.py:131
  708.0 27.8 %reduce-scatter.55.cloned.1.call-done = f32[256,512]{1,0:T(8,128)} async-done(((f32[1024,512]{1,0:T(8,128)}), f32[256,512]{1,0:T(8,128)}) %reduce-scatter.55.cloned.1.call-update) | async-done | bytes 524304 | tf_op jit(solution)/shard_map/reduce_scatter | solution.py:131
  735.8 33.6 %reduce-scatter.65.cloned.1.call-done = f32[256,512]{1,0:T(8,128)} async-done(((f32[1024,512]{1,0:T(8,128)}), f32[256,512]{1,0:T(8,128)}) %reduce-scatter.65.cloned.1.call-update) | async-done | bytes 524304 | tf_op jit(solution)/shard_map/reduce_scatter | solution.py:131
  825.7 21.6 %reduce-scatter.57.cloned.1.call-done = f32[256,512]{1,0:T(8,128)} async-done(((f32[1024,512]{1,0:T(8,128)}), f32[256,512]{1,0:T(8,128)}) %reduce-scatter.57.cloned.1.call-update) | async-done | bytes 524304 | tf_op jit(solution)/shard_map/reduce_scatter | solution.py:131
  847.3 33.6 %reduce-scatter.67.cloned.1.call-done = f32[256,512]{1,0:T(8,128)} async-done(((f32[1024,512]{1,0:T(8,128)}), f32[256,512]{1,0:T(8,128)}) %reduce-scatter.67.cloned.1.call-update) | async-done | bytes 524304 | tf_op jit(solution)/shard_map/reduce_scatter | solution.py:131
  906.3 15.4 multiply_reduce_fusion
  1004.6 19.8 %reduce-scatter.71.cloned.1.call-done = f32[1024,128]{0,1:T(8,128)} async-done(((f32[2048,128]{0,1:T(8,128)}), f32[1024,128]{0,1:T(8,128)}) %reduce-scatter.71.cloned.1.call-update) | async-done | bytes 524304 | tf_op jit(solution)/shard_map/reduce_scatter | solution.py:317
  1049.9 19.7 %reduce-scatter.61.cloned.1.call-done = f32[1024,128]{0,1:T(8,128)} async-done(((f32[2048,128]{0,1:T(8,128)}), f32[1024,128]{0,1:T(8,128)}) %reduce-scatter.61.cloned.1.call-update) | async-done | bytes 524304 | tf_op jit(solution)/shard_map/reduce_scatter | solution.py:317
  1138.9 41.1 %all-reduce = (f32[512]{0:T(512)}, f32[512]{0:T(512)}, f32[512]{0:T(512)}, f32[512]{0:T(512)}, f32[512]{0:T(512)}, /*index=5*/f32[512]{0:T(512)}, f32[512]{0:T(5...) all-reduce(f32[512]{0:T(512)S(1)} %get-tuple-element.254, ...), channel_id=1, replica_groups=mesh['fsdp'=4,'ctx'=2,'tp'=4] {'fsdp','ctx','tp'}, use_global_device_ids=true, to_apply=%region_80.81 | all-reduce | flops 8704 | bytes 69632 | tf_op jit(solution)/shard_map/psum | solution.py:376
  1188.8 66.0 %reduce-scatter.95.cloned.1.call-done = f32[512,64]{0,1:T(8,128)} async-done(((f32[512,512]{0,1:T(8,128)}), f32[512,64]{0,1:T(8,128)}) %reduce-scatter.95.cloned.1.call-update) | async-done | bytes 131088 | tf_op jit(solution)/shard_map/reduce_scatter | solution.py:122
  1254.7 67.0 %reduce-scatter.93.cloned.1.call-done = f32[64,512]{1,0:T(8,128)} async-done(((f32[512,512]{1,0:T(8,128)}), f32[64,512]{1,0:T(8,128)}) %reduce-scatter.93.cloned.1.call-update) | async-done | bytes 131088 | tf_op jit(solution)/shard_map/reduce_scatter | solution.py:121
  1321.7 64.9 %reduce-scatter.91.cloned.1.call-done = f32[128,64]{0,1:T(8,128)} async-done(((f32[128,512]{0,1:T(8,128)}), f32[128,64]{0,1:T(8,128)}) %reduce-scatter.91.cloned.1.call-update) | async-done | bytes 32784 | tf_op jit(solution)/shard_map/reduce_scatter | solution.py:120
  1386.6 65.1 %reduce-scatter.89.cloned.1.call-done = f32[64,128]{1,0:T(8,128)} async-done(((f32[512,128]{1,0:T(8,128)}), f32[64,128]{1,0:T(8,128)}) %reduce-scatter.89.cloned.1.call-update) | async-done | bytes 32784 | tf_op jit(solution)/shard_map/reduce_scatter | solution.py:117
  1451.7 65.0 %reduce-scatter.105.cloned.1.call-done = f32[64,128]{1,0:T(8,128)} async-done(((f32[512,128]{1,0:T(8,128)}), f32[64,128]{1,0:T(8,128)}) %reduce-scatter.105.cloned.1.call-update) | async-done | bytes 32784
  1516.7 65.1 %reduce-scatter.103.cloned.1.call-done = f32[64,128]{1,0:T(8,128)} async-done(((f32[512,128]{1,0:T(8,128)}), f32[64,128]{1,0:T(8,128)}) %reduce-scatter.103.cloned.1.call-update) | async-done | bytes 32784
  1581.7 65.1 %reduce-scatter.87.cloned.1.call-done = f32[128,64]{0,1:T(8,128)} async-done(((f32[128,512]{0,1:T(8,128)}), f32[128,64]{0,1:T(8,128)}) %reduce-scatter.87.cloned.1.call-update) | async-done | bytes 32784 | tf_op jit(solution)/shard_map/reduce_scatter | solution.py:116
  1646.8 65.1 %reduce-scatter.97.cloned.1.call-done = f32[64,128]{1,0:T(8,128)} async-done(((f32[512,128]{1,0:T(8,128)}), f32[64,128]{1,0:T(8,128)}) %reduce-scatter.97.cloned.1.call-update) | async-done | bytes 32784
  1711.9 64.9 %reduce-scatter.101.cloned.1.call-done = f32[64,128]{1,0:T(8,128)} async-done(((f32[512,128]{1,0:T(8,128)}), f32[64,128]{1,0:T(8,128)}) %reduce-scatter.101.cloned.1.call-update) | async-done | bytes 32784
  1776.8 65.0 %reduce-scatter.99.cloned.1.call-done = f32[64,128]{1,0:T(8,128)} async-done(((f32[512,128]{1,0:T(8,128)}), f32[64,128]{1,0:T(8,128)}) %reduce-scatter.99.cloned.1.call-update) | async-done | bytes 32784
  (658 shorter events, 524.2 us)
Async XLA Ops:
  7.2 138.0 %all-gather.39.cloned.1.call-start = ((), (), s32[]{:S(2)}) async-start(), calls=%async_computation.65 | async-start | bytes 1310720 | tf_op jit(solution)/shard_map/all_gather | solution.py:241
  9.1 145.8 %all-gather.37.cloned.1.call-start = ((), (), s32[]{:S(2)}) async-start(), calls=%async_computation.64 | async-start | bytes 1310720 | tf_op jit(solution)/shard_map/all_gather | solution.py:241
  9.9 219.4 %reduce-scatter.43.cloned.1.call-start = ((), (), s32[]{:S(2)}) async-start(), calls=%async_computation.32 | async-start | bytes 2621440 | tf_op jit(solution)/shard_map/reduce_scatter | solution.py:131
  226.7 193.6 %all-gather.17.cloned.1.call-start = ((), (), s32[]{:S(2)}) async-start(), calls=%async_computation.33 | async-start | bytes 1310720 | tf_op jit(solution)/shard_map/all_gather | solution.py:127
  266.6 187.5 %all-gather.21.cloned.1.call-start = ((), (), s32[]{:S(2)}) async-start(), calls=%async_computation.38 | async-start | bytes 1310720 | tf_op jit(solution)/shard_map/all_gather | solution.py:127
  464.6 114.8 %all-gather.23.cloned.1.call-start = ((), (), s32[]{:S(2)}) async-start(), calls=%async_computation.40 | async-start | bytes 1310720 | tf_op jit(solution)/shard_map/all_gather | solution.py:127
  511.1 106.6 %reduce-scatter.53.cloned.1.call-start = ((), (), s32[]{:S(2)}) async-start(), calls=%async_computation.41 | async-start | bytes 2621440 | tf_op jit(solution)/shard_map/reduce_scatter | solution.py:131
  592.8 82.8 %all-gather.31.cloned.1.call-start = ((), (), s32[]{:S(2)}) async-start(), calls=%async_computation.50 | async-start | bytes 1310720 | tf_op jit(solution)/shard_map/all_gather | solution.py:127
  708.0 87.5 %all-gather.27.cloned.1.call-start = ((), (), s32[]{:S(2)}) async-start(), calls=%async_computation.44 | async-start | bytes 1310720 | tf_op jit(solution)/shard_map/all_gather | solution.py:127
  825.7 78.9 %all-gather.35.cloned.1.call-start = ((), (), s32[]{:S(2)}) async-start(), calls=%async_computation.54 | async-start | bytes 1310720 | tf_op jit(solution)/shard_map/all_gather | solution.py:127
  890.9 96.8 %reduce-scatter.75.cloned.1.call-start = ((), (), s32[]{:S(2)}) async-start(), calls=%async_computation.58 | async-start | bytes 393216 | tf_op jit(solution)/shard_map/reduce_scatter | solution.py:318
  894.1 94.8 %reduce-scatter.77.cloned.1.call-start = ((), (), s32[]{:S(2)}) async-start(), calls=%async_computation.59 | async-start | bytes 393216 | tf_op jit(solution)/shard_map/reduce_scatter | solution.py:319
  897.6 93.4 %reduce-scatter.81.cloned.1.call-start = ((), (), s32[]{:S(2)}) async-start(), calls=%async_computation.61 | async-start | bytes 393216 | tf_op jit(solution)/shard_map/reduce_scatter | solution.py:318
  900.8 91.4 %reduce-scatter.83.cloned.1.call-start = ((), (), s32[]{:S(2)}) async-start(), calls=%async_computation.62 | async-start | bytes 393216 | tf_op jit(solution)/shard_map/reduce_scatter | solution.py:319
  903.9 97.8 %reduce-scatter.69.cloned.1.call-start = ((), (), s32[]{:S(2)}) async-start(), calls=%async_computation.55 | async-start | bytes 1572864 | tf_op jit(solution)/shard_map/reduce_scatter | solution.py:316
  937.7 86.8 %reduce-scatter.71.cloned.1.call-start = ((), (), s32[]{:S(2)}) async-start(), calls=%async_computation.56 | async-start | bytes 1572864 | tf_op jit(solution)/shard_map/reduce_scatter | solution.py:317
  962.0 85.1 %reduce-scatter.59.cloned.1.call-start = ((), (), s32[]{:S(2)}) async-start(), calls=%async_computation.47 | async-start | bytes 1572864 | tf_op jit(solution)/shard_map/reduce_scatter | solution.py:316
  978.2 91.4 %reduce-scatter.61.cloned.1.call-start = ((), (), s32[]{:S(2)}) async-start(), calls=%async_computation.48 | async-start | bytes 1572864 | tf_op jit(solution)/shard_map/reduce_scatter | solution.py:317
  987.6 119.9 %reduce-scatter.79.cloned.1.call-start = ((), (), s32[]{:S(2)}) async-start(), calls=%async_computation.60 | async-start | bytes 655360 | tf_op jit(solution)/shard_map/reduce_scatter | solution.py:341
  991.0 127.0 %reduce-scatter.85.cloned.1.call-start = ((), (), s32[]{:S(2)}) async-start(), calls=%async_computation.63 | async-start | bytes 655360 | tf_op jit(solution)/shard_map/reduce_scatter | solution.py:341
  994.2 185.8 %reduce-scatter.73.cloned.1.call-start = ((), (), s32[]{:S(2)}) async-start(), calls=%async_computation.57 | async-start | bytes 2621440 | tf_op jit(solution)/shard_map/reduce_scatter | solution.py:340
  1028.0 158.5 %reduce-scatter.63.cloned.1.call-start = ((), (), s32[]{:S(2)}) async-start(), calls=%async_computation.49 | async-start | bytes 2621440 | tf_op jit(solution)/shard_map/reduce_scatter | solution.py:340
  1073.2 181.6 %reduce-scatter.95.cloned.1.call-start = ((), (), s32[]{:S(2)}) async-start(), calls=%async_computation.70 | async-start | bytes 1179648 | tf_op jit(solution)/shard_map/reduce_scatter | solution.py:122
  1077.9 243.8 %reduce-scatter.93.cloned.1.call-start = ((), (), s32[]{:S(2)}) async-start(), calls=%async_computation.69 | async-start | bytes 1179648 | tf_op jit(solution)/shard_map/reduce_scatter | solution.py:121
  1083.6 303.0 %reduce-scatter.91.cloned.1.call-start = ((), (), s32[]{:S(2)}) async-start(), calls=%async_computation.68 | async-start | bytes 294912 | tf_op jit(solution)/shard_map/reduce_scatter | solution.py:120
  1091.7 360.0 %reduce-scatter.89.cloned.1.call-start = ((), (), s32[]{:S(2)}) async-start(), calls=%async_computation.67 | async-start | bytes 294912 | tf_op jit(solution)/shard_map/reduce_scatter | solution.py:117
  1094.7 421.9 %reduce-scatter.105.cloned.1.call-start = ((), (), s32[]{:S(2)}) async-start(), calls=%async_computation.75 | async-start | bytes 294912
  1102.7 479.0 %reduce-scatter.103.cloned.1.call-start = ((), (), s32[]{:S(2)}) async-start(), calls=%async_computation.74 | async-start | bytes 294912
  1107.5 539.3 %reduce-scatter.87.cloned.1.call-start = ((), (), s32[]{:S(2)}) async-start(), calls=%async_computation.66 | async-start | bytes 294912 | tf_op jit(solution)/shard_map/reduce_scatter | solution.py:116
  1127.7 584.1 %reduce-scatter.97.cloned.1.call-start = ((), (), s32[]{:S(2)}) async-start(), calls=%async_computation.71 | async-start | bytes 294912
  1129.5 647.3 %reduce-scatter.101.cloned.1.call-start = ((), (), s32[]{:S(2)}) async-start(), calls=%async_computation.73 | async-start | bytes 294912
  1132.4 709.4 %reduce-scatter.99.cloned.1.call-start = ((), (), s32[]{:S(2)}) async-start(), calls=%async_computation.72 | async-start | bytes 294912
  (174 other events, 3799.8 us)
Sparse Core Ops, SparseCore 0:
  10.1 19.4 all-gather.38
  198.2 31.0 reduce-scatter.42
  231.7 31.1 reduce-scatter.48
  266.7 16.6 all-gather.16
  420.3 18.1 all-gather.20
  441.0 31.1 reduce-scatter.44
  474.7 31.1 reduce-scatter.50
  586.1 31.4 reduce-scatter.52
  620.0 31.1 reduce-scatter.46
  658.9 16.6 all-gather.30
  704.6 31.1 reduce-scatter.54
  738.2 31.1 reduce-scatter.64
  816.1 31.1 reduce-scatter.56
  849.7 31.1 reduce-scatter.66
  981.3 20.3 reduce-scatter.68
  1004.0 20.3 reduce-scatter.70
  1026.7 20.3 reduce-scatter.58
  1049.2 20.3 reduce-scatter.60
  1072.1 21.6 reduce-scatter.78
  1096.3 21.6 reduce-scatter.84
  1120.4 31.7 reduce-scatter.72
  1154.7 31.8 reduce-scatter.62
  1190.5 64.1 reduce-scatter.94
  1258.5 63.1 reduce-scatter.92
  1325.5 61.0 reduce-scatter.90
  1390.5 61.1 reduce-scatter.88
  1455.5 61.1 reduce-scatter.104
  1520.6 61.1 reduce-scatter.102
  1585.6 61.1 reduce-scatter.86
  1650.7 61.1 reduce-scatter.96
  1715.6 61.1 reduce-scatter.100
  1780.7 61.0 reduce-scatter.98
  (12 shorter events, 179.9 us)
where the time goes:
time: 1860 us; the launch traced here: 1850 us
  waiting for transfers between devices  1020 us (55%)
  blocking collectives  425 us (23%)
  matrix products  220 us (12%)
  other arithmetic  107 us (6%)
  local copies, waits for them, and re-layouts  56.2 us (3%)
    unnamed x49, waiting for transfers between devices  327 us
    reduce_scatter x10, waiting for transfers between devices, row_sums(): return lax.psum_scatter(values, 'tp', scatter_dimension=0, tiled=True)  250 us
    reduce_scatter x1, waiting for transfers between devices, reduce_weights(): lax.psum_scatter(parts[8], ('fsdp', 'ctx'), scatter_dimension=0, tiled=True)  67 us
    reduce_scatter x1, waiting for transfers between devices, reduce_weights(): lax.psum_scatter(parts[9], ('fsdp', 'ctx'), scatter_dimension=1, tiled=True)  66 us
    reduce_scatter x1, waiting for transfers between devices, reduce_weights(): lax.psum_scatter(parts[4], ('fsdp', 'ctx'), scatter_dimension=0, tiled=True)  65.1 us
    reduce_scatter x1, waiting for transfers between devices, reduce_weights(): lax.psum_scatter(parts[3], ('fsdp', 'ctx'), scatter_dimension=1, tiled=True)  65.1 us
    reduce_scatter x1, waiting for transfers between devices, reduce_weights(): lax.psum_scatter(parts[7], ('fsdp', 'ctx'), scatter_dimension=1, tiled=True)  64.9 us
    all_gather x10, waiting for transfers between devices, token_rows(): return lax.all_gather(values, 'tp', axis=0, tiled=True)  48.5 us
  transfers between devices with their start and end apart: 44, of which 31 were waited for; matrix products, arithmetic and copies ran while one was open for 16% of the time, Pallas kernels for 0%

commit v1 on v0

v1 whole, which is shorter than its diff:
```python
import functools

import jax
import jax.numpy as jnp
from jax import lax
from jax.experimental import pallas as pl
from jax.experimental.pallas import tpu as pltpu
from jax.sharding import PartitionSpec as P

HEAD_DIM = 64
EPSILON = 1e-05
NEGATIVE = -1e30
F32 = jnp.float32
BF16 = jnp.bfloat16
SCALE = HEAD_DIM ** -0.5
VMEM_BYTES = 58 * 2 ** 20


def contract(left, right, left_dim, right_dim):
    return lax.dot_general(
        left, right, (((left_dim,), (right_dim,)), ((), ())), preferred_element_type=F32
    )


def product(left, right):
    return contract(left, right, 1, 0)


def product_left(left, right):
    return contract(left, right, 0, 0)


def product_right(left, right):
    return contract(left, right, 1, 1)


def layer_norm(values, gain, shift):
    center = values - jnp.mean(values, axis=-1, keepdims=True)
    spread = jnp.mean(center * center, axis=-1, keepdims=True)
    return center * lax.rsqrt(spread + EPSILON) * gain + shift


def norm_back(values, gain, grad):
    center = values - jnp.mean(values, axis=-1, keepdims=True)
    spread = jnp.mean(center * center, axis=-1, keepdims=True)
    rate = lax.rsqrt(spread + EPSILON)
    normal = center * rate
    scaled = grad * gain
    back = rate * (
        scaled
        - jnp.mean(scaled, axis=-1, keepdims=True)
        - normal * jnp.mean(scaled * normal, axis=-1, keepdims=True)
    )
    return back, jnp.sum(grad * normal, axis=0), jnp.sum(grad, axis=0)


def attend_kernel(heads, q, k, v, qp, kp, out, weights, inverse):
    allowed = kp[...] <= qp[...]
    for head in range(heads):
        cols = slice(head * HEAD_DIM, (head + 1) * HEAD_DIM)
        scores = contract(k[:, cols], q[:, cols] * SCALE, 1, 1)
        scores = jnp.where(allowed, scores, NEGATIVE)
        largest = jnp.max(scores, axis=0, keepdims=True)
        power = jnp.exp(scores - largest)
        rate = 1.0 / jnp.sum(power, axis=0, keepdims=True)
        low = power.astype(BF16)
        weights[head] = low
        inverse[head] = rate
        out[:, cols] = (contract(v[:, cols], low, 0, 0) * rate).T.astype(BF16)


def attend_back_kernel(heads, q, k, v, weights, inverse, out, grad, dq, dk, dv):
    for head in range(heads):
        cols = slice(head * HEAD_DIM, (head + 1) * HEAD_DIM)
        grads = grad[:, cols].astype(F32).T
        outs = out[:, cols].astype(F32).T
        inner = jnp.sum(grads * outs, axis=0, keepdims=True) * inverse[head]
        scaled = (grads * inverse[head]).astype(BF16)
        weight = weights[head]
        grad_weight = contract(v[:, cols], scaled, 1, 0)
        grad_scores = (weight.astype(F32) * (grad_weight - inner)).astype(BF16)
        dq[:, cols] = (contract(k[:, cols], grad_scores, 0, 0) * SCALE).T.astype(BF16)
        dv[:, cols] = contract(weight, scaled, 1, 1).astype(BF16)
        dk[:, cols] = (contract(grad_scores, q[:, cols], 1, 0) * SCALE).astype(BF16)


HEADS_PER_STEP = 2


def column_block(rows):
    return pl.BlockSpec((rows, HEADS_PER_STEP * HEAD_DIM), lambda i: (0, i))


def head_block(*dims):
    return pl.BlockSpec((HEADS_PER_STEP,) + dims, lambda i: (i, 0, 0))


def attend(q, k, v, qp, kp):
    rows, width = q.shape
    keys = k.shape[0]
    heads = width // HEAD_DIM
    return pl.pallas_call(
        functools.partial(attend_kernel, HEADS_PER_STEP),
        grid=(heads // HEADS_PER_STEP,),
        in_specs=[
            column_block(rows),
            column_block(keys),
            column_block(keys),
            pl.BlockSpec((1, rows), lambda i: (0, 0)),
            pl.BlockSpec((keys, 1), lambda i: (0, 0)),
        ],
        out_specs=[column_block(rows), head_block(keys, rows), head_block(1, rows)],
        out_shape=[
            jax.ShapeDtypeStruct((rows, width), BF16),
            jax.ShapeDtypeStruct((heads, keys, rows), BF16),
            jax.ShapeDtypeStruct((heads, 1, rows), F32),
        ],
        compiler_params=pltpu.CompilerParams(vmem_limit_bytes=VMEM_BYTES),
        cost_estimate=pl.CostEstimate(
            flops=4 * rows * keys * width * 4,
            transcendentals=heads * rows * keys,
            bytes_accessed=2 * heads * rows * keys,
        ),
        name="attend",
    )(q, k, v, qp, kp)


def attend_back(q, k, v, weights, inverse, out, grad):
    rows, width = q.shape
    keys = k.shape[0]
    heads = width // HEAD_DIM
    return pl.pallas_call(
        functools.partial(attend_back_kernel, HEADS_PER_STEP),
        grid=(heads // HEADS_PER_STEP,),
        in_specs=[
            column_block(rows),
            column_block(keys),
            column_block(keys),
            head_block(keys, rows),
            head_block(1, rows),
            column_block(rows),
            column_block(rows),
        ],
        out_specs=[column_block(rows), column_block(keys), column_block(keys)],
        out_shape=[
            jax.ShapeDtypeStruct((rows, width), BF16),
            jax.ShapeDtypeStruct((keys, width), BF16),
            jax.ShapeDtypeStruct((keys, width), BF16),
        ],
        compiler_params=pltpu.CompilerParams(vmem_limit_bytes=VMEM_BYTES),
        cost_estimate=pl.CostEstimate(
            flops=8 * rows * keys * width * 4,
            transcendentals=0,
            bytes_accessed=2 * heads * rows * keys,
        ),
        name="attend_back",
    )(q, k, v, weights, inverse, out, grad)


def move(sources, shapes, plan, name):
    def body(*refs):
        given = refs[: len(sources)]
        made = refs[len(sources) : len(sources) + len(shapes)]
        sems = refs[-1]
        copies = []
        for at, (i, a, j, b) in enumerate(plan()):
            copies.append(pltpu.make_async_copy(given[i].at[a], made[j].at[b], sems.at[at]))
        for copy in copies:
            copy.start()
        for copy in copies:
            copy.wait()

    count = move_count(plan)
    return pl.pallas_call(
        body,
        in_specs=[pl.BlockSpec(memory_space=pl.ANY)] * len(sources),
        out_specs=[pl.BlockSpec(memory_space=pl.ANY)] * len(shapes),
        out_shape=[jax.ShapeDtypeStruct(shape, BF16) for shape in shapes],
        scratch_shapes=[pltpu.SemaphoreType.DMA((count,))],
        name=name,
    )(*sources)


def move_count(plan):
    return len(plan())


def sizes():
    return lax.axis_size("fsdp"), lax.axis_size("ctx"), lax.axis_size("tp") // 2


def places():
    tp = lax.axis_index("tp")
    return lax.axis_index("fsdp"), lax.axis_index("ctx"), tp // 2, tp % 2


def swap(value):
    total = lax.axis_size("tp")
    return lax.ppermute(value, "tp", [(i, i ^ 1) for i in range(total)])


def shift_x(value, step):
    total = lax.axis_size("tp")
    return lax.ppermute(value, "tp", [(i, (i + 2 * step) % total) for i in range(total)])


def shift(value, axis, step):
    total = lax.axis_size(axis)
    return lax.ppermute(value, axis, [(i, (i + step) % total) for i in range(total)])


def offsets():
    unused, high, wide = sizes()
    return [(dx, dy) for dy in range(high) for dx in range(wide)]


def is_square():
    unused, high, wide = sizes()
    return high == 2 and wide == 2


def gather_plane(first, second):
    if is_square():
        side = (shift_x(first, 1), shift_x(second, 1))
        front = (shift(first, "ctx", 1), shift(second, "ctx", 1))
        far = (shift(side[0], "ctx", 1), shift_x(front[1], 1))
        return [(first, second), side, front, far]
    unused, high, wide = sizes()
    row = [(first, second)] + [(shift_x(first, k), shift_x(second, k)) for k in range(1, wide)]
    blocks = list(row)
    for step in range(1, high):
        blocks += [(shift(a, "ctx", step), shift(b, "ctx", step)) for a, b in row]
    return blocks


def add(left, right):
    return (left.astype(F32) + right.astype(F32)).astype(BF16)


def scatter_plane(blocks):
    if is_square():
        own, side, front, far = blocks
        side_first = add(side[0], shift(far[0], "ctx", 1))
        front_second = add(front[1], shift_x(far[1], 1))
        from_side = (shift_x(side_first, 1), shift_x(side[1], 1))
        from_front = (shift(front[0], "ctx", 1), shift(front_second, "ctx", 1))
        return [own, from_side, from_front]
    unused, high, wide = sizes()
    row = []
    for dx in range(wide):
        total = blocks[dx]
        for dy in range(1, high):
            other = blocks[dy * wide + dx]
            total = tuple(add(a, shift(b, "ctx", -dy)) for a, b in zip(total, other))
        row.append(total)
    return [row[0]] + [
        (shift_x(row[dx][0], -dx), shift_x(row[dx][1], -dx)) for dx in range(1, wide)
    ]


def summed(parts):
    return sum(part.astype(F32) for part in parts)


def gather_weights(packed, widths):
    deep, high, wide = sizes()
    rows, total = packed.shape
    half = deep // 2
    pieces = [packed] + [shift(packed, "fsdp", k) for k in range(1, deep)]

    def by_depth():
        at = lax.axis_index("fsdp")
        return [(k, slice(None), 0, (at - k + deep) % deep) for k in range(deep)]

    stacked = move(pieces, [(deep, rows, total)], by_depth, "stack_depth")[0]
    blocks = gather_plane(stacked[:half], stacked[half:])
    order = offsets()

    def side_by_side():
        steps = []
        for n in range(len(order)):
            steps.append((2 * n, slice(None), 0, (n, slice(0, half))))
            steps.append((2 * n + 1, slice(None), 0, (n, slice(half, deep))))
        return steps

    own = move(
        [part for block in blocks for part in block],
        [(len(order), deep, rows, total)],
        side_by_side,
        "stack_plane",
    )[0]
    other = swap(own)
    starts = [sum(widths[:i]) for i in range(len(widths))]
    if all(width % 128 == 0 for width in widths):

        def into_place():
            unused, y, x, core = places()
            steps = []
            for n, (dx, dy) in enumerate(order):
                at_y = (y - dy + high) % high
                at_x = (x - dx + wide) % wide
                for who in range(2):
                    at = 2 * at_x + (core if who == 0 else 1 - core)
                    for j, width in enumerate(widths):
                        cols = slice(starts[j], starts[j] + width)
                        here = pl.ds(pl.multiple_of(at * width, 128), width)
                        steps.append(
                            (
                                who,
                                (n, slice(None), slice(None), cols),
                                j,
                                (slice(None), at_y, slice(None), here),
                            )
                        )
            return steps

        made = move(
            [own, other],
            [(deep, high, rows, 2 * wide * width) for width in widths],
            into_place,
            "place_weights",
        )
        return [m.reshape(deep * high * rows, -1) for m in made]
    unused, y, x, core = places()
    whole = jnp.zeros((high, wide, 2, deep, rows, total), BF16)
    for n, (dx, dy) in enumerate(order):
        for who, part in ((core, own), (1 - core, other)):
            at = ((y - dy + high) % high, (x - dx + wide) % wide, who, 0, 0, 0)
            whole = lax.dynamic_update_slice(whole, part[n][None, None, None], at)
    made = []
    for start, width in zip(starts, widths):
        part = whole[..., start : start + width]
        part = part.transpose(3, 0, 4, 1, 2, 5)
        made.append(part.reshape(deep * high * rows, 2 * wide * width))
    return made


def scatter_weights(grads, widths):
    deep, high, wide = sizes()
    rows = grads[0].shape[0] // (deep * high)
    total = sum(widths)
    half = deep // 2
    order = offsets()
    starts = [sum(widths[:i]) for i in range(len(widths))]
    shaped = [g.reshape(deep, high, rows, 2 * wide * w) for g, w in zip(grads, widths)]
    if all(width % 128 == 0 for width in widths):

        def into_blocks():
            unused, y, x, core = places()
            steps = []
            for n, (dx, dy) in enumerate(order):
                at_y = (y - dy + high) % high
                at_x = (x - dx + wide) % wide
                for who in range(2):
                    at = 2 * at_x + (core if who == 0 else 1 - core)
                    for j, width in enumerate(widths):
                        cols = slice(starts[j], starts[j] + width)
                        here = pl.ds(pl.multiple_of(at * width, 128), width)
                        steps.append(
                            (
                                j,
                                (slice(None), at_y, slice(None), here),
                                who,
                                (n, slice(None), slice(None), cols),
                            )
                        )
            return steps

        keep, send = move(
            shaped, [(len(order), deep, rows, total)] * 2, into_blocks, "split_weights"
        )
    else:
        unused, y, x, core = places()
        whole = jnp.concatenate(
            [g.reshape(deep, high, rows, wide, 2, w) for g, w in zip(shaped, widths)], axis=-1
        ).transpose(1, 3, 4, 0, 2, 5)
        size = (1, 1, 1, deep, rows, total)

        def pick(dx, dy, who):
            at = ((y - dy + high) % high, (x - dx + wide) % wide, who, 0, 0, 0)
            return lax.dynamic_slice(whole, at, size).reshape(size[3:])

        keep = jnp.stack([pick(dx, dy, core) for dx, dy in order])
        send = jnp.stack([pick(dx, dy, 1 - core) for dx, dy in order])
    other = swap(send)
    blocks = [
        (add(keep[n, :half], other[n, :half]), add(keep[n, half:], other[n, half:]))
        for n in range(len(order))
    ]
    left = scatter_plane(blocks)
    own = jnp.concatenate([summed([part[h] for part in left]) for h in range(2)], axis=0)
    low = own.astype(BF16)
    at = lax.axis_index("fsdp")
    result = lax.dynamic_index_in_dim(own, at, 0, keepdims=False)
    for k in range(1, deep):
        piece = lax.dynamic_index_in_dim(low, (at + k) % deep, 0, keepdims=False)
        result = result + shift(piece, "fsdp", k).astype(F32)
    return result


def all_sum(value):
    for axis in ("tp", "ctx", "fsdp"):
        total = lax.axis_size(axis)
        step = 1
        while step < total:
            pairs = [(i, i ^ step) for i in range(total)]
            value = value + lax.ppermute(value, axis, pairs)
            step *= 2
    return value


def per_device(
    inputs,
    memory,
    cotangent,
    positions,
    lengths,
    memory_lengths,
    query_weight,
    key_weight,
    value_weight,
    output_weight,
    cross_query_weight,
    cross_key_weight,
    cross_value_weight,
    cross_output_weight,
    expand_weight,
    reduce_weight,
    query_bias,
    value_bias,
    output_bias,
    first_gain,
    first_shift,
    cross_query_bias,
    cross_value_bias,
    cross_output_bias,
    second_gain,
    second_shift,
    expand_bias,
    reduce_bias,
    third_gain,
    third_shift,
):
    deep, high, wide = sizes()
    z, y, x, core = places()
    own_rows, width = inputs.shape[1:]
    own_memory = memory.shape[1]
    rows = 2 * own_rows
    head_width = query_weight.shape[1]
    hidden_width = expand_weight.shape[1]

    def exchange(value):
        keep = lax.dynamic_index_in_dim(value, core, 0, keepdims=False)
        give = lax.dynamic_index_in_dim(value, 1 - core, 0, keepdims=False)
        return keep, swap(give)

    input_pair = exchange(inputs)
    memory_pair = exchange(memory)
    cotangent_pair = exchange(cotangent)
    blocks = gather_plane(
        jnp.concatenate([input_pair[0], memory_pair[0]], axis=0),
        jnp.concatenate([input_pair[1], memory_pair[1]], axis=0),
    )
    rows_in = jnp.concatenate(input_pair, axis=0)
    wide_rows = jnp.concatenate([p[:own_rows] for b in blocks for p in b], axis=0)
    wide_memory = jnp.concatenate([p[own_rows:] for b in blocks for p in b], axis=0)

    slots = lax.dynamic_index_in_dim(positions, core, 0, keepdims=False)
    length = lax.dynamic_index_in_dim(lengths, core, 0, keepdims=False)
    memory_length = lax.dynamic_index_in_dim(memory_lengths, core, 0, keepdims=False)
    key_positions = []
    memory_slots = []
    for dx, dy in offsets():
        at_y = (y - dy + high) % high
        at_x = (x - dx + wide) % wide
        for who in (core, 1 - core):
            block = (at_y * wide + at_x) * 2 + who
            key_positions.append(lax.dynamic_slice_in_dim(slots, block * own_rows, own_rows))
            memory_slots.append(block * own_memory + jnp.arange(own_memory, dtype=jnp.int32))
    own_positions = jnp.concatenate(key_positions[:2])
    key_positions = jnp.concatenate(key_positions)
    last = positions.shape[1]
    key_positions = jnp.where(key_positions < length, key_positions, last)[:, None]
    query_positions = own_positions[None, :]
    memory_slots = jnp.concatenate(memory_slots)[:, None]
    memory_limit = jnp.broadcast_to(memory_length - 1, (1, rows))

    first_widths = [head_width] * 3
    second_widths = [head_width] * 5
    third_widths = [hidden_width] * 2
    full_query, full_key, full_value = gather_weights(
        jnp.concatenate([query_weight, key_weight, value_weight], axis=1), first_widths
    )
    full_cross_key, full_cross_value, full_output, full_cross_query, full_cross_output = (
        gather_weights(
            jnp.concatenate(
                [
                    cross_key_weight,
                    cross_value_weight,
                    output_weight.T,
                    cross_query_weight,
                    cross_output_weight.T,
                ],
                axis=1,
            ),
            second_widths,
        )
    )
    full_expand, full_reduce = gather_weights(
        jnp.concatenate([expand_weight, reduce_weight.T], axis=1), third_widths
    )

    query_low = (product(rows_in, full_query) + query_bias).astype(BF16)
    keys = product(wide_rows, full_key).astype(BF16)
    values = (product(wide_rows, full_value) + value_bias).astype(BF16)
    attended, weights, inverse = attend(query_low, keys, values, query_positions, key_positions)
    memory_key = product(wide_memory, full_cross_key).astype(BF16)
    memory_value = (product(wide_memory, full_cross_value) + cross_value_bias).astype(BF16)

    first_in = rows_in.astype(F32) + product_right(attended, full_output) + output_bias
    first_out = layer_norm(first_in, first_gain, first_shift)
    first_low = first_out.astype(BF16)
    cross_query = (product(first_low, full_cross_query) + cross_query_bias).astype(BF16)
    cross_attended, cross_weights, cross_inverse = attend(
        cross_query, memory_key, memory_value, memory_limit, memory_slots
    )
    second_in = first_out + product_right(cross_attended, full_cross_output) + cross_output_bias
    second_out = layer_norm(second_in, second_gain, second_shift)
    second_low = second_out.astype(BF16)
    expanded = product(second_low, full_expand) + expand_bias
    gate = jax.nn.sigmoid(expanded)
    activated = (expanded * gate).astype(BF16)
    third_in = second_out + product_right(activated, full_reduce) + reduce_bias
    outputs = layer_norm(third_in, third_gain, third_shift)

    grad_in = jnp.concatenate(cotangent_pair, axis=0).astype(F32)
    masked_grad = jnp.where((own_positions < length)[:, None], grad_in, 0.0)
    third_grad, third_gain_part, third_shift_part = norm_back(third_in, third_gain, masked_grad)
    third_low = third_grad.astype(BF16)
    activated_grad = product(third_low, full_reduce)
    expanded_grad = (activated_grad * gate * (1.0 + expanded * (1.0 - gate))).astype(BF16)
    third_part = [
        product_left(second_low, expanded_grad).astype(BF16),
        product_left(third_low, activated).astype(BF16),
    ]
    third_shard = scatter_weights(third_part, third_widths)

    second_grad = third_grad + product_right(expanded_grad, full_expand)
    second_in_grad, second_gain_part, second_shift_part = norm_back(
        second_in, second_gain, second_grad
    )
    second_grad_low = second_in_grad.astype(BF16)
    cross_attended_grad = product(second_grad_low, full_cross_output).astype(BF16)
    cross_query_grad, memory_key_grad, memory_value_grad = attend_back(
        cross_query,
        memory_key,
        memory_value,
        cross_weights,
        cross_inverse,
        cross_attended,
        cross_attended_grad,
    )
    first_grad = second_in_grad + product_right(cross_query_grad, full_cross_query)
    first_in_grad, first_gain_part, first_shift_part = norm_back(first_in, first_gain, first_grad)
    first_grad_low = first_in_grad.astype(BF16)
    attended_grad = product(first_grad_low, full_output).astype(BF16)
    second_part = [
        product_left(wide_memory, memory_key_grad).astype(BF16),
        product_left(wide_memory, memory_value_grad).astype(BF16),
        product_left(first_grad_low, attended).astype(BF16),
        product_left(first_low, cross_query_grad).astype(BF16),
        product_left(second_grad_low, cross_attended).astype(BF16),
    ]
    second_shard = scatter_weights(second_part, second_widths)
    memory_part = product_right(memory_key_grad, full_cross_key) + product_right(
        memory_value_grad, full_cross_value
    )

    query_grad, key_grad, value_grad = attend_back(
        query_low, keys, values, weights, inverse, attended, attended_grad
    )
    input_part = product_right(key_grad, full_key) + product_right(value_grad, full_value)
    input_own = first_in_grad + product_right(query_grad, full_query)
    first_part = [
        product_left(rows_in, query_grad).astype(BF16),
        product_left(wide_rows, key_grad).astype(BF16),
        product_left(wide_rows, value_grad).astype(BF16),
    ]
    first_shard = scatter_weights(first_part, first_widths)

    def halves(part, block_rows):
        return [
            tuple(
                part[(2 * n + h) * block_rows : (2 * n + h + 1) * block_rows] for h in range(2)
            )
            for n in range(len(offsets()))
        ]

    row_blocks = halves(input_part, own_rows)
    memory_blocks = halves(memory_part, own_memory)
    low_blocks = [
        tuple(jnp.concatenate([r, m], axis=0).astype(BF16) for r, m in zip(rb, mb))
        for rb, mb in zip(row_blocks, memory_blocks)
    ]
    left = scatter_plane(low_blocks)[1:]
    pair = [summed([part[h] for part in left]) for h in range(2)]
    input_pair = [
        input_own[h * own_rows : (h + 1) * own_rows] + row_blocks[0][h] + pair[h][:own_rows]
        for h in range(2)
    ]
    memory_pair = [memory_blocks[0][h] + pair[h][own_rows:] for h in range(2)]

    def restore(pair):
        other = swap(pair[1])
        return jnp.where(
            core == 0, jnp.stack([pair[0], other]), jnp.stack([other, pair[0]])
        )

    output_result = restore([outputs[:own_rows], outputs[own_rows:]])
    input_result = restore(input_pair)
    memory_result = restore(memory_pair)

    vectors = [
        jnp.sum(query_grad.astype(F32), axis=0),
        jnp.sum(value_grad.astype(F32), axis=0),
        jnp.sum(first_in_grad, axis=0),
        first_gain_part,
        first_shift_part,
        jnp.sum(cross_query_grad.astype(F32), axis=0),
        jnp.sum(memory_value_grad.astype(F32), axis=0),
        jnp.sum(second_in_grad, axis=0),
        second_gain_part,
        second_shift_part,
        jnp.sum(expanded_grad.astype(F32), axis=0),
        jnp.sum(third_grad, axis=0),
        third_gain_part,
        third_shift_part,
    ]
    joined = all_sum(jnp.concatenate(vectors))
    split = []
    start = 0
    for vector in vectors:
        split.append(joined[start : start + vector.shape[0]])
        start += vector.shape[0]

    def shards(packed, widths):
        start = 0
        parts = []
        for one in widths:
            parts.append(packed[:, start : start + one])
            start += one
        return parts

    g_query, g_key, g_value = shards(first_shard, first_widths)
    g_cross_key, g_cross_value, g_output, g_cross_query, g_cross_output = shards(
        second_shard, second_widths
    )
    g_expand, g_reduce = shards(third_shard, third_widths)
    return (
        output_result,
        input_result,
        memory_result,
        g_query,
        g_key,
        g_value,
        g_output.T,
        g_cross_query,
        g_cross_key,
        g_cross_value,
        g_cross_output.T,
        g_expand,
        g_reduce.T,
        *split,
    )


def solution(mesh):
    rows = P("fsdp", ("ctx", "tp"), None)
    tall = P(("fsdp", "ctx"), "tp")
    flat = P("tp", ("fsdp", "ctx"))
    weights = (tall, tall, tall, flat, tall, tall, tall, flat, tall, flat)
    return jax.shard_map(
        per_device,
        mesh=mesh,
        in_specs=(rows, rows, rows, P("fsdp", None), P("fsdp"), P("fsdp"))
        + weights
        + (P(),) * 14,
        out_specs=(rows, rows, rows) + weights + (P(),) * 14,
        check_vma=False,
    )
```

time: 1860 us -> 1040 us (0.56)
  waiting for transfers between devices: 1020 us -> 63.3 us
  Pallas kernels: 0 us -> 742 us
  blocking collectives: 425 us -> 0 us
  matrix products: 220 us -> 55.1 us
  starting transfers between devices: 3.08 us -> 85 us
  other arithmetic: 107 us -> 37.8 us
    pallas_call x0 -> x16, Pallas kernels: none -> 742 us  [the longest x12 682 us: move(): pl.pallas_call(body, in_specs=[pl.BlockSpec(memory_space=pl.ANY)] * len(s...]
    reduce_scatter x27 -> x0, waiting for transfers between devices: 645 us -> none  [the longest x10 250 us: row_sums(): return lax.psum_scatter(values, 'tp', scatter_dimension=0, tiled=True)]
    all_gather x20 -> x0, blocking collectives: 384 us -> none  [the longest x1 33.6 us: gather_weights(): lax.all_gather(parts[9], ('fsdp', 'ctx'), axis=1, tiled=True)]
    unnamed x49 -> x0, waiting for transfers between devices: 327 us -> none
    dot_general x84 -> x30, matrix products: 220 us -> 55.1 us  [contract(): lax.dot_general(left, right, (((left_dim,), (right_dim,)), ((), ())), pre...]
    ppermute x0 -> x83, starting transfers between devices: none -> 85 us  [the longest x42 55.4 us: shift(): lax.ppermute(value, axis, [(i, (i + step) % total) for i in range(total)])]
    ppermute x0 -> x83, waiting for transfers between devices: none -> 63.3 us  [the longest x42 31.9 us: shift(): lax.ppermute(value, axis, [(i, (i + step) % total) for i in range(total)])]
    all_gather x12 -> x0, waiting for transfers between devices: 48.6 us -> none  [the longest x10 48.5 us: token_rows(): return lax.all_gather(values, 'tp', axis=0, tiled=True)]
  transfers between devices with their start and end apart: 44 -> 83, of which waited for: 31 -> 24; matrix products, arithmetic and copies ran while one was open for 16% -> 10% of each run, Pallas kernels for 0% -> 69%
where the time goes in v1:
time: 1040 us
  Pallas kernels  742 us (71%)
  starting transfers between devices  85 us (8%)
  waiting for transfers between devices  63.3 us (6%)
  matrix products  55.1 us (5%)
  local copies, waits for them, and re-layouts  51.3 us (5%)
  other arithmetic  37.8 us (4%)
    pallas_call x12, Pallas kernels, move(): pl.pallas_call(body, in_specs=[pl.BlockSpec(memory_space=pl.ANY)] * len(s...  682 us
    ppermute x42, starting transfers between devices, shift(): lax.ppermute(value, axis, [(i, (i + step) % total) for i in range(total)])  55.4 us
    dot_general x30, matrix products, contract(): lax.dot_general(left, right, (((left_dim,), (right_dim,)), ((), ())), pre...  55.1 us
    ppermute x42, waiting for transfers between devices, shift(): lax.ppermute(value, axis, [(i, (i + step) % total) for i in range(total)])  31.9 us
    pallas_call x2, Pallas kernels, attend_back(): pl.pallas_call(functools.partial(attend_back_kernel, HEADS_PER_STEP), gri...  30.5 us
    pallas_call x2, Pallas kernels, attend(): pl.pallas_call(functools.partial(attend_kernel, HEADS_PER_STEP), grid=(he...  29.6 us
    unnamed x228, local copies, waits for them, and re-layouts  25 us
    ppermute x24, starting transfers between devices, shift_x(): lax.ppermute(value, 'tp', [(i, (i + 2 * step) % total) for i in range(tot...  24.5 us
  transfers between devices with their start and end apart: 83, of which 24 were waited for; matrix products, arithmetic and copies ran while one was open for 10% of the time, Pallas kernels for 69%

profile of v1, /device:TPU:0, one launch (start us, length us, event | category | flops | bytes accessed | tf_op | source)
XLA Modules:
  0.0 1038.0 jit_solution(9112480622498572129)
XLA Ops:
  4.4 3.1 collective-permute-start.18
  26.0 7.1 stack_depth.3
  37.8 11.1 %stack_depth.4 = bf16[4,64,640]{2,1,0:T(8,128)(2,1)} custom-call(bf16[64,640]{1,0:T(8,128)(2,1)} %copy-done.55, bf16[64,640]{1,0:T(8,128)(2,1)} %copy-done.63, bf16[64,640]{1,0:T(8,128)(2,1)} %collective-permute-done.19.refs_2_, bf16[64,640]{1,0:T(8,128)(2,1)} %copy-done.64), custom_call_target="tpu_custom_call" | custom-call | tf_op jit(solution)/shard_map/stack_depth/pallas_call | solution.py:174
  61.6 17.0 %stack_depth.5 = bf16[4,64,1024]{2,1,0:T(8,128)(2,1)} custom-call(bf16[64,1024]{1,0:T(8,128)(2,1)} %copy-done.37, bf16[64,1024]{1,0:T(8,128)(2,1)} %copy-done.52, bf16[64,1024]{1,0:T(8,128)(2,1)} %copy-done.53, bf16[64,1024]{1,0:T(8,128)(2,1)} %copy-done.54), custom_call_target="tpu_custom_call" | custom-call | tf_op jit(solution)/shard_map/stack_depth/pallas_call | solution.py:174
  90.7 7.0 collective-permute-done.8.refs_6_
  101.5 25.0 %stack_plane.3.refs_0_ = bf16[4,4,64,384]{3,2,1,0:T(8,128)(2,1)} custom-call(bf16[2,64,384]{2,1,0:T(8,128)(2,1)} %copy-done.39, bf16[2,64,384]{2,1,0:T(8,128)(2,1)} %copy-done.38, bf16[2,64,384]{2,1,0:T(8,128)(2,1)} %copy-done.56, bf16[2,64,384]{2,1,0:T(8,128)(2,1)} %copy-done.58, bf16[2,64,384]{2,1,0:T(8,128)(2,1)} %collective-permute-done.6.refs_4_, ...), custom_call_target="tpu_custom_call" | custom-call | tf_op jit(solution)/shard_map/stack_plane/pallas_call | solution.py:174
  132.1 40.9 %stack_plane.4.refs_0_ = bf16[4,4,64,640]{3,2,1,0:T(8,128)(2,1)} custom-call(bf16[2,64,640]{2,1,0:T(8,128)(2,1)} %copy-done.19, bf16[2,64,640]{2,1,0:T(8,128)(2,1)} %copy-done.18, bf16[2,64,640]{2,1,0:T(8,128)(2,1)} %copy-done.48, bf16[2,64,640]{2,1,0:T(8,128)(2,1)} %collective-permute-done.22.refs_3_, bf16[2,64,640]{2,1,0:T(8,128)(2,1)} %copy-done.49, ...), custom_call_target="tpu_custom_call" | custom-call | tf_op jit(solution)/shard_map/stack_plane/pallas_call | solution.py:174
  188.9 6.2 collective-permute-done.35.refs_6_
  196.6 64.7 %stack_plane.5.refs_0_ = bf16[4,4,64,1024]{3,2,1,0:T(8,128)(2,1)} custom-call(bf16[2,64,1024]{2,1,0:T(8,128)(2,1)} %copy-done.14, bf16[2,64,1024]{2,1,0:T(8,128)(2,1)} %copy-done.13, bf16[2,64,1024]{2,1,0:T(8,128)(2,1)} %collective-permute-done.31.refs_2_, bf16[2,64,1024]{2,1,0:T(8,128)(2,1)} %collective-permute-done.32.refs_3_, ...), custom_call_target="tpu_custom_call" | custom-call | tf_op jit(solution)/shard_map/stack_plane/pallas_call | solution.py:174
  269.8 49.0 %place_weights.3 = (bf16[4,2,64,512]{3,2,1,0:T(8,128)(2,1)}, bf16[4,2,64,512]{3,2,1,0:T(8,128)(2,1)}, bf16[4,2,64,512]{3,2,1,0:T(8,128)(2,1)}) custom-call(bf16[4,4,64,384]{3,2,1,0:T(8,128)(2,1)} %stack_plane.3.refs_0_, bf16[4,4,64,384]{3,2,1,0:T(8,128)(2,1)} %collective-permute-done.10.refs_1_), custom_call_target="tpu_custom_call" | custom-call | tf_op jit(solution)/shard_map/place_weights/pallas_call | solution.py:174
  318.8 4.5 convolution_convert_fusion.2.k
  324.6 2.7 add_convert_fusion.v
  327.3 21.0 %attend.2 = (bf16[512,512]{1,0:T(8,128)(2,1)}, bf16[8,2048,512]{2,1,0:T(8,128)(2,1)}, f32[8,1,512]{2,1,0:T(1,128)}) custom-call(bf16[512,512]{1,0:T(8,128)(2,1)} %fusion.2.q, bf16[2048,512]{1,0:T(8,128)(2,1)} %convolution_convert_fusion.2.k, bf16[2048,512]{1,0:T(8,128)(2,1)} %add_convert_fusion.v, s32[1,512]{1,0:T(1,128)} %bitcast.286, ...), custom_call_target="tpu_custom_call" | custom-call | flops 8589934592 | bytes 16777216 | tf_op jit(solution)/shard_map/attend/pallas_call | solution.py:102
  348.4 80.9 %place_weights.4 = (bf16[4,2,64,512]{3,2,1,0:T(8,128)(2,1)}, bf16[4,2,64,512]{3,2,1,0:T(8,128)(2,1)}, bf16[4,2,64,512]{3,2,1,0:T(8,128)(2,1)}, bf16[4,2,64,512]{3,2,1,0:T(8,128)(2,1)}, bf16[4,2,64,512]{3,2,1,0:T(8,128)(2,1)}) custom-call(bf16[4,4,64,640]{3,2,1,0:T(8,128)(2,1)} %stack_plane.4.refs_0_, bf16[4,4,64,640]{3,2,1,0:T(8,128)(2,1)} %collective-permute-done.27.refs_1_), custom_call_target="tpu_custom_call" | custom-call | tf_op jit(solution)/shard_map/place_weights/pallas_call | solution.py:174
  435.8 8.6 attend.3
  446.2 128.3 %place_weights.5 = (bf16[4,2,64,2048]{3,2,1,0:T(8,128)(2,1)}, bf16[4,2,64,2048]{3,2,1,0:T(8,128)(2,1)}) custom-call(bf16[4,4,64,1024]{3,2,1,0:T(8,128)(2,1)} %stack_plane.5.refs_0_, bf16[4,4,64,1024]{3,2,1,0:T(8,128)(2,1)} %collective-permute-done.37.refs_1_), custom_call_target="tpu_custom_call" | custom-call | tf_op jit(solution)/shard_map/place_weights/pallas_call | solution.py:174
  574.5 3.8 multiply_convert_fusion.1
  590.6 8.2 attend_back.2
  603.0 22.3 %attend_back.3 = (bf16[512,512]{1,0:T(8,128)(2,1)}, bf16[2048,512]{1,0:T(8,128)(2,1)}, bf16[2048,512]{1,0:T(8,128)(2,1)}) custom-call(bf16[512,512]{1,0:T(8,128)(2,1)} %fusion.2.q, bf16[2048,512]{1,0:T(8,128)(2,1)} %convolution_convert_fusion.2.k, bf16[2048,512]{1,0:T(8,128)(2,1)} %add_convert_fusion.v, bf16[8,2048,512]{2,1,0:T(8,128)(2,1)} %get-tuple-element.70.weights, ...), custom_call_target="tpu_custom_call" | custom-call | flops 17179869184 | bytes 16777216 | tf_op jit(solution)/shard_map/attend_back/pallas_call | solution.py:132
  625.3 3.0 fusion.94
  636.1 2.7 convolution_convert_fusion.1
  649.4 3.3 fusion.93
  662.3 12.3 %collective-permute-done.80 = f32[8704]{0:T(1024)S(1)} collective-permute-done((f32[8704]{0:T(1024)S(1)}, f32[8704]{0:T(1024)S(1)}, u32[]{:S(2)}, u32[]{:S(2)}) %collective-permute-start.80) | collective-permute-done | bytes 34848 | tf_op jit(solution)/shard_map/ppermute | solution.py:407
  681.0 128.3 %split_weights.5 = (bf16[4,4,64,1024]{3,2,1,0:T(8,128)(2,1)}, bf16[4,4,64,1024]{3,2,1,0:T(8,128)(2,1)}) custom-call(bf16[4,2,64,2048]{3,2,1,0:T(8,128)(2,1)} %bitcast.251, bf16[4,2,64,2048]{3,2,1,0:T(8,128)(2,1)} %bitcast.252), custom_call_target="tpu_custom_call" | custom-call | tf_op jit(solution)/shard_map/split_weights/pallas_call | solution.py:174
  809.3 49.0 %split_weights.3 = (bf16[4,4,64,384]{3,2,1,0:T(8,128)(2,1)}, bf16[4,4,64,384]{3,2,1,0:T(8,128)(2,1)}) custom-call(bf16[4,2,64,512]{3,2,1,0:T(8,128)(2,1)} %bitcast.268, bf16[4,2,64,512]{3,2,1,0:T(8,128)(2,1)} %bitcast.265, bf16[4,2,64,512]{3,2,1,0:T(8,128)(2,1)} %bitcast.260), custom_call_target="tpu_custom_call" | custom-call | tf_op jit(solution)/shard_map/split_weights/pallas_call | solution.py:174
  858.3 80.9 %split_weights.4 = (bf16[4,4,64,640]{3,2,1,0:T(8,128)(2,1)}, bf16[4,4,64,640]{3,2,1,0:T(8,128)(2,1)}) custom-call(bf16[4,2,64,512]{3,2,1,0:T(8,128)(2,1)} %bitcast.250, bf16[4,2,64,512]{3,2,1,0:T(8,128)(2,1)} %bitcast.249, bf16[4,2,64,512]{3,2,1,0:T(8,128)(2,1)} %bitcast.253, bf16[4,2,64,512]{3,2,1,0:T(8,128)(2,1)} %bitcast.259, ...), custom_call_target="tpu_custom_call" | custom-call | tf_op jit(solution)/shard_map/split_weights/pallas_call | solution.py:174
  949.9 7.1 collective-permute-done.41
  969.7 2.6 collective-permute-done.54
  977.0 2.9 collective-permute-done.50
  1008.9 3.0 collective-permute-start.67
  1026.3 3.1 collective-permute-start.77
  1031.9 5.1 collective-permute-done.76
  (520 shorter events, 220.0 us)
Async XLA Ops:
  4.4 29.7 %collective-permute-start.18 = (bf16[64,640]{1,0:T(8,128)(2,1)S(1)}, bf16[64,640]{1,0:T(8,128)(2,1)S(1)}, u32[]{:S(2)}, u32[]{:S(2)}) collective-permute-start(bf16[64,640]{1,0:T(8,128)(2,1)S(1)} %constant_dynamic-update-slice_fusion.15.refs_0_), channel_id=1, source_target_pairs={{0,8},{8,16},{16,24},{24,0},{1,9},{9,17},{17,25},{25,1},{2,10},{10... | collective-permute-start | bytes 245768 | tf_op jit(solution)/shard_map/ppermute | solution.py:209
  7.4 28.8 %collective-permute-start.19 = (bf16[64,640]{1,0:T(8,128)(2,1)S(1)}, bf16[64,640]{1,0:T(8,128)(2,1)}, u32[]{:S(2)}, u32[]{:S(2)}) collective-permute-start(bf16[64,640]{1,0:T(8,128)(2,1)S(1)} %constant_dynamic-update-slice_fusion.15.refs_0_), channel_id=1, source_target_pairs={{0,16},{8,24},{16,0},{24,8},{1,17},{9,25},{17,1},{25,9},{2,18},{10... | collective-permute-start | bytes 245768 | tf_op jit(solution)/shard_map/ppermute | solution.py:209
  24.0 26.5 %collective-permute-start.28 = (bf16[64,1024]{1,0:T(8,128)(2,1)S(1)}, bf16[64,1024]{1,0:T(8,128)(2,1)S(1)}, u32[]{:S(2)}, u32[]{:S(2)}) collective-permute-start(bf16[64,1024]{1,0:T(8,128)(2,1)S(1)} %pad_maximum_fusion.12.refs_0_), channel_id=1, source_target_pairs={{0,8},{8,16},{16,24},{24,0},{1,9},{9,17},{17,25},{25,1},{2,10},{10... | collective-permute-start | bytes 393224 | tf_op jit(solution)/shard_map/ppermute | solution.py:209
  25.4 23.5 %collective-permute-start.12 = (bf16[64,512]{0,1:T(8,128)(2,1)S(1)}, bf16[64,512]{0,1:T(8,128)(2,1)S(1)}, u32[]{:S(2)}, u32[]{:S(2)}) collective-permute-start(bf16[64,512]{0,1:T(8,128)(2,1)S(1)} %bitcast.279), channel_id=1, source_target_pairs={{0,1},{1,0},{2,3},{3,2},{4,5},{5,4},{6,7},{7,6},{8,9},{9,8},{10,11... | collective-permute-start | bytes 196616 | tf_op jit(solution)/shard_map/ppermute | solution.py:199
  37.2 43.7 %collective-permute-start = (bf16[256,512]{0,1:T(8,128)(2,1)S(1)}, bf16[256,512]{0,1:T(8,128)(2,1)S(1)}, u32[]{:S(2)}, u32[]{:S(2)}) collective-permute-start(bf16[256,512]{0,1:T(8,128)(2,1)S(1)} %bitcast.277), channel_id=1, source_target_pairs={{0,1},{1,0},{2,3},{3,2},{4,5},{5,4},{6,7},{7,6},{8,9},{9,8},{10,11... | collective-permute-start | bytes 786440 | tf_op jit(solution)/shard_map/ppermute | solution.py:199
  52.1 26.6 %collective-permute-start.6 = (bf16[2,64,384]{2,1,0:T(8,128)(2,1)S(1)}, bf16[2,64,384]{2,1,0:T(8,128)(2,1)}, u32[]{:S(2)}, u32[]{:S(2)}) collective-permute-start(bf16[2,64,384]{2,1,0:T(8,128)(2,1)S(1)} %get-tuple-element.274.refs_0_), channel_id=1, source_target_pairs={{0,4},{4,0},{1,5},{5,1},{2,6},{6,2},{3,7},{7,3},{8,12},{12,8},{9,1... | collective-permute-start | bytes 294920 | tf_op jit(solution)/shard_map/ppermute | solution.py:209
  53.7 30.7 %collective-permute-start.21 = (bf16[2,64,640]{2,1,0:T(8,128)(2,1)S(1)}, bf16[2,64,640]{2,1,0:T(8,128)(2,1)S(1)}, u32[]{:S(2)}, u32[]{:S(2)}) collective-permute-start(bf16[2,64,640]{2,1,0:T(8,128)(2,1)S(1)} %get-tuple-element.265.refs_0_), channel_id=1, source_target_pairs={{0,2},{1,3},{2,0},{3,1},{4,6},{5,7},{6,4},{7,5},{8,10},{9,11},{10,... | collective-permute-start | bytes 491528 | tf_op jit(solution)/shard_map/ppermute | solution.py:204
  55.2 31.3 %collective-permute-start.23 = (bf16[2,64,640]{2,1,0:T(8,128)(2,1)S(1)}, bf16[2,64,640]{2,1,0:T(8,128)(2,1)S(1)}, u32[]{:S(2)}, u32[]{:S(2)}) collective-permute-start(bf16[2,64,640]{2,1,0:T(8,128)(2,1)S(1)} %get-tuple-element.265.refs_0_), channel_id=1, source_target_pairs={{0,4},{4,0},{1,5},{5,1},{2,6},{6,2},{3,7},{7,3},{8,12},{12,8},{9,1... | collective-permute-start | bytes 491528 | tf_op jit(solution)/shard_map/ppermute | solution.py:209
  56.1 29.9 %collective-permute-start.22 = (bf16[2,64,640]{2,1,0:T(8,128)(2,1)S(1)}, bf16[2,64,640]{2,1,0:T(8,128)(2,1)}, u32[]{:S(2)}, u32[]{:S(2)}) collective-permute-start(bf16[2,64,640]{2,1,0:T(8,128)(2,1)S(1)} %get-tuple-element.264.refs_1_), channel_id=1, source_target_pairs={{0,2},{1,3},{2,0},{3,1},{4,6},{5,7},{6,4},{7,5},{8,10},{9,11},{10,... | collective-permute-start | bytes 491528 | tf_op jit(solution)/shard_map/ppermute | solution.py:204
  83.8 42.7 %collective-permute-start.11 = (bf16[320,512]{0,1:T(8,128)(2,1)S(1)}, bf16[320,512]{0,1:T(8,128)(2,1)S(1)}, u32[]{:S(2)}, u32[]{:S(2)}) collective-permute-start(bf16[320,512]{0,1:T(8,128)(2,1)S(1)} %pad_maximum_fusion.5), channel_id=1, source_target_pairs={{0,2},{1,3},{2,0},{3,1},{4,6},{5,7},{6,4},{7,5},{8,10},{9,11},{10,... | collective-permute-start | bytes 983048 | tf_op jit(solution)/shard_map/ppermute | solution.py:204
  84.4 43.4 %collective-permute-start.14 = (bf16[320,512]{0,1:T(8,128)(2,1)S(1)}, bf16[320,512]{0,1:T(8,128)(2,1)S(1)}, u32[]{:S(2)}, u32[]{:S(2)}) collective-permute-start(bf16[320,512]{0,1:T(8,128)(2,1)S(1)} %pad_maximum_fusion.5), channel_id=1, source_target_pairs={{0,4},{4,0},{1,5},{5,1},{2,6},{6,2},{3,7},{7,3},{8,12},{12,8},{9,1... | collective-permute-start | bytes 983048 | tf_op jit(solution)/shard_map/ppermute | solution.py:209
  88.7 40.3 %collective-permute-start.25 = (bf16[2,64,640]{2,1,0:T(8,128)(2,1)S(1)}, bf16[2,64,640]{2,1,0:T(8,128)(2,1)S(1)}, u32[]{:S(2)}, u32[]{:S(2)}) collective-permute-start(bf16[2,64,640]{2,1,0:T(8,128)(2,1)S(1)} %collective-permute-done.21.refs_2_), channel_id=1, source_target_pairs={{0,4},{4,0},{1,5},{5,1},{2,6},{6,2},{3,7},{7,3},{8,12},{12,8},{9,1... | collective-permute-start | bytes 491528 | tf_op jit(solution)/shard_map/ppermute | solution.py:209
  97.7 32.7 %collective-permute-start.26 = (bf16[2,64,640]{2,1,0:T(8,128)(2,1)}, bf16[2,64,640]{2,1,0:T(8,128)(2,1)}, u32[]{:S(2)}, u32[]{:S(2)}) collective-permute-start(bf16[2,64,640]{2,1,0:T(8,128)(2,1)} %collective-permute-done.24.refs_5_), channel_id=1, source_target_pairs={{0,2},{1,3},{2,0},{3,1},{4,6},{5,7},{6,4},{7,5},{8,10},{9,11},{10,... | collective-permute-start | bytes 491528 | tf_op jit(solution)/shard_map/ppermute | solution.py:204
  99.5 73.5 %collective-permute-start.13 = (bf16[320,512]{0,1:T(8,128)(2,1)}, bf16[320,512]{0,1:T(8,128)(2,1)}, u32[]{:S(2)}, u32[]{:S(2)}) collective-permute-start(bf16[320,512]{0,1:T(8,128)(2,1)} %constant_dynamic-update-slice_fusion.3), channel_id=1, source_target_pairs={{0,2},{1,3},{2,0},{3,1},{4,6},{5,7},{6,4},{7,5},{8,10},{9,11},{10,... | collective-permute-start | bytes 983048 | tf_op jit(solution)/shard_map/ppermute | solution.py:204
  126.5 50.1 %collective-permute-start.31 = (bf16[2,64,1024]{2,1,0:T(8,128)(2,1)S(1)}, bf16[2,64,1024]{2,1,0:T(8,128)(2,1)}, u32[]{:S(2)}, u32[]{:S(2)}) collective-permute-start(bf16[2,64,1024]{2,1,0:T(8,128)(2,1)S(1)} %get-tuple-element.260.refs_0_), channel_id=1, source_target_pairs={{0,2},{1,3},{2,0},{3,1},{4,6},{5,7},{6,4},{7,5},{8,10},{9,11},{10,... | collective-permute-start | bytes 786440 | tf_op jit(solution)/shard_map/ppermute | solution.py:204
  127.8 49.2 %collective-permute-start.33 = (bf16[2,64,1024]{2,1,0:T(8,128)(2,1)S(1)}, bf16[2,64,1024]{2,1,0:T(8,128)(2,1)}, u32[]{:S(2)}, u32[]{:S(2)}) collective-permute-start(bf16[2,64,1024]{2,1,0:T(8,128)(2,1)S(1)} %get-tuple-element.260.refs_0_), channel_id=1, source_target_pairs={{0,4},{4,0},{1,5},{5,1},{2,6},{6,2},{3,7},{7,3},{8,12},{12,8},{9,1... | collective-permute-start | bytes 786440 | tf_op jit(solution)/shard_map/ppermute | solution.py:209
  129.1 47.6 %collective-permute-start.32 = (bf16[2,64,1024]{2,1,0:T(8,128)(2,1)S(1)}, bf16[2,64,1024]{2,1,0:T(8,128)(2,1)}, u32[]{:S(2)}, u32[]{:S(2)}) collective-permute-start(bf16[2,64,1024]{2,1,0:T(8,128)(2,1)S(1)} %get-tuple-element.259.refs_1_), channel_id=1, source_target_pairs={{0,2},{1,3},{2,0},{3,1},{4,6},{5,7},{6,4},{7,5},{8,10},{9,11},{10,... | collective-permute-start | bytes 786440 | tf_op jit(solution)/shard_map/ppermute | solution.py:204
  130.5 48.3 %collective-permute-start.34 = (bf16[2,64,1024]{2,1,0:T(8,128)(2,1)S(1)}, bf16[2,64,1024]{2,1,0:T(8,128)(2,1)}, u32[]{:S(2)}, u32[]{:S(2)}) collective-permute-start(bf16[2,64,1024]{2,1,0:T(8,128)(2,1)S(1)} %get-tuple-element.259.refs_1_), channel_id=1, source_target_pairs={{0,4},{4,0},{1,5},{5,1},{2,6},{6,2},{3,7},{7,3},{8,12},{12,8},{9,1... | collective-permute-start | bytes 786440 | tf_op jit(solution)/shard_map/ppermute | solution.py:209
  176.6 93.2 %collective-permute-start.10 = (bf16[4,4,64,384]{3,2,1,0:T(8,128)(2,1)S(1)}, bf16[4,4,64,384]{3,2,1,0:T(8,128)(2,1)}, u32[]{:S(2)}, u32[]{:S(2)}) collective-permute-start(bf16[4,4,64,384]{3,2,1,0:T(8,128)(2,1)S(1)} %copy-done.5), channel_id=1, source_target_pairs={{0,1},{1,0},{2,3},{3,2},{4,5},{5,4},{6,7},{7,6},{8,9},{9,8},{10,11... | collective-permute-start | bytes 2359304 | tf_op jit(solution)/shard_map/ppermute | solution.py:199
  176.6 84.6 %collective-permute-start.16 = (bf16[320,512]{0,1:T(8,128)(2,1)}, bf16[320,512]{0,1:T(8,128)(2,1)}, u32[]{:S(2)}, u32[]{:S(2)}) collective-permute-start(bf16[320,512]{0,1:T(8,128)(2,1)} %copy-done.40), channel_id=1, source_target_pairs={{0,4},{4,0},{1,5},{5,1},{2,6},{6,2},{3,7},{7,3},{8,12},{12,8},{9,1... | collective-permute-start | bytes 983048 | tf_op jit(solution)/shard_map/ppermute | solution.py:209
  183.2 81.9 %collective-permute-start.17 = (bf16[320,512]{0,1:T(8,128)(2,1)}, bf16[320,512]{0,1:T(8,128)(2,1)S(1)}, u32[]{:S(2)}, u32[]{:S(2)}) collective-permute-start(bf16[320,512]{0,1:T(8,128)(2,1)} %collective-permute-done.15), channel_id=1, source_target_pairs={{0,2},{1,3},{2,0},{3,1},{4,6},{5,7},{6,4},{7,5},{8,10},{9,11},{10,... | collective-permute-start | bytes 983048 | tf_op jit(solution)/shard_map/ppermute | solution.py:204
  195.1 384.9 %collective-permute-start.39 = (bf16[256,512]{0,1:T(8,128)(2,1)}, bf16[256,512]{0,1:T(8,128)(2,1)}, u32[]{:S(2)}, u32[]{:S(2)}) collective-permute-start(bf16[256,512]{0,1:T(8,128)(2,1)} %bitcast.34), channel_id=1, source_target_pairs={{0,1},{1,0},{2,3},{3,2},{4,5},{5,4},{6,7},{7,6},{8,9},{9,8},{10,11... | collective-permute-start | bytes 786440 | tf_op jit(solution)/shard_map/ppermute | solution.py:199
  196.5 151.8 %collective-permute-start.27 = (bf16[4,4,64,640]{3,2,1,0:T(8,128)(2,1)S(1)}, bf16[4,4,64,640]{3,2,1,0:T(8,128)(2,1)}, u32[]{:S(2)}, u32[]{:S(2)}) collective-permute-start(bf16[4,4,64,640]{3,2,1,0:T(8,128)(2,1)S(1)} %copy-done.2), channel_id=1, source_target_pairs={{0,1},{1,0},{2,3},{3,2},{4,5},{5,4},{6,7},{7,6},{8,9},{9,8},{10,11... | collective-permute-start | bytes 3932168 | tf_op jit(solution)/shard_map/ppermute | solution.py:199
  261.3 184.9 %collective-permute-start.37 = (bf16[4,4,64,1024]{3,2,1,0:T(8,128)(2,1)}, bf16[4,4,64,1024]{3,2,1,0:T(8,128)(2,1)}, u32[]{:S(2)}, u32[]{:S(2)}) collective-permute-start(bf16[4,4,64,1024]{3,2,1,0:T(8,128)(2,1)} %stack_plane.5.refs_0_), channel_id=1, source_target_pairs={{0,1},{1,0},{2,3},{3,2},{4,5},{5,4},{6,7},{7,6},{8,9},{9,8},{10,11... | collective-permute-start | bytes 6291464 | tf_op jit(solution)/shard_map/ppermute | solution.py:199
  644.2 301.1 %collective-permute-start.38 = (f32[256,512]{0,1:T(8,128)}, f32[256,512]{0,1:T(8,128)}, u32[]{:S(2)}, u32[]{:S(2)}) collective-permute-start(f32[256,512]{0,1:T(8,128)} %get-tuple-element.245), channel_id=1, source_target_pairs={{0,1},{1,0},{2,3},{3,2},{4,5},{5,4},{6,7},{7,6},{8,9},{9,8},{10,11... | collective-permute-start | bytes 1572872 | tf_op jit(solution)/shard_map/ppermute | solution.py:199
  654.2 295.6 %collective-permute-start.42 = (bf16[320,512]{0,1:T(8,128)(2,1)S(1)}, bf16[320,512]{0,1:T(8,128)(2,1)}, u32[]{:S(2)}, u32[]{:S(2)}) collective-permute-start(bf16[320,512]{0,1:T(8,128)(2,1)S(1)} %pad_maximum_fusion.7), channel_id=1, source_target_pairs={{0,4},{4,0},{1,5},{5,1},{2,6},{6,2},{3,7},{7,3},{8,12},{12,8},{9,1... | collective-permute-start | bytes 983048 | tf_op jit(solution)/shard_map/ppermute | solution.py:209
  657.6 284.0 %collective-permute-start.40 = (bf16[320,512]{0,1:T(8,128)(2,1)}, bf16[320,512]{0,1:T(8,128)(2,1)}, u32[]{:S(2)}, u32[]{:S(2)}) collective-permute-start(bf16[320,512]{0,1:T(8,128)(2,1)} %pad_maximum_fusion.6), channel_id=1, source_target_pairs={{0,4},{4,0},{1,5},{5,1},{2,6},{6,2},{3,7},{7,3},{8,12},{12,8},{9,1... | collective-permute-start | bytes 983048 | tf_op jit(solution)/shard_map/ppermute | solution.py:209
  661.6 281.9 %collective-permute-start.44 = (bf16[320,512]{0,1:T(8,128)(2,1)}, bf16[320,512]{0,1:T(8,128)(2,1)S(1)}, u32[]{:S(2)}, u32[]{:S(2)}) collective-permute-start(bf16[320,512]{0,1:T(8,128)(2,1)} %pad_maximum_fusion.9), channel_id=1, source_target_pairs={{0,2},{1,3},{2,0},{3,1},{4,6},{5,7},{6,4},{7,5},{8,10},{9,11},{10,... | collective-permute-start | bytes 983048 | tf_op jit(solution)/shard_map/ppermute | solution.py:204
  678.6 260.6 %collective-permute-start.82 = (f32[8704]{0:T(1024)S(1)}, f32[8704]{0:T(1024)S(1)}, u32[]{:S(2)}, u32[]{:S(2)}) collective-permute-start(f32[8704]{0:T(1024)S(1)} %add.770), channel_id=1, source_target_pairs={{0,16},{8,24},{16,0},{24,8},{1,17},{9,25},{17,1},{25,9},{2,18},{10... | collective-permute-start | bytes 104456 | tf_op jit(solution)/shard_map/ppermute | solution.py:407
  949.9 33.1 %collective-permute-start.58 = (bf16[4,4,64,640]{3,2,1,0:T(8,128)(2,1)}, bf16[4,4,64,640]{3,2,1,0:T(8,128)(2,1)}, u32[]{:S(2)}, u32[]{:S(2)}) collective-permute-start(bf16[4,4,64,640]{3,2,1,0:T(8,128)(2,1)} %get-tuple-element.80), channel_id=1, source_target_pairs={{0,1},{1,0},{2,3},{3,2},{4,5},{5,4},{6,7},{7,6},{8,9},{9,8},{10,11... | collective-permute-start | bytes 3932168 | tf_op jit(solution)/shard_map/ppermute | solution.py:199
  957.0 36.1 %collective-permute-start.68 = (bf16[4,4,64,1024]{3,2,1,0:T(8,128)(2,1)}, bf16[4,4,64,1024]{3,2,1,0:T(8,128)(2,1)}, u32[]{:S(2)}, u32[]{:S(2)}) collective-permute-start(bf16[4,4,64,1024]{3,2,1,0:T(8,128)(2,1)} %get-tuple-element.82), channel_id=1, source_target_pairs={{0,1},{1,0},{2,3},{3,2},{4,5},{5,4},{6,7},{7,6},{8,9},{9,8},{10,11... | collective-permute-start | bytes 6291464 | tf_op jit(solution)/shard_map/ppermute | solution.py:199
  968.9 49.3 %collective-permute-start.46 = (f32[256,512]{0,1:T(8,128)}, f32[256,512]{0,1:T(8,128)}, u32[]{:S(2)}, u32[]{:S(2)}) collective-permute-start(f32[256,512]{0,1:T(8,128)} %get-tuple-element.216), channel_id=1, source_target_pairs={{0,1},{1,0},{2,3},{3,2},{4,5},{5,4},{6,7},{7,6},{8,9},{9,8},{10,11... | collective-permute-start | bytes 1572872 | tf_op jit(solution)/shard_map/ppermute | solution.py:199
  (147 other events, 2117.6 us)

commit v2 on v1

--- a/solution.py
+++ b/solution.py
@@ -174,9 +174,10 @@
     return pl.pallas_call(
         body,
         in_specs=[pl.BlockSpec(memory_space=pl.ANY)] * len(sources),
-        out_specs=[pl.BlockSpec(memory_space=pl.ANY)] * len(shapes),
+        out_specs=[pl.BlockSpec(memory_space=pltpu.VMEM)] * len(shapes),
         out_shape=[jax.ShapeDtypeStruct(shape, BF16) for shape in shapes],
         scratch_shapes=[pltpu.SemaphoreType.DMA((count,))],
+        compiler_params=pltpu.CompilerParams(vmem_limit_bytes=VMEM_BYTES),
         name=name,
     )(*sources)
 

time: 1040 us -> 401 us (0.39)
  Pallas kernels: 742 us -> 95.1 us
  waiting for transfers between devices: 63.3 us -> 76.3 us
    pallas_call x12, Pallas kernels: 682 us -> 35 us  [move(): pl.pallas_call(body, in_specs=[pl.BlockSpec(memory_space=pl.ANY)] * len(s...]
    unnamed x228 -> x240, local copies, waits for them, and re-layouts: 25 us -> 18.9 us
  transfers between devices with their start and end apart: 83 -> 83, of which waited for: 24 -> 27; matrix products, arithmetic and copies ran while one was open for 10% -> 24% of each run, Pallas kernels for 69% -> 16%
where the time goes in v2:
time: 401 us; the launch traced here: 394 us
  Pallas kernels  95.1 us (24%)
  starting transfers between devices  85.7 us (21%)
  waiting for transfers between devices  76.3 us (19%)
  matrix products  55.1 us (14%)
  local copies, waits for them, and re-layouts  42.9 us (11%)
  other arithmetic  35.6 us (9%)
    dot_general x30, matrix products, contract(): lax.dot_general(left, right, (((left_dim,), (right_dim,)), ((), ())), pre...  55.1 us
    ppermute x42, starting transfers between devices, shift(): lax.ppermute(value, axis, [(i, (i + step) % total) for i in range(total)])  52.6 us
    ppermute x42, waiting for transfers between devices, shift(): lax.ppermute(value, axis, [(i, (i + step) % total) for i in range(total)])  38.5 us
    pallas_call x12, Pallas kernels, move(): pl.pallas_call(body, in_specs=[pl.BlockSpec(memory_space=pl.ANY)] * len(s...  35 us
    pallas_call x2, Pallas kernels, attend_back(): pl.pallas_call(functools.partial(attend_back_kernel, HEADS_PER_STEP), gri...  30.5 us
    pallas_call x2, Pallas kernels, attend(): pl.pallas_call(functools.partial(attend_kernel, HEADS_PER_STEP), grid=(he...  29.6 us
    ppermute x24, starting transfers between devices, shift_x(): lax.ppermute(value, 'tp', [(i, (i + 2 * step) % total) for i in range(tot...  24.2 us
    ppermute x24, waiting for transfers between devices, shift_x(): lax.ppermute(value, 'tp', [(i, (i + 2 * step) % total) for i in range(tot...  21.1 us
  transfers between devices with their start and end apart: 83, of which 27 were waited for; matrix products, arithmetic and copies ran while one was open for 24% of the time, Pallas kernels for 16%

profile of v2, /device:TPU:0, one launch (start us, length us, event | category | flops | bytes accessed | tf_op | source)
XLA Modules:
  0.0 393.9 jit_solution(12454373679539320790)
XLA Ops:
  4.4 3.1 collective-permute-start.18
  7.4 2.6 collective-permute-start.19
  63.2 7.9 %collective-permute-done.8.refs_6_ = bf16[2,64,384]{2,1,0:T(8,128)(2,1)S(1)} collective-permute-done((bf16[2,64,384]{2,1,0:T(8,128)(2,1)S(1)}, bf16[2,64,384]{2,1,0:T(8,128)(2,1)S(1)}, u32[]{:S(2)}, u32[]{:S(2)}) %collective-permute-start.8) | collective-permute-done | bytes 98336 | tf_op jit(solution)/shard_map/ppermute | solution.py:210
  89.5 2.9 collective-permute-done.32.refs_3_
  100.9 8.7 %collective-permute-done.35.refs_6_ = bf16[2,64,1024]{2,1,0:T(8,128)(2,1)S(1)} collective-permute-done((bf16[2,64,1024]{2,1,0:T(8,128)(2,1)S(1)}, bf16[2,64,1024]{2,1,0:T(8,128)(2,1)S(1)}, u32[]{:S(2)}, u32[]{:S(2)}) %collective-permute-start.35) | collective-permute-done | bytes 262176 | tf_op jit(solution)/shard_map/ppermute | solution.py:210
  110.4 3.0 stack_plane.5.refs_0_
  120.1 2.8 place_weights.3
  122.9 4.5 %convolution_convert_fusion.2.k = bf16[2048,512]{1,0:T(8,128)(2,1)} fusion(bf16[2048,512]{0,1:T(8,128)(2,1)} %slice_dynamic-update-slice_fusion, bf16[512,512]{1,0:T(8,128)(2,1)} %bitcast.258), kind=kOutput, calls=%fused_computation.9 | convolution fusion | flops 1074790400 | bytes 4718592 | tf_op jit(solution)/shard_map/dot_general | solution.py:20
  128.7 2.7 add_convert_fusion.v
  131.4 21.1 %attend.2 = (bf16[512,512]{1,0:T(8,128)(2,1)}, bf16[8,2048,512]{2,1,0:T(8,128)(2,1)}, f32[8,1,512]{2,1,0:T(1,128)}) custom-call(bf16[512,512]{1,0:T(8,128)(2,1)} %fusion.2.q, bf16[2048,512]{1,0:T(8,128)(2,1)} %convolution_convert_fusion.2.k, bf16[2048,512]{1,0:T(8,128)(2,1)} %add_convert_fusion.v, s32[1,512]{1,0:T(1,128)} %bitcast.287, ...), custom_call_target="tpu_custom_call" | custom-call | flops 8589934592 | bytes 16777216 | tf_op jit(solution)/shard_map/attend/pallas_call | solution.py:102
  152.4 3.7 place_weights.4
  162.7 8.5 %attend.3 = (bf16[512,512]{1,0:T(8,128)(2,1)}, bf16[8,512,512]{2,1,0:T(8,128)(2,1)}, f32[8,1,512]{2,1,0:T(1,128)}) custom-call(bf16[512,512]{1,0:T(8,128)(2,1)} %fusion.3.q, bf16[512,512]{1,0:T(8,128)(2,1)} %convolution_convert_fusion.13.k, bf16[512,512]{1,0:T(8,128)(2,1)} %fusion.4.v, s32[1,512]{1,0:T(1,128)} %broadcast_in_dim.20.qp, s32[512,1]{1,0:T(8,128)} %copy.127.kp), custom_call_target="tpu_custom_call" | custom-call | flops 2147483648 | bytes 4194304 | tf_op jit(solution)/shard_map/attend/pallas_call | solution.py:102
  173.1 4.4 %place_weights.5 = (bf16[4,2,64,2048]{3,2,1,0:T(8,128)(2,1)}, bf16[4,2,64,2048]{3,2,1,0:T(8,128)(2,1)}) custom-call(bf16[4,4,64,1024]{3,2,1,0:T(8,128)(2,1)} %stack_plane.5.refs_0_, bf16[4,4,64,1024]{3,2,1,0:T(8,128)(2,1)} %collective-permute-done.37.refs_1_), custom_call_target="tpu_custom_call" | custom-call | tf_op jit(solution)/shard_map/place_weights/pallas_call | solution.py:174
  177.5 3.8 multiply_convert_fusion.1
  185.0 2.6 convert_reduce_fusion
  191.0 8.1 %attend_back.2 = (bf16[512,512]{1,0:T(8,128)(2,1)}, bf16[512,512]{1,0:T(8,128)(2,1)}, bf16[512,512]{1,0:T(8,128)(2,1)}) custom-call(bf16[512,512]{1,0:T(8,128)(2,1)} %fusion.3.q, bf16[512,512]{1,0:T(8,128)(2,1)} %convolution_convert_fusion.13.k, bf16[512,512]{1,0:T(8,128)(2,1)} %fusion.4.v, bf16[8,512,512]{2,1,0:T(8,128)(2,1)} %get-tuple-element.67.weights, ...), custom_call_target="tpu_custom_call" | custom-call | flops 4294967296 | bytes 4194304 | tf_op jit(solution)/shard_map/attend_back/pallas_call | solution.py:132
  203.4 22.3 %attend_back.3 = (bf16[512,512]{1,0:T(8,128)(2,1)}, bf16[2048,512]{1,0:T(8,128)(2,1)}, bf16[2048,512]{1,0:T(8,128)(2,1)}) custom-call(bf16[512,512]{1,0:T(8,128)(2,1)} %fusion.2.q, bf16[2048,512]{1,0:T(8,128)(2,1)} %convolution_convert_fusion.2.k, bf16[2048,512]{1,0:T(8,128)(2,1)} %add_convert_fusion.v, bf16[8,2048,512]{2,1,0:T(8,128)(2,1)} %get-tuple-element.70.weights, ...), custom_call_target="tpu_custom_call" | custom-call | flops 17179869184 | bytes 16777216 | tf_op jit(solution)/shard_map/attend_back/pallas_call | solution.py:132
  225.8 3.0 fusion.94
  236.5 2.7 convolution_convert_fusion.1
  239.2 2.6 convolution_convert_fusion
  249.1 3.4 fusion.93
  261.6 13.6 %collective-permute-done.80 = f32[8704]{0:T(1024)S(1)} collective-permute-done((f32[8704]{0:T(1024)S(1)}, f32[8704]{0:T(1024)S(1)}, u32[]{:S(2)}, u32[]{:S(2)}) %collective-permute-start.80) | collective-permute-done | bytes 34848 | tf_op jit(solution)/shard_map/ppermute | solution.py:408
  275.2 3.0 collective-permute-start.81
  280.1 2.7 collective-permute-start.82
  283.6 4.4 %split_weights.5 = (bf16[4,4,64,1024]{3,2,1,0:T(8,128)(2,1)}, bf16[4,4,64,1024]{3,2,1,0:T(8,128)(2,1)}) custom-call(bf16[4,2,64,2048]{3,2,1,0:T(8,128)(2,1)} %bitcast.251, bf16[4,2,64,2048]{3,2,1,0:T(8,128)(2,1)} %bitcast.252), custom_call_target="tpu_custom_call" | custom-call | tf_op jit(solution)/shard_map/split_weights/pallas_call | solution.py:174
  288.0 2.9 split_weights.3
  290.8 3.8 split_weights.4
  304.7 8.1 %collective-permute-done.41 = bf16[320,512]{0,1:T(8,128)(2,1)} collective-permute-done((bf16[320,512]{0,1:T(8,128)(2,1)}, bf16[320,512]{0,1:T(8,128)(2,1)}, u32[]{:S(2)}, u32[]{:S(2)}) %collective-permute-start.41) | collective-permute-done | bytes 327712 | tf_op jit(solution)/shard_map/ppermute | solution.py:205
  332.7 2.9 collective-permute-done.50
  364.8 3.1 collective-permute-start.67
  382.7 2.5 collective-permute-start.77
  387.8 5.1 %collective-permute-done.76 = bf16[64,1024]{1,0:T(8,128)(2,1)S(1)} collective-permute-done((bf16[64,1024]{1,0:T(8,128)(2,1)S(1)}, bf16[64,1024]{1,0:T(8,128)(2,1)S(1)}, u32[]{:S(2)}, u32[]{:S(2)}) %collective-permute-start.76) | collective-permute-done | bytes 131104 | tf_op jit(solution)/shard_map/ppermute | solution.py:210
  (532 shorter events, 214.2 us)
Async XLA Ops:
  4.4 25.7 %collective-permute-start.18 = (bf16[64,640]{1,0:T(8,128)(2,1)S(1)}, bf16[64,640]{1,0:T(8,128)(2,1)S(1)}, u32[]{:S(2)}, u32[]{:S(2)}) collective-permute-start(bf16[64,640]{1,0:T(8,128)(2,1)S(1)} %constant_dynamic-update-slice_fusion.15.refs_0_), channel_id=1, source_target_pairs={{0,8},{8,16},{16,24},{24,0},{1,9},{9,17},{17,25},{25,1},{2,10},{10... | collective-permute-start | bytes 245768 | tf_op jit(solution)/shard_map/ppermute | solution.py:210
  7.4 24.8 %collective-permute-start.19 = (bf16[64,640]{1,0:T(8,128)(2,1)S(1)}, bf16[64,640]{1,0:T(8,128)(2,1)}, u32[]{:S(2)}, u32[]{:S(2)}) collective-permute-start(bf16[64,640]{1,0:T(8,128)(2,1)S(1)} %constant_dynamic-update-slice_fusion.15.refs_0_), channel_id=1, source_target_pairs={{0,16},{8,24},{16,0},{24,8},{1,17},{9,25},{17,1},{25,9},{2,18},{10... | collective-permute-start | bytes 245768 | tf_op jit(solution)/shard_map/ppermute | solution.py:210
  33.2 19.8 %collective-permute-start = (bf16[256,512]{0,1:T(8,128)(2,1)S(1)}, bf16[256,512]{0,1:T(8,128)(2,1)S(1)}, u32[]{:S(2)}, u32[]{:S(2)}) collective-permute-start(bf16[256,512]{0,1:T(8,128)(2,1)S(1)} %bitcast.278), channel_id=1, source_target_pairs={{0,1},{1,0},{2,3},{3,2},{4,5},{5,4},{6,7},{7,6},{8,9},{9,8},{10,11... | collective-permute-start | bytes 786440 | tf_op jit(solution)/shard_map/ppermute | solution.py:200
  41.5 16.7 %collective-permute-start.21 = (bf16[2,64,640]{2,1,0:T(8,128)(2,1)S(1)}, bf16[2,64,640]{2,1,0:T(8,128)(2,1)S(1)}, u32[]{:S(2)}, u32[]{:S(2)}) collective-permute-start(bf16[2,64,640]{2,1,0:T(8,128)(2,1)S(1)} %get-tuple-element.265.refs_0_), channel_id=1, source_target_pairs={{0,2},{1,3},{2,0},{3,1},{4,6},{5,7},{6,4},{7,5},{8,10},{9,11},{10,... | collective-permute-start | bytes 491528 | tf_op jit(solution)/shard_map/ppermute | solution.py:205
  43.1 17.3 %collective-permute-start.23 = (bf16[2,64,640]{2,1,0:T(8,128)(2,1)S(1)}, bf16[2,64,640]{2,1,0:T(8,128)(2,1)S(1)}, u32[]{:S(2)}, u32[]{:S(2)}) collective-permute-start(bf16[2,64,640]{2,1,0:T(8,128)(2,1)S(1)} %get-tuple-element.265.refs_0_), channel_id=1, source_target_pairs={{0,4},{4,0},{1,5},{5,1},{2,6},{6,2},{3,7},{7,3},{8,12},{12,8},{9,1... | collective-permute-start | bytes 491528 | tf_op jit(solution)/shard_map/ppermute | solution.py:210
  44.3 15.3 %collective-permute-start.22 = (bf16[2,64,640]{2,1,0:T(8,128)(2,1)S(1)}, bf16[2,64,640]{2,1,0:T(8,128)(2,1)S(1)}, u32[]{:S(2)}, u32[]{:S(2)}) collective-permute-start(bf16[2,64,640]{2,1,0:T(8,128)(2,1)S(1)} %get-tuple-element.264.refs_1_), channel_id=1, source_target_pairs={{0,2},{1,3},{2,0},{3,1},{4,6},{5,7},{6,4},{7,5},{8,10},{9,11},{10,... | collective-permute-start | bytes 491528 | tf_op jit(solution)/shard_map/ppermute | solution.py:205
  57.1 19.7 %collective-permute-start.11 = (bf16[320,512]{0,1:T(8,128)(2,1)S(1)}, bf16[320,512]{0,1:T(8,128)(2,1)S(1)}, u32[]{:S(2)}, u32[]{:S(2)}) collective-permute-start(bf16[320,512]{0,1:T(8,128)(2,1)S(1)} %pad_maximum_fusion.5), channel_id=1, source_target_pairs={{0,2},{1,3},{2,0},{3,1},{4,6},{5,7},{6,4},{7,5},{8,10},{9,11},{10,... | collective-permute-start | bytes 983048 | tf_op jit(solution)/shard_map/ppermute | solution.py:205
  58.3 19.7 %collective-permute-start.14 = (bf16[320,512]{0,1:T(8,128)(2,1)S(1)}, bf16[320,512]{0,1:T(8,128)(2,1)S(1)}, u32[]{:S(2)}, u32[]{:S(2)}) collective-permute-start(bf16[320,512]{0,1:T(8,128)(2,1)S(1)} %pad_maximum_fusion.5), channel_id=1, source_target_pairs={{0,4},{4,0},{1,5},{5,1},{2,6},{6,2},{3,7},{7,3},{8,12},{12,8},{9,1... | collective-permute-start | bytes 983048 | tf_op jit(solution)/shard_map/ppermute | solution.py:210
  61.8 17.5 %collective-permute-start.25 = (bf16[2,64,640]{2,1,0:T(8,128)(2,1)S(1)}, bf16[2,64,640]{2,1,0:T(8,128)(2,1)S(1)}, u32[]{:S(2)}, u32[]{:S(2)}) collective-permute-start(bf16[2,64,640]{2,1,0:T(8,128)(2,1)S(1)} %collective-permute-done.21.refs_2_), channel_id=1, source_target_pairs={{0,4},{4,0},{1,5},{5,1},{2,6},{6,2},{3,7},{7,3},{8,12},{12,8},{9,1... | collective-permute-start | bytes 491528 | tf_op jit(solution)/shard_map/ppermute | solution.py:210
  72.3 14.3 %collective-permute-start.13 = (bf16[320,512]{0,1:T(8,128)(2,1)}, bf16[320,512]{0,1:T(8,128)(2,1)S(1)}, u32[]{:S(2)}, u32[]{:S(2)}) collective-permute-start(bf16[320,512]{0,1:T(8,128)(2,1)} %constant_dynamic-update-slice_fusion.3), channel_id=1, source_target_pairs={{0,2},{1,3},{2,0},{3,1},{4,6},{5,7},{6,4},{7,5},{8,10},{9,11},{10,... | collective-permute-start | bytes 983048 | tf_op jit(solution)/shard_map/ppermute | solution.py:205
  78.0 15.7 %collective-permute-start.33 = (bf16[2,64,1024]{2,1,0:T(8,128)(2,1)S(1)}, bf16[2,64,1024]{2,1,0:T(8,128)(2,1)S(1)}, u32[]{:S(2)}, u32[]{:S(2)}) collective-permute-start(bf16[2,64,1024]{2,1,0:T(8,128)(2,1)S(1)} %get-tuple-element.260.refs_0_), channel_id=1, source_target_pairs={{0,4},{4,0},{1,5},{5,1},{2,6},{6,2},{3,7},{7,3},{8,12},{12,8},{9,1... | collective-permute-start | bytes 786440 | tf_op jit(solution)/shard_map/ppermute | solution.py:210
  80.2 14.2 %collective-permute-start.34 = (bf16[2,64,1024]{2,1,0:T(8,128)(2,1)S(1)}, bf16[2,64,1024]{2,1,0:T(8,128)(2,1)}, u32[]{:S(2)}, u32[]{:S(2)}) collective-permute-start(bf16[2,64,1024]{2,1,0:T(8,128)(2,1)S(1)} %get-tuple-element.259.refs_1_), channel_id=1, source_target_pairs={{0,4},{4,0},{1,5},{5,1},{2,6},{6,2},{3,7},{7,3},{8,12},{12,8},{9,1... | collective-permute-start | bytes 786440 | tf_op jit(solution)/shard_map/ppermute | solution.py:210
  89.4 30.6 %collective-permute-start.10 = (bf16[4,4,64,384]{3,2,1,0:T(8,128)(2,1)S(1)}, bf16[4,4,64,384]{3,2,1,0:T(8,128)(2,1)}, u32[]{:S(2)}, u32[]{:S(2)}) collective-permute-start(bf16[4,4,64,384]{3,2,1,0:T(8,128)(2,1)S(1)} %copy-done.5), channel_id=1, source_target_pairs={{0,1},{1,0},{2,3},{3,2},{4,5},{5,4},{6,7},{7,6},{8,9},{9,8},{10,11... | collective-permute-start | bytes 2359304 | tf_op jit(solution)/shard_map/ppermute | solution.py:200
  92.4 21.1 %collective-permute-start.16 = (bf16[320,512]{0,1:T(8,128)(2,1)S(1)}, bf16[320,512]{0,1:T(8,128)(2,1)S(1)}, u32[]{:S(2)}, u32[]{:S(2)}) collective-permute-start(bf16[320,512]{0,1:T(8,128)(2,1)S(1)} %collective-permute-done.11), channel_id=1, source_target_pairs={{0,4},{4,0},{1,5},{5,1},{2,6},{6,2},{3,7},{7,3},{8,12},{12,8},{9,1... | collective-permute-start | bytes 983048 | tf_op jit(solution)/shard_map/ppermute | solution.py:210
  93.7 15.9 %collective-permute-start.35 = (bf16[2,64,1024]{2,1,0:T(8,128)(2,1)S(1)}, bf16[2,64,1024]{2,1,0:T(8,128)(2,1)S(1)}, u32[]{:S(2)}, u32[]{:S(2)}) collective-permute-start(bf16[2,64,1024]{2,1,0:T(8,128)(2,1)S(1)} %collective-permute-done.31.refs_2_), channel_id=1, source_target_pairs={{0,4},{4,0},{1,5},{5,1},{2,6},{6,2},{3,7},{7,3},{8,12},{12,8},{9,1... | collective-permute-start | bytes 786440 | tf_op jit(solution)/shard_map/ppermute | solution.py:210
  94.4 15.3 %collective-permute-start.36 = (bf16[2,64,1024]{2,1,0:T(8,128)(2,1)}, bf16[2,64,1024]{2,1,0:T(8,128)(2,1)S(1)}, u32[]{:S(2)}, u32[]{:S(2)}) collective-permute-start(bf16[2,64,1024]{2,1,0:T(8,128)(2,1)} %collective-permute-done.34.refs_5_), channel_id=1, source_target_pairs={{0,2},{1,3},{2,0},{3,1},{4,6},{5,7},{6,4},{7,5},{8,10},{9,11},{10,... | collective-permute-start | bytes 786440 | tf_op jit(solution)/shard_map/ppermute | solution.py:205
  98.6 16.7 %collective-permute-start.17 = (bf16[320,512]{0,1:T(8,128)(2,1)S(1)}, bf16[320,512]{0,1:T(8,128)(2,1)S(1)}, u32[]{:S(2)}, u32[]{:S(2)}) collective-permute-start(bf16[320,512]{0,1:T(8,128)(2,1)S(1)} %collective-permute-done.15), channel_id=1, source_target_pairs={{0,2},{1,3},{2,0},{3,1},{4,6},{5,7},{6,4},{7,5},{8,10},{9,11},{10,... | collective-permute-start | bytes 983048 | tf_op jit(solution)/shard_map/ppermute | solution.py:205
  109.6 73.3 %collective-permute-start.39 = (bf16[256,512]{0,1:T(8,128)(2,1)}, bf16[256,512]{0,1:T(8,128)(2,1)S(1)}, u32[]{:S(2)}, u32[]{:S(2)}) collective-permute-start(bf16[256,512]{0,1:T(8,128)(2,1)} %bitcast.34), channel_id=1, source_target_pairs={{0,1},{1,0},{2,3},{3,2},{4,5},{5,4},{6,7},{7,6},{8,9},{9,8},{10,11... | collective-permute-start | bytes 786440 | tf_op jit(solution)/shard_map/ppermute | solution.py:200
  109.7 42.8 %collective-permute-start.27 = (bf16[4,4,64,640]{3,2,1,0:T(8,128)(2,1)S(1)}, bf16[4,4,64,640]{3,2,1,0:T(8,128)(2,1)}, u32[]{:S(2)}, u32[]{:S(2)}) collective-permute-start(bf16[4,4,64,640]{3,2,1,0:T(8,128)(2,1)S(1)} %copy-done.2), channel_id=1, source_target_pairs={{0,1},{1,0},{2,3},{3,2},{4,5},{5,4},{6,7},{7,6},{8,9},{9,8},{10,11... | collective-permute-start | bytes 3932168 | tf_op jit(solution)/shard_map/ppermute | solution.py:200
  113.4 59.6 %collective-permute-start.37 = (bf16[4,4,64,1024]{3,2,1,0:T(8,128)(2,1)}, bf16[4,4,64,1024]{3,2,1,0:T(8,128)(2,1)}, u32[]{:S(2)}, u32[]{:S(2)}) collective-permute-start(bf16[4,4,64,1024]{3,2,1,0:T(8,128)(2,1)} %stack_plane.5.refs_0_), channel_id=1, source_target_pairs={{0,1},{1,0},{2,3},{3,2},{4,5},{5,4},{6,7},{7,6},{8,9},{9,8},{10,11... | collective-permute-start | bytes 6291464 | tf_op jit(solution)/shard_map/ppermute | solution.py:200
  243.6 58.1 %collective-permute-start.38 = (f32[256,512]{0,1:T(8,128)S(1)}, f32[256,512]{0,1:T(8,128)S(1)}, u32[]{:S(2)}, u32[]{:S(2)}) collective-permute-start(f32[256,512]{0,1:T(8,128)S(1)} %get-tuple-element.245), channel_id=1, source_target_pairs={{0,1},{1,0},{2,3},{3,2},{4,5},{5,4},{6,7},{7,6},{8,9},{9,8},{10,11... | collective-permute-start | bytes 1572872 | tf_op jit(solution)/shard_map/ppermute | solution.py:200
  254.5 50.1 %collective-permute-start.42 = (bf16[320,512]{0,1:T(8,128)(2,1)}, bf16[320,512]{0,1:T(8,128)(2,1)}, u32[]{:S(2)}, u32[]{:S(2)}) collective-permute-start(bf16[320,512]{0,1:T(8,128)(2,1)} %pad_maximum_fusion.7), channel_id=1, source_target_pairs={{0,4},{4,0},{1,5},{5,1},{2,6},{6,2},{3,7},{7,3},{8,12},{12,8},{9,1... | collective-permute-start | bytes 983048 | tf_op jit(solution)/shard_map/ppermute | solution.py:210
  256.9 39.9 %collective-permute-start.40 = (bf16[320,512]{0,1:T(8,128)(2,1)S(1)}, bf16[320,512]{0,1:T(8,128)(2,1)}, u32[]{:S(2)}, u32[]{:S(2)}) collective-permute-start(bf16[320,512]{0,1:T(8,128)(2,1)S(1)} %pad_maximum_fusion.6), channel_id=1, source_target_pairs={{0,4},{4,0},{1,5},{5,1},{2,6},{6,2},{3,7},{7,3},{8,12},{12,8},{9,1... | collective-permute-start | bytes 983048 | tf_op jit(solution)/shard_map/ppermute | solution.py:210
  259.9 15.3 %collective-permute-start.80 = (f32[8704]{0:T(1024)S(1)}, f32[8704]{0:T(1024)S(1)}, u32[]{:S(2)}, u32[]{:S(2)}) collective-permute-start(f32[8704]{0:T(1024)S(1)} %add.768), channel_id=1, source_target_pairs={{0,4},{4,0},{1,5},{5,1},{2,6},{6,2},{3,7},{7,3},{8,12},{12,8},{9,1... | collective-permute-start | bytes 104456 | tf_op jit(solution)/shard_map/ppermute | solution.py:408
  260.7 38.0 %collective-permute-start.44 = (bf16[320,512]{0,1:T(8,128)(2,1)S(1)}, bf16[320,512]{0,1:T(8,128)(2,1)}, u32[]{:S(2)}, u32[]{:S(2)}) collective-permute-start(bf16[320,512]{0,1:T(8,128)(2,1)S(1)} %pad_maximum_fusion.9), channel_id=1, source_target_pairs={{0,2},{1,3},{2,0},{3,1},{4,6},{5,7},{6,4},{7,5},{8,10},{9,11},{10,... | collective-permute-start | bytes 983048 | tf_op jit(solution)/shard_map/ppermute | solution.py:205
  280.1 14.5 %collective-permute-start.82 = (f32[8704]{0:T(1024)S(1)}, f32[8704]{0:T(1024)S(1)}, u32[]{:S(2)}, u32[]{:S(2)}) collective-permute-start(f32[8704]{0:T(1024)S(1)} %add.770), channel_id=1, source_target_pairs={{0,16},{8,24},{16,0},{24,8},{1,17},{9,25},{17,1},{25,9},{2,18},{10... | collective-permute-start | bytes 104456 | tf_op jit(solution)/shard_map/ppermute | solution.py:408
  294.6 19.4 %collective-permute-start.43 = (bf16[320,512]{0,1:T(8,128)(2,1)}, bf16[320,512]{0,1:T(8,128)(2,1)}, u32[]{:S(2)}, u32[]{:S(2)}) collective-permute-start(bf16[320,512]{0,1:T(8,128)(2,1)} %pad_maximum_fusion.8), channel_id=1, source_target_pairs={{0,2},{1,3},{2,0},{3,1},{4,6},{5,7},{6,4},{7,5},{8,10},{9,11},{10,... | collective-permute-start | bytes 983048 | tf_op jit(solution)/shard_map/ppermute | solution.py:205
  296.8 18.4 %collective-permute-start.48 = (bf16[4,4,64,384]{3,2,1,0:T(8,128)(2,1)}, bf16[4,4,64,384]{3,2,1,0:T(8,128)(2,1)}, u32[]{:S(2)}, u32[]{:S(2)}) collective-permute-start(bf16[4,4,64,384]{3,2,1,0:T(8,128)(2,1)} %get-tuple-element.78), channel_id=1, source_target_pairs={{0,1},{1,0},{2,3},{3,2},{4,5},{5,4},{6,7},{7,6},{8,9},{9,8},{10,11... | collective-permute-start | bytes 2359304 | tf_op jit(solution)/shard_map/ppermute | solution.py:200
  298.6 14.2 %collective-permute-start.41 = (bf16[320,512]{0,1:T(8,128)(2,1)}, bf16[320,512]{0,1:T(8,128)(2,1)}, u32[]{:S(2)}, u32[]{:S(2)}) collective-permute-start(bf16[320,512]{0,1:T(8,128)(2,1)} %add_convert_fusion.2), channel_id=1, source_target_pairs={{0,2},{1,3},{2,0},{3,1},{4,6},{5,7},{6,4},{7,5},{8,10},{9,11},{10,... | collective-permute-start | bytes 983048 | tf_op jit(solution)/shard_map/ppermute | solution.py:205
  304.7 35.3 %collective-permute-start.58 = (bf16[4,4,64,640]{3,2,1,0:T(8,128)(2,1)}, bf16[4,4,64,640]{3,2,1,0:T(8,128)(2,1)}, u32[]{:S(2)}, u32[]{:S(2)}) collective-permute-start(bf16[4,4,64,640]{3,2,1,0:T(8,128)(2,1)} %get-tuple-element.80), channel_id=1, source_target_pairs={{0,1},{1,0},{2,3},{3,2},{4,5},{5,4},{6,7},{7,6},{8,9},{9,8},{10,11... | collective-permute-start | bytes 3932168 | tf_op jit(solution)/shard_map/ppermute | solution.py:200
  312.8 37.1 %collective-permute-start.68 = (bf16[4,4,64,1024]{3,2,1,0:T(8,128)(2,1)}, bf16[4,4,64,1024]{3,2,1,0:T(8,128)(2,1)S(1)}, u32[]{:S(2)}, u32[]{:S(2)}) collective-permute-start(bf16[4,4,64,1024]{3,2,1,0:T(8,128)(2,1)} %get-tuple-element.82), channel_id=1, source_target_pairs={{0,1},{1,0},{2,3},{3,2},{4,5},{5,4},{6,7},{7,6},{8,9},{9,8},{10,11... | collective-permute-start | bytes 6291464 | tf_op jit(solution)/shard_map/ppermute | solution.py:200
  324.7 50.0 %collective-permute-start.46 = (f32[256,512]{0,1:T(8,128)}, f32[256,512]{0,1:T(8,128)}, u32[]{:S(2)}, u32[]{:S(2)}) collective-permute-start(f32[256,512]{0,1:T(8,128)} %get-tuple-element.216), channel_id=1, source_target_pairs={{0,1},{1,0},{2,3},{3,2},{4,5},{5,4},{6,7},{7,6},{8,9},{9,8},{10,11... | collective-permute-start | bytes 1572872 | tf_op jit(solution)/shard_map/ppermute | solution.py:200
  (153 other events, 1360.7 us)

commit v3 on v2

v3 whole, which is shorter than its diff:
```python
import functools

import jax
import jax.numpy as jnp
from jax import lax
from jax.experimental import pallas as pl
from jax.experimental.pallas import tpu as pltpu
from jax.sharding import PartitionSpec as P

HEAD_DIM = 64
EPSILON = 1e-05
NEGATIVE = -1e30
F32 = jnp.float32
BF16 = jnp.bfloat16
SCALE = HEAD_DIM ** -0.5
VMEM_BYTES = 58 * 2 ** 20


def contract(left, right, left_dim, right_dim):
    return lax.dot_general(
        left, right, (((left_dim,), (right_dim,)), ((), ())), preferred_element_type=F32
    )


def product(left, right):
    return contract(left, right, 1, 0)


def product_left(left, right):
    return contract(left, right, 0, 0)


def product_right(left, right):
    return contract(left, right, 1, 1)


def layer_norm(values, gain, shift):
    center = values - jnp.mean(values, axis=-1, keepdims=True)
    spread = jnp.mean(center * center, axis=-1, keepdims=True)
    return center * lax.rsqrt(spread + EPSILON) * gain + shift


def norm_back(values, gain, grad):
    center = values - jnp.mean(values, axis=-1, keepdims=True)
    spread = jnp.mean(center * center, axis=-1, keepdims=True)
    rate = lax.rsqrt(spread + EPSILON)
    normal = center * rate
    scaled = grad * gain
    back = rate * (
        scaled
        - jnp.mean(scaled, axis=-1, keepdims=True)
        - normal * jnp.mean(scaled * normal, axis=-1, keepdims=True)
    )
    return back, jnp.sum(grad * normal, axis=0), jnp.sum(grad, axis=0)


def attend_kernel(heads, q, k, v, qp, kp, *refs):
    out, exact, weights, inverse = refs[-4:]
    allowed = kp[...] <= qp[...]
    for head in range(heads):
        cols = slice(head * HEAD_DIM, (head + 1) * HEAD_DIM)
        scores = contract(k[:, cols], q[:, cols] * SCALE, 1, 1)
        scores = jnp.where(allowed, scores, NEGATIVE)
        largest = jnp.max(scores, axis=0, keepdims=True)
        power = jnp.exp(scores - largest)
        rate = 1.0 / jnp.sum(power, axis=0, keepdims=True)
        low = power.astype(BF16)
        weights[head] = low
        inverse[head] = rate
        mixed = contract(v[:, cols], low, 0, 0) * rate
        exact[cols, :] = mixed
        out[:, cols] = mixed.T.astype(BF16)


def attend_back_kernel(heads, q, k, v, weights, inverse, exact, grad, *refs):
    dq, dk, dv = refs[-3:]
    for head in range(heads):
        cols = slice(head * HEAD_DIM, (head + 1) * HEAD_DIM)
        grads = grad[:, cols].astype(F32).T
        inner = jnp.sum(grads * exact[cols, :], axis=0, keepdims=True) * inverse[head]
        scaled = (grads * inverse[head]).astype(BF16)
        weight = weights[head]
        grad_weight = contract(v[:, cols], scaled, 1, 0)
        grad_scores = (weight.astype(F32) * (grad_weight - inner)).astype(BF16)
        dq[:, cols] = (contract(k[:, cols], grad_scores, 0, 0) * SCALE).T.astype(BF16)
        dv[:, cols] = contract(weight, scaled, 1, 1).astype(BF16)
        dk[:, cols] = (contract(grad_scores, q[:, cols], 1, 0) * SCALE).astype(BF16)


HEADS_PER_STEP = 2


def attend_call(body, arrays, specs, shapes, out_specs, earlier, steps, cost, name):
    given = [] if earlier is None else list(earlier)
    return pl.pallas_call(
        functools.partial(body, HEADS_PER_STEP),
        grid=(steps,),
        in_specs=specs + [pl.BlockSpec(memory_space=pl.ANY)] * len(given),
        out_specs=out_specs,
        out_shape=shapes,
        input_output_aliases={len(arrays) + i: i for i in range(len(given))},
        compiler_params=pltpu.CompilerParams(vmem_limit_bytes=VMEM_BYTES),
        cost_estimate=cost,
        name=name,
    )(*arrays, *given)


def head_specs(first):
    def columns(rows):
        return pl.BlockSpec((rows, HEADS_PER_STEP * HEAD_DIM), lambda i: (0, i + first))

    def lines(rows):
        return pl.BlockSpec((HEADS_PER_STEP * HEAD_DIM, rows), lambda i: (i + first, 0))

    def heads(*dims):
        return pl.BlockSpec((HEADS_PER_STEP,) + dims, lambda i: (i + first, 0, 0))

    return columns, lines, heads


def attend(q, k, v, qp, kp, part=0, parts=1, earlier=None):
    rows, width = q.shape
    keys = k.shape[0]
    heads = width // HEAD_DIM
    steps = heads // HEADS_PER_STEP // parts
    columns, lines, by_head = head_specs(part * steps)
    return attend_call(
        attend_kernel,
        (q, k, v, qp, kp),
        [
            columns(rows),
            columns(keys),
            columns(keys),
            pl.BlockSpec((1, rows), lambda i: (0, 0)),
            pl.BlockSpec((keys, 1), lambda i: (0, 0)),
        ],
        [
            jax.ShapeDtypeStruct((rows, width), BF16),
            jax.ShapeDtypeStruct((width, rows), F32),
            jax.ShapeDtypeStruct((heads, keys, rows), BF16),
            jax.ShapeDtypeStruct((heads, 1, rows), F32),
        ],
        [columns(rows), lines(rows), by_head(keys, rows), by_head(1, rows)],
        earlier,
        steps,
        pl.CostEstimate(
            flops=16 * rows * keys * width // parts,
            transcendentals=heads * rows * keys // parts,
            bytes_accessed=2 * heads * rows * keys // parts,
        ),
        "attend",
    )


def attend_back(q, k, v, weights, inverse, exact, grad, part=0, parts=1, earlier=None):
    rows, width = q.shape
    keys = k.shape[0]
    heads = width // HEAD_DIM
    steps = heads // HEADS_PER_STEP // parts
    columns, lines, by_head = head_specs(part * steps)
    return attend_call(
        attend_back_kernel,
        (q, k, v, weights, inverse, exact, grad),
        [
            columns(rows),
            columns(keys),
            columns(keys),
            by_head(keys, rows),
            by_head(1, rows),
            lines(rows),
            columns(rows),
        ],
        [
            jax.ShapeDtypeStruct((rows, width), BF16),
            jax.ShapeDtypeStruct((keys, width), BF16),
            jax.ShapeDtypeStruct((keys, width), BF16),
        ],
        [columns(rows), columns(keys), columns(keys)],
        earlier,
        steps,
        pl.CostEstimate(
            flops=32 * rows * keys * width // parts,
            transcendentals=0,
            bytes_accessed=2 * heads * rows * keys // parts,
        ),
        "attend_back",
    )


def move(sources, shapes, plan, name):
    def body(*refs):
        given = refs[: len(sources)]
        made = refs[len(sources) : len(sources) + len(shapes)]
        sems = refs[-1]
        copies = []
        for at, (i, a, j, b) in enumerate(plan()):
            copies.append(pltpu.make_async_copy(given[i].at[a], made[j].at[b], sems.at[at]))
        for copy in copies:
            copy.start()
        for copy in copies:
            copy.wait()

    count = move_count(plan)
    return pl.pallas_call(
        body,
        in_specs=[pl.BlockSpec(memory_space=pl.ANY)] * len(sources),
        out_specs=[pl.BlockSpec(memory_space=pltpu.VMEM)] * len(shapes),
        out_shape=[jax.ShapeDtypeStruct(shape, BF16) for shape in shapes],
        scratch_shapes=[pltpu.SemaphoreType.DMA((count,))],
        compiler_params=pltpu.CompilerParams(vmem_limit_bytes=VMEM_BYTES),
        name=name,
    )(*sources)


def move_count(plan):
    return len(plan())


def sizes():
    return lax.axis_size("fsdp"), lax.axis_size("ctx"), lax.axis_size("tp") // 2


def places():
    tp = lax.axis_index("tp")
    return lax.axis_index("fsdp"), lax.axis_index("ctx"), tp // 2, tp % 2


def swap(value):
    total = lax.axis_size("tp")
    return lax.ppermute(value, "tp", [(i, i ^ 1) for i in range(total)])


def shift_x(value, step):
    total = lax.axis_size("tp")
    return lax.ppermute(value, "tp", [(i, (i + 2 * step) % total) for i in range(total)])


def shift(value, axis, step):
    total = lax.axis_size(axis)
    return lax.ppermute(value, axis, [(i, (i + step) % total) for i in range(total)])


def offsets():
    unused, high, wide = sizes()
    return [(dx, dy) for dy in range(high) for dx in range(wide)]


def is_square():
    unused, high, wide = sizes()
    return high == 2 and wide == 2


def shift_plane(value, dx, dy):
    high, total = lax.axis_size("ctx"), lax.axis_size("tp")
    pairs = [
        (c * total + t, (c + dy) % high * total + (t + 2 * dx) % total)
        for c in range(high)
        for t in range(total)
    ]
    return lax.ppermute(value, ("ctx", "tp"), pairs)


def plane_direct(value):
    return [(value,)] + [(shift_plane(value, dx, dy),) for dx, dy in offsets()[1:]]


def sum_direct(blocks):
    moved = [(shift_plane(b[0], -dx, -dy),) for b, (dx, dy) in zip(blocks[1:], offsets()[1:])]
    return [blocks[0]] + moved


def plane_one(first, second):
    if is_square():
        side = (shift_x(first, 1), shift_x(second, 1))
        front = (shift(first, "ctx", 1), shift(second, "ctx", 1))
        return [(first, second), side, front]
    unused, high, wide = sizes()
    row = [(first, second)] + [(shift_x(first, k), shift_x(second, k)) for k in range(1, wide)]
    blocks = list(row)
    for step in range(1, high):
        blocks += [(shift(a, "ctx", step), shift(b, "ctx", step)) for a, b in row]
    return blocks


def plane_two(blocks):
    if is_square():
        own, side, front = blocks
        return [own, side, front, (shift(side[0], "ctx", 1), shift_x(front[1], 1))]
    return blocks


def add(left, right):
    return (left.astype(F32) + right.astype(F32)).astype(BF16)


def add_kernel(*refs):
    count = len(refs) // 3
    for n in range(count):
        total = refs[n][...].astype(F32) + refs[count + n][...].astype(F32)
        refs[2 * count + n][...] = total.astype(BF16)


def add_many(left, right):
    steps = left[0].shape[0]
    if sum(part.size for part in left) < 2**20:
        steps = 1

    def spec(part):
        rest = part.shape[1:]
        return pl.BlockSpec((part.shape[0] // steps,) + rest, lambda i: (i,) + (0,) * len(rest))

    return pl.pallas_call(
        add_kernel,
        grid=(steps,),
        in_specs=[spec(part) for part in left] * 2,
        out_specs=[spec(part) for part in left],
        out_shape=[jax.ShapeDtypeStruct(part.shape, BF16) for part in left],
        name="add_many",
    )(*left, *right)


def sum_one(blocks):
    if is_square():
        own, side, front, far = blocks
        return [own, side, front, (shift(far[0], "ctx", 1), shift_x(far[1], 1))]
    return blocks


def sum_adds(blocks):
    if is_square():
        own, side, front, far = blocks
        first, second = add_many([side[0], front[1]], [far[0], far[1]])
        return [own, (first, side[1]), (front[0], second)]
    return blocks


def sum_two(blocks):
    if is_square():
        own, side, front = blocks
        from_side = (shift_x(side[0], 1), shift_x(side[1], 1))
        from_front = (shift(front[0], "ctx", 1), shift(front[1], "ctx", 1))
        return [own, from_side, from_front]
    unused, high, wide = sizes()
    row = []
    for dx in range(wide):
        total = blocks[dx]
        for dy in range(1, high):
            other = blocks[dy * wide + dx]
            total = tuple(add(a, shift(b, "ctx", -dy)) for a, b in zip(total, other))
        row.append(total)
    return [row[0]] + [
        (shift_x(row[dx][0], -dx), shift_x(row[dx][1], -dx)) for dx in range(1, wide)
    ]


def summed(parts):
    return sum(part.astype(F32) for part in parts)


def spread(packed):
    return [packed] + [shift(packed, "fsdp", k) for k in range(1, lax.axis_size("fsdp"))]


def depth_blocks(pieces, cuts, name):
    deep = len(pieces)
    rows, total = pieces[0].shape
    half = rows // cuts

    def by_depth():
        at = lax.axis_index("fsdp")
        steps = []
        for k in range(deep):
            for h in range(cuts):
                steps.append((k, slice(h * half, (h + 1) * half), h, (at - k + deep) % deep))
        return steps

    return move(pieces, [(deep, half, total)] * cuts, by_depth, name)


def aligned(widths):
    return all(width % 128 == 0 for width in widths)


def column_starts(widths):
    return [sum(widths[:i]) for i in range(len(widths))]


def block_place(n, who):
    unused, high, wide = sizes()
    unused, y, x, core = places()
    dx, dy = offsets()[n]
    at_y = (y - dy + high) % high
    at_x = (x - dx + wide) % wide
    return at_y, 2 * at_x + (core if who == 0 else 1 - core)


def whole_weights(blocks, widths, name):
    deep, high, wide = sizes()
    half, total = blocks[0][0].shape[1:]
    cuts = len(blocks[0])
    rows = cuts * half
    others = [tuple(swap(part) for part in block) for block in blocks]
    starts = column_starts(widths)
    if aligned(widths):

        def into_place():
            steps = []
            for n in range(len(blocks)):
                for who in range(2):
                    at_y, at = block_place(n, who)
                    for h in range(cuts):
                        lines = slice(h * half, (h + 1) * half)
                        for j, width in enumerate(widths):
                            cols = slice(starts[j], starts[j] + width)
                            here = pl.ds(pl.multiple_of(at * width, 128), width)
                            steps.append(
                                (
                                    (cuts * n + h) + cuts * len(blocks) * who,
                                    (slice(None), slice(None), cols),
                                    j,
                                    (slice(None), at_y, lines, here),
                                )
                            )
            return steps

        made = move(
            [part for block in blocks + others for part in block],
            [(deep, high, rows, 2 * wide * width) for width in widths],
            into_place,
            name,
        )
        return [m.reshape(deep * high * rows, -1) for m in made]
    whole = jnp.zeros((high, 2 * wide, deep, rows, total), BF16)
    for n in range(len(blocks)):
        for who, part in ((0, blocks[n]), (1, others[n])):
            at = block_place(n, who) + (0, 0, 0)
            part = jnp.concatenate(part, axis=1)[None, None]
            whole = lax.dynamic_update_slice(whole, part, at)
    made = []
    for start, width in zip(starts, widths):
        part = whole[..., start : start + width]
        part = part.transpose(2, 0, 3, 1, 4)
        made.append(part.reshape(deep * high * rows, 2 * wide * width))
    return made


def split_grads(grads, widths, cuts, riders, name):
    deep, high, wide = sizes()
    rows = grads[0].shape[0] // (deep * high)
    half = rows // cuts
    total = sum(widths)
    count = len(offsets())
    starts = column_starts(widths)
    if aligned(widths):
        shaped = [g.reshape(deep, high, rows, 2 * wide * w) for g, w in zip(grads, widths)]

        def into_blocks():
            steps = []
            for n in range(count):
                for who in range(2):
                    at_y, at = block_place(n, who)
                    for h in range(cuts):
                        lines = slice(h * half, (h + 1) * half)
                        for j, width in enumerate(widths):
                            cols = slice(starts[j], starts[j] + width)
                            here = pl.ds(pl.multiple_of(at * width, 128), width)
                            steps.append(
                                (
                                    j,
                                    (slice(None), at_y, lines, here),
                                    cuts * (n + count * who) + h,
                                    (slice(None), lines_of(h), cols),
                                )
                            )
                        if h == 0 and riders is not None:
                            below = slice(half, half + riders.shape[1])
                            steps.append(
                                (
                                    len(widths),
                                    (slice(None), slice(None), slice(None)),
                                    cuts * (n + count * who),
                                    (slice(None), below, slice(None)),
                                )
                            )
            return steps

        def lines_of(h):
            return slice(0, half)

        sizes_made = [(deep, half, total)] * cuts
        if riders is not None:
            sizes_made[0] = (deep, half + riders.shape[1], total)
            shaped.append(riders)
        made = move(shaped, sizes_made * (2 * count), into_blocks, name)
        pairs = [tuple(made[cuts * n : cuts * (n + 1)]) for n in range(2 * count)]
        return pairs[:count], pairs[count:]
    whole = jnp.concatenate(
        [g.reshape(deep, high, rows, 2 * wide, w) for g, w in zip(grads, widths)], axis=-1
    ).transpose(1, 3, 0, 2, 4)

    def pick(n, who):
        at = block_place(n, who) + (0, 0, 0)
        part = lax.dynamic_slice(whole, at, (1, 1, deep, rows, total))[0, 0]
        return tuple(part[:, h * half : (h + 1) * half] for h in range(cuts))

    return [pick(n, 0) for n in range(count)], [pick(n, 1) for n in range(count)]


def swap_blocks(blocks):
    return [tuple(swap(part) for part in block) for block in blocks]


def add_blocks(blocks, others):
    made = add_many([a for x in blocks for a in x], [b for y in others for b in y])
    each = len(blocks[0])
    return [tuple(made[each * n : each * (n + 1)]) for n in range(len(blocks))]


def depth_sum(left):
    deep = lax.axis_size("fsdp")
    own = [summed([part[h] for part in left]) for h in range(len(left[0]))]
    own = jnp.concatenate(own, axis=1) if len(own) > 1 else own[0]
    low = own.astype(BF16)
    at = lax.axis_index("fsdp")
    result = lax.dynamic_index_in_dim(own, at, 0, keepdims=False)
    moved = []
    for k in range(1, deep):
        piece = lax.dynamic_index_in_dim(low, (at + k) % deep, 0, keepdims=False)
        moved.append(shift(piece, "fsdp", k))
    return result, moved


def depth_rest(result, moved, end, lines=0):
    result = result + summed(moved)
    if lines:
        rest = [result[: end - lines]] + ([result[end:]] if end < result.shape[0] else [])
        return jnp.concatenate(rest, axis=0), result[end - lines : end]
    return result


def after(value, *gates):
    return lax.optimization_barrier((value,) + gates)[0]


def gated(blocks, *gates):
    flat = [part for block in blocks for part in block]
    made = list(lax.optimization_barrier(tuple(flat) + gates))
    out = []
    for block in blocks:
        out.append(tuple(made[: len(block)]))
        made = made[len(block) :]
    return [out] + made


def regroup(first, second, third):
    made = gated(first + second + third)[0]
    at = len(first)
    return made[:at], made[at : at + len(second)], made[-1]


def row_grads_kernel(own_rows, own_memory, dk, dv, wk, wv, memory, own, own_mem, *blocks):
    n = pl.program_id(0)
    part = product_right(dk[...], wk[...]) + product_right(dv[...], wv[...])

    @pl.when(n == 0)
    def _():
        own[...] = part
        own_mem[...] = memory[...]

    for m in range(1, len(blocks) // 2 + 1):

        @pl.when(n == m)
        def _():
            for h in range(2):
                block = blocks[2 * (m - 1) + h]
                block[:own_rows] = part[h * own_rows : (h + 1) * own_rows].astype(BF16)
                lines = slice(h * own_memory, (h + 1) * own_memory)
                block[own_rows:] = memory[lines].astype(BF16)


def row_grads(dk, dv, wk, wv, memory, own_rows):
    count = len(offsets())
    width = wk.shape[0]
    own_memory = memory.shape[0] // (2 * count)

    def rows_of(size, columns):
        return pl.BlockSpec((size, columns), lambda n: (n, 0))

    def whole(*shape):
        return pl.BlockSpec(shape, lambda n: (0, 0))

    block = (own_rows + own_memory, width)
    own, own_mem, *blocks = pl.pallas_call(
        functools.partial(row_grads_kernel, own_rows, own_memory),
        grid=(count,),
        in_specs=[
            rows_of(2 * own_rows, dk.shape[1]),
            rows_of(2 * own_rows, dv.shape[1]),
            whole(*wk.shape),
            whole(*wv.shape),
            rows_of(2 * own_memory, width),
        ],
        out_specs=[whole(2 * own_rows, width), whole(2 * own_memory, width)]
        + [whole(*block)] * (2 * (count - 1)),
        out_shape=[
            jax.ShapeDtypeStruct((2 * own_rows, width), F32),
            jax.ShapeDtypeStruct((2 * own_memory, width), F32),
        ]
        + [jax.ShapeDtypeStruct(block, BF16)] * (2 * (count - 1)),
        compiler_params=pltpu.CompilerParams(vmem_limit_bytes=VMEM_BYTES),
        name="row_grads",
    )(dk, dv, wk, wv, memory)
    pairs = [(blocks[2 * n], blocks[2 * n + 1]) for n in range(count - 1)]
    return own, own_mem, [pairs[0]] + pairs


RIDER_LINES = 8


def pack_kernel(chunk, *refs):
    made = refs[-1]
    made[...] = jnp.zeros(made.shape, BF16)
    per_line = made.shape[2] // chunk
    at = 0
    for ref in refs[:-1]:
        for row in range(ref.shape[0]):
            for start in range(0, ref.shape[1], chunk):
                line, column = at // per_line, at % per_line * chunk
                value = ref[row : row + 1, start : start + chunk].astype(BF16)
                for copy in range(made.shape[0]):
                    made[copy, line : line + 1, column : column + chunk] = value
                at += 1


def pack_riders(vectors, chunk, deep, total):
    return pl.pallas_call(
        functools.partial(pack_kernel, chunk),
        out_shape=jax.ShapeDtypeStruct((deep, RIDER_LINES, total), BF16),
        name="pack_riders",
    )(*[v.reshape(-1, vectors[0].shape[0]) for v in vectors])


def unpack_riders(lines, chunk, lengths):
    per_line = lines.shape[1] // chunk
    flat = lines[:, : per_line * chunk].reshape(-1)
    starts = column_starts(lengths)
    return [flat[start : start + size] for start, size in zip(starts, lengths)]


def prologue_kernel(inputs, memory, *refs):
    weights, (keep, give, first, second) = refs[:10], refs[10:]
    core = lax.axis_index("tp") % 2
    rows = inputs.shape[1]
    keep[:rows] = inputs[core]
    keep[rows:] = memory[core]
    give[:rows] = inputs[1 - core]
    give[rows:] = memory[1 - core]
    for target, group in ((first, weights[:3]), (second, weights[3:])):
        start = 0
        for ref in group:
            target[:, start : start + ref.shape[1]] = ref[...]
            start += ref.shape[1]


def prologue(inputs, memory, weights):
    rows = weights[0].shape[0]
    widths = [w.shape[1] for w in weights]
    if not aligned(widths):
        core = lax.axis_index("tp") % 2
        both = jnp.concatenate([inputs, memory], axis=1)
        keep = lax.dynamic_index_in_dim(both, core, 0, keepdims=False)
        give = lax.dynamic_index_in_dim(both, 1 - core, 0, keepdims=False)
        return (
            keep,
            give,
            jnp.concatenate(weights[:3], axis=1),
            jnp.concatenate(weights[3:], axis=1),
        )
    block = (inputs.shape[1] + memory.shape[1], inputs.shape[2])
    return pl.pallas_call(
        prologue_kernel,
        out_shape=[
            jax.ShapeDtypeStruct(block, BF16),
            jax.ShapeDtypeStruct(block, BF16),
            jax.ShapeDtypeStruct((rows, sum(widths[:3])), BF16),
            jax.ShapeDtypeStruct((rows, sum(widths[3:])), BF16),
        ],
        compiler_params=pltpu.CompilerParams(vmem_limit_bytes=VMEM_BYTES),
        name="prologue",
    )(inputs, memory, *weights)


def all_sum(value, axes):
    for axis in axes:
        total = lax.axis_size(axis)
        step = 1
        while step < total:
            pairs = [(i, i ^ step) for i in range(total)]
            value = value + lax.ppermute(value, axis, pairs)
            step *= 2
    return value


def per_device(
    inputs,
    memory,
    cotangent,
    positions,
    lengths,
    memory_lengths,
    query_weight,
    key_weight,
    value_weight,
    output_weight,
    cross_query_weight,
    cross_key_weight,
    cross_value_weight,
    cross_output_weight,
    expand_weight,
    reduce_weight,
    query_bias,
    value_bias,
    output_bias,
    first_gain,
    first_shift,
    cross_query_bias,
    cross_value_bias,
    cross_output_bias,
    second_gain,
    second_shift,
    expand_bias,
    reduce_bias,
    third_gain,
    third_shift,
):
    deep, high, wide = sizes()
    z, y, x, core = places()
    own_rows, width = inputs.shape[1:]
    own_memory = memory.shape[1]
    rows = 2 * own_rows
    head_width = query_weight.shape[1]
    hidden_width = expand_weight.shape[1]

    keep, give, first_pack, second_pack = prologue(
        inputs,
        memory,
        [
            query_weight,
            key_weight,
            value_weight,
            cross_key_weight,
            cross_value_weight,
            output_weight.T,
            cross_query_weight,
            cross_output_weight.T,
            expand_weight,
            reduce_weight.T,
        ],
    )
    first_widths = [head_width] * 3
    second_widths = [head_width] * 5 + [hidden_width] * 2

    got = swap(give)
    first_pieces = spread(after(first_pack, got))
    blocks = plane_one(keep, got)
    first_depth = depth_blocks(first_pieces, 1, "stack_first")[0]
    *blocks, (first_depth,) = gated(blocks + [(first_depth,)])[0]
    blocks = plane_two(blocks)
    first_blocks = plane_direct(first_depth)
    second_pieces = spread(after(second_pack, *first_pieces[1:]))
    cotangent_pair = (
        lax.dynamic_index_in_dim(cotangent, core, 0, keepdims=False),
        swap(lax.dynamic_index_in_dim(cotangent, 1 - core, 0, keepdims=False)),
    )
    full_query, full_key, full_value = whole_weights(first_blocks, first_widths, "place_first")
    pieces = [p for b in blocks for p in b]

    def rows_together():
        steps = []
        for n in range(len(pieces)):
            at = n * own_rows
            steps.append((n, slice(0, own_rows), 0, slice(at, at + own_rows)))
            at = n * own_memory
            steps.append(
                (n, slice(own_rows, own_rows + own_memory), 1, slice(at, at + own_memory))
            )
        return steps

    wide_rows, wide_memory = move(
        pieces,
        [(len(pieces) * own_rows, width), (len(pieces) * own_memory, width)],
        rows_together,
        "rows_together",
    )
    rows_in = wide_rows[:rows]
    second_half = plane_one(
        *depth_blocks([after(p, wide_rows) for p in second_pieces], 2, "stack_second")
    )

    slots = lax.dynamic_index_in_dim(positions, core, 0, keepdims=False)
    length = lax.dynamic_index_in_dim(lengths, core, 0, keepdims=False)
    memory_length = lax.dynamic_index_in_dim(memory_lengths, core, 0, keepdims=False)
    key_positions = []
    memory_slots = []
    for dx, dy in offsets():
        at_y = (y - dy + high) % high
        at_x = (x - dx + wide) % wide
        for who in (core, 1 - core):
            block = (at_y * wide + at_x) * 2 + who
            key_positions.append(lax.dynamic_slice_in_dim(slots, block * own_rows, own_rows))
            memory_slots.append(block * own_memory + jnp.arange(own_memory, dtype=jnp.int32))
    own_positions = jnp.concatenate(key_positions[:2])
    key_positions = jnp.concatenate(key_positions)
    last = positions.shape[1]
    key_positions = jnp.where(key_positions < length, key_positions, last)[:, None]
    query_positions = own_positions[None, :]
    memory_slots = jnp.concatenate(memory_slots)[:, None]
    memory_limit = jnp.broadcast_to(memory_length - 1, (1, rows))

    query_low = (product(rows_in, full_query) + query_bias).astype(BF16)
    keys = product(wide_rows, full_key).astype(BF16)
    values = (product(wide_rows, full_value) + value_bias).astype(BF16)
    early = list(attend(query_low, keys, values, query_positions, key_positions, 0, 2))
    second_half, late_query, ready = gated(second_half, query_low, early[1])
    early[1] = ready
    second_blocks = plane_two(second_half)
    attended, attended_exact, weights, inverse = attend(
        late_query, keys, values, query_positions, key_positions, 1, 2, early
    )
    second_blocks, attended = gated(second_blocks, attended)
    (
        full_cross_key,
        full_cross_value,
        full_output,
        full_cross_query,
        full_cross_output,
        full_expand,
        full_reduce,
    ) = whole_weights(second_blocks, second_widths, "place_second")
    memory_key = product(wide_memory, full_cross_key).astype(BF16)
    memory_value = (product(wide_memory, full_cross_value) + cross_value_bias).astype(BF16)

    first_in = rows_in.astype(F32) + product_right(attended, full_output) + output_bias
    first_out = layer_norm(first_in, first_gain, first_shift)
    first_low = first_out.astype(BF16)
    cross_query = (product(first_low, full_cross_query) + cross_query_bias).astype(BF16)
    cross_attended, cross_exact, cross_weights, cross_inverse = attend(
        cross_query, memory_key, memory_value, memory_limit, memory_slots
    )
    second_in = first_out + product_right(cross_attended, full_cross_output) + cross_output_bias
    second_out = layer_norm(second_in, second_gain, second_shift)
    second_low = second_out.astype(BF16)
    expanded = product(second_low, full_expand) + expand_bias
    gate = jax.nn.sigmoid(expanded)
    activated = (expanded * gate).astype(BF16)
    third_in = second_out + product_right(activated, full_reduce) + reduce_bias
    outputs = layer_norm(third_in, third_gain, third_shift)

    grad_in = jnp.concatenate(cotangent_pair, axis=0).astype(F32)
    masked_grad = jnp.where((own_positions < length)[:, None], grad_in, 0.0)
    third_grad, third_gain_part, third_shift_part = norm_back(third_in, third_gain, masked_grad)
    third_low = third_grad.astype(BF16)
    activated_grad = product(third_low, full_reduce)
    expanded_grad = (activated_grad * gate * (1.0 + expanded * (1.0 - gate))).astype(BF16)
    third_part = [
        product_left(second_low, expanded_grad).astype(BF16),
        product_left(third_low, activated).astype(BF16),
    ]
    second_grad = third_grad + product_right(expanded_grad, full_expand)
    second_in_grad, second_gain_part, second_shift_part = norm_back(
        second_in, second_gain, second_grad
    )
    second_grad_low = second_in_grad.astype(BF16)
    cross_attended_grad = product(second_grad_low, full_cross_output).astype(BF16)
    cross_query_grad, memory_key_grad, memory_value_grad = attend_back(
        cross_query,
        memory_key,
        memory_value,
        cross_weights,
        cross_inverse,
        cross_exact,
        cross_attended_grad,
    )
    first_grad = second_in_grad + product_right(cross_query_grad, full_cross_query)
    first_in_grad, first_gain_part, first_shift_part = norm_back(first_in, first_gain, first_grad)
    first_grad_low = first_in_grad.astype(BF16)
    attended_grad = product(first_grad_low, full_output).astype(BF16)
    second_part = [
        product_left(wide_memory, memory_key_grad).astype(BF16),
        product_left(wide_memory, memory_value_grad).astype(BF16),
        product_left(first_grad_low, attended).astype(BF16),
        product_left(first_low, cross_query_grad).astype(BF16),
        product_left(second_grad_low, cross_attended).astype(BF16),
    ]
    early_vectors = [
        jnp.sum(first_in_grad, axis=0),
        first_gain_part,
        first_shift_part,
        jnp.sum(cross_query_grad.astype(F32), axis=0),
        jnp.sum(memory_value_grad.astype(F32), axis=0),
        jnp.sum(second_in_grad, axis=0),
        second_gain_part,
        second_shift_part,
        jnp.sum(expanded_grad.astype(F32), axis=0),
        jnp.sum(third_grad, axis=0),
        third_gain_part,
        third_shift_part,
    ]
    ride = aligned(first_widths + second_widths) and rows % 256 == 0
    early_riders = late_riders = None
    if ride:
        early_riders = pack_riders(early_vectors, 512, deep, sum(second_widths))
    second_keep, second_give = split_grads(
        second_part + third_part, second_widths, 2, early_riders, "split_second"
    )
    second_other = swap_blocks(second_give)
    memory_part = product_right(memory_key_grad, full_cross_key) + product_right(
        memory_value_grad, full_cross_value
    )

    second_blocks = add_blocks(second_keep, second_other)
    second_blocks, early_grad = gated(second_blocks, attended_grad)
    second_blocks = sum_one(second_blocks)
    early = list(
        attend_back(query_low, keys, values, weights, inverse, attended_exact, early_grad, 0, 2)
    )
    second_blocks, early[0] = gated(second_blocks, early[0])
    second_blocks = sum_adds(second_blocks)
    second_blocks, late_grad = gated(second_blocks, attended_grad)
    second_left = sum_two(second_blocks)
    query_grad, key_grad, value_grad = attend_back(
        query_low, keys, values, weights, inverse, attended_exact, late_grad, 1, 2, early
    )
    input_part, memory_own, low_blocks = row_grads(
        key_grad, value_grad, full_key, full_value, memory_part, own_rows
    )
    low_blocks, second_left, (query_late, key_late, value_late) = regroup(
        low_blocks, second_left, [(query_grad, key_grad, value_grad)]
    )
    low_blocks = sum_one(low_blocks)
    second_own, second_moved = depth_sum(second_left)
    input_own = first_in_grad + product_right(query_late, full_query)
    first_part = [
        product_left(rows_in, query_late).astype(BF16),
        product_left(wide_rows, key_late).astype(BF16),
        product_left(wide_rows, value_late).astype(BF16),
    ]
    late_vectors = [
        jnp.sum(query_late.astype(F32), axis=0),
        jnp.sum(value_late.astype(F32), axis=0),
    ]
    low_blocks = sum_adds(low_blocks)
    low_blocks, unused, first_part = regroup(low_blocks, [], [tuple(first_part)])
    left = sum_two(low_blocks)[1:]
    if ride:
        late_riders = pack_riders(late_vectors, 128, deep, sum(first_widths))
    first_keep, first_give = split_grads(first_part, first_widths, 1, late_riders, "split_first")
    first_other = swap_blocks(first_give)
    left, first_keep, unused = regroup(left, first_keep, [()])
    first_blocks = add_blocks(first_keep, first_other)
    first_left = sum_direct(first_blocks)
    first_left, unused, second_moved = regroup(first_left, [], [tuple(second_moved)])
    first_own, first_moved = depth_sum(first_left)
    ends = first_left[0][0].shape[1], second_left[0][0].shape[1]
    first_shard = depth_rest(first_own, first_moved, ends[0], RIDER_LINES if ride else 0)
    second_shard = depth_rest(second_own, second_moved, ends[1], RIDER_LINES if ride else 0)
    pair = [summed([part[h] for part in left]) for h in range(2)]
    input_pair = [
        input_own[h * own_rows : (h + 1) * own_rows]
        + input_part[h * own_rows : (h + 1) * own_rows]
        + pair[h][:own_rows]
        for h in range(2)
    ]
    memory_pair = [
        memory_own[h * own_memory : (h + 1) * own_memory] + pair[h][own_rows:] for h in range(2)
    ]

    def restore(pair):
        other = swap(pair[1])
        return jnp.where(
            core == 0, jnp.stack([pair[0], other]), jnp.stack([other, pair[0]])
        )

    output_result = restore([outputs[:own_rows], outputs[own_rows:]])
    input_result = restore(input_pair)
    memory_result = restore(memory_pair)

    vectors = late_vectors + early_vectors
    lengths = [v.shape[0] for v in vectors]
    if ride:
        first_shard, late_lines = first_shard
        second_shard, early_lines = second_shard
        split = unpack_riders(late_lines, 128, lengths[:2])
        split += unpack_riders(early_lines, 512, lengths[2:])
    else:
        joined = all_sum(jnp.concatenate(vectors), ("fsdp", "tp", "ctx"))
        starts = column_starts(lengths)
        split = [joined[start : start + size] for start, size in zip(starts, lengths)]

    def shards(packed, widths):
        start = 0
        parts = []
        for one in widths:
            parts.append(packed[:, start : start + one])
            start += one
        return parts

    g_query, g_key, g_value = shards(first_shard, first_widths)
    (
        g_cross_key,
        g_cross_value,
        g_output,
        g_cross_query,
        g_cross_output,
        g_expand,
        g_reduce,
    ) = shards(second_shard, second_widths)
    return (
        output_result,
        input_result,
        memory_result,
        g_query,
        g_key,
        g_value,
        g_output.T,
        g_cross_query,
        g_cross_key,
        g_cross_value,
        g_cross_output.T,
        g_expand,
        g_reduce.T,
        *split,
    )


def solution(mesh):
    rows = P("fsdp", ("ctx", "tp"), None)
    tall = P(("fsdp", "ctx"), "tp")
    flat = P("tp", ("fsdp", "ctx"))
    weights = (tall, tall, tall, flat, tall, tall, tall, flat, tall, flat)
    return jax.shard_map(
        per_device,
        mesh=mesh,
        in_specs=(rows, rows, rows, P("fsdp", None), P("fsdp"), P("fsdp"))
        + weights
        + (P(),) * 14,
        out_specs=(rows, rows, rows) + weights + (P(),) * 14,
        check_vma=False,
    )
```

time: 401 us -> 314 us (0.78)
  waiting for transfers between devices: 76.3 us -> 28.4 us
  starting transfers between devices: 85.7 us -> 54 us
  Pallas kernels: 95.1 us -> 122 us
  local copies, waits for them, and re-layouts: 42.9 us -> 26.3 us
  other arithmetic: 35.6 us -> 25.5 us
  matrix products: 55.1 us -> 49.3 us
    pallas_call x4 -> x14, Pallas kernels: 60.1 us -> 94 us  [the longest x6 67.8 us: attend_call(): pl.pallas_call(functools.partial(body, HEADS_PER_STEP), grid=(steps,), in...]
    ppermute x42 -> x24, starting transfers between devices: 52.6 us -> 27.9 us  [shift(): lax.ppermute(value, axis, [(i, (i + step) % total) for i in range(total)])]
    ppermute x42 -> x24, waiting for transfers between devices: 38.5 us -> 15.8 us  [shift(): lax.ppermute(value, axis, [(i, (i + step) % total) for i in range(total)])]
    ppermute x24 -> x12, waiting for transfers between devices: 21.1 us -> 5.13 us  [shift_x(): lax.ppermute(value, 'tp', [(i, (i + 2 * step) % total) for i in range(tot...]
    ppermute x24 -> x12, starting transfers between devices: 24.2 us -> 12.8 us  [shift_x(): lax.ppermute(value, 'tp', [(i, (i + 2 * step) % total) for i in range(tot...]
    ppermute x5 -> x6, waiting for transfers between devices: 16.6 us -> 5.88 us  [shift_plane(): return lax.ppermute(value, ('ctx', 'tp'), pairs)]
    convert_element_type x11 -> x2, other arithmetic: 9.99 us -> 0.22 us  [depth_sum(): low = own.astype(BF16)]
    pallas_call x12 -> x7, Pallas kernels: 35 us -> 27.7 us  [move(): pl.pallas_call(body, in_specs=[pl.BlockSpec(memory_space=pl.ANY)] * len(s...]
  transfers between devices with their start and end apart: 83 -> 71, of which waited for: 27 -> 16; matrix products, arithmetic and copies ran while one was open for 24% -> 22% of each run, Pallas kernels for 16% -> 33%
where the time goes in v3:
time: 314 us; the launch traced here: 308 us
  Pallas kernels  122 us (39%)
  starting transfers between devices  54 us (17%)
  matrix products  49.3 us (16%)
  waiting for transfers between devices  28.4 us (9%)
  local copies, waits for them, and re-layouts  26.3 us (8%)
  other arithmetic  25.5 us (8%)
    pallas_call x6, Pallas kernels, attend_call(): pl.pallas_call(functools.partial(body, HEADS_PER_STEP), grid=(steps,), in...  67.8 us
    dot_general x28, matrix products, contract(): lax.dot_general(left, right, (((left_dim,), (right_dim,)), ((), ())), pre...  49.3 us
    ppermute x24, starting transfers between devices, shift(): lax.ppermute(value, axis, [(i, (i + step) % total) for i in range(total)])  27.9 us
    pallas_call x7, Pallas kernels, move(): pl.pallas_call(body, in_specs=[pl.BlockSpec(memory_space=pl.ANY)] * len(s...  27.7 us
    ppermute x24, waiting for transfers between devices, shift(): lax.ppermute(value, axis, [(i, (i + step) % total) for i in range(total)])  15.8 us
    unnamed x211, local copies, waits for them, and re-layouts  15.7 us
    pallas_call x4, Pallas kernels, add_many(): pl.pallas_call(add_kernel, grid=(steps,), in_specs=[spec(part) for part i...  13.3 us
    ppermute x12, starting transfers between devices, shift_x(): lax.ppermute(value, 'tp', [(i, (i + 2 * step) % total) for i in range(tot...  12.8 us
  transfers between devices with their start and end apart: 71, of which 16 were waited for; matrix products, arithmetic and copies ran while one was open for 22% of the time, Pallas kernels for 33%

profile of v3, /device:TPU:0, one launch (start us, length us, event | category | flops | bytes accessed | tf_op | source)
XLA Modules:
  0.0 308.0 jit_solution(12718732771644703894)
XLA Ops:
  2.9 3.0 collective-permute-start.1
  12.0 2.6 collective-permute-start.6
  29.5 2.4 collective-permute-start.19
  33.1 5.4 %collective-permute-done.11.refs_2_ = bf16[64,1664]{1,0:T(8,128)(2,1)S(1)} collective-permute-done((bf16[64,1664]{1,0:T(8,128)(2,1)}, bf16[64,1664]{1,0:T(8,128)(2,1)S(1)}, u32[]{:S(2)}, u32[]{:S(2)}) %collective-permute-start.11) | collective-permute-done | bytes 213024 | tf_op jit(solution)/shard_map/ppermute | solution.py:240
  41.7 4.3 %collective-permute-done.8.refs_6_ = bf16[320,512]{1,0:T(8,128)(2,1)S(1)} collective-permute-done((bf16[320,512]{1,0:T(8,128)(2,1)S(1)}, bf16[320,512]{1,0:T(8,128)(2,1)S(1)}, u32[]{:S(2)}, u32[]{:S(2)}) %collective-permute-start.8) | collective-permute-done | bytes 327712 | tf_op jit(solution)/shard_map/ppermute | solution.py:240
  49.3 3.3 %rows_together.1 = (bf16[2048,512]{1,0:T(8,128)(2,1)}, bf16[512,512]{1,0:T(8,128)(2,1)}) custom-call(bf16[320,512]{1,0:T(8,128)(2,1)} %get-tuple-element.210.refs_0_, bf16[320,512]{1,0:T(8,128)(2,1)} %copy-done.56, bf16[320,512]{1,0:T(8,128)(2,1)} %copy-done.54, bf16[320,512]{1,0:T(8,128)(2,1)} %copy-done.57, bf16[320,512]{1,0:T(8,128)(2,1)} %copy-done.55, ...), custom_call_target="tpu_custom_call" | custom-call | tf_op jit(solution)/shard_map/rows_together/pallas_call | solution.py:204
  60.5 2.8 place_first.1
  63.4 3.7 %convolution_convert_fusion.2.k = bf16[2048,512]{1,0:T(8,128)(2,1)} fusion(bf16[2048,512]{1,0:T(8,128)(2,1)S(1)} %copy-done.1, bf16[512,512]{1,0:T(8,128)(2,1)} %bitcast.149), kind=kOutput, calls=%fused_computation.8 | convolution fusion | flops 1074790400 | bytes 4718592 | tf_op jit(solution)/shard_map/dot_general | solution.py:20
  67.1 2.6 add_convert_fusion.v
  70.9 13.2 %attend.3 = (bf16[512,512]{1,0:T(8,128)(2,1)}, f32[512,512]{1,0:T(8,128)}, bf16[8,2048,512]{2,1,0:T(8,128)(2,1)}, f32[8,1,512]{2,1,0:T(1,128)}) custom-call(bf16[512,512]{1,0:T(8,128)(2,1)} %fusion.3.q, bf16[2048,512]{1,0:T(8,128)(2,1)} %convolution_convert_fusion.2.k, bf16[2048,512]{1,0:T(8,128)(2,1)} %add_convert_fusion.v, s32[1,512]{1,0:T(1,128)} %bitcast.185, ...), custom_call_target="tpu_custom_call" | custom-call | flops 4294967296 | bytes 8388608 | tf_op jit(solution)/shard_map/attend/pallas_call | solution.py:95
  86.2 12.9 %attend.4 = (bf16[512,512]{1,0:T(8,128)(2,1)}, f32[512,512]{1,0:T(8,128)}, bf16[8,2048,512]{2,1,0:T(8,128)(2,1)}, f32[8,1,512]{2,1,0:T(1,128)}) custom-call(bf16[512,512]{1,0:T(8,128)(2,1)} %fusion.3.q, bf16[2048,512]{1,0:T(8,128)(2,1)} %convolution_convert_fusion.2.k, ...), custom_call_target="tpu_custom_call", output_to_operand_aliasing={{0}: (5, {}), {1}: (6, {}), {2}: (7, {}), {3}: (8, {})} | custom-call | flops 4294967296 | bytes 8388608 | tf_op jit(solution)/shard_map/attend/pallas_call | solution.py:95
  106.9 7.1 %place_second.1 = (bf16[4,2,64,512]{3,2,1,0:T(8,128)(2,1)}, bf16[4,2,64,512]{3,2,1,0:T(8,128)(2,1)}, bf16[4,2,64,512]{3,2,1,0:T(8,128)(2,1)}, bf16[4,2,64,512]{3...) custom-call(bf16[4,32,1664]{2,1,0:T(8,128)(2,1)} %get-tuple-element., ...), custom_call_target="tpu_custom_call" | custom-call | tf_op jit(solution)/shard_map/place_second/pallas_call | solution.py:204
  120.5 8.3 %attend.5 = (bf16[512,512]{1,0:T(8,128)(2,1)}, f32[512,512]{1,0:T(8,128)}, bf16[8,512,512]{2,1,0:T(8,128)(2,1)}, f32[8,1,512]{2,1,0:T(1,128)}) custom-call(bf16[512,512]{1,0:T(8,128)(2,1)} %fusion.4.q, bf16[512,512]{1,0:T(8,128)(2,1)} %convolution_convert_fusion.13.k, bf16[512,512]{1,0:T(8,128)(2,1)} %fusion.5.v, s32[1,512]{1,0:T(1,128)} %broadcast_in_dim.20.qp, ...), custom_call_target="tpu_custom_call" | custom-call | flops 2147483648 | bytes 4194304 | tf_op jit(solution)/shard_map/attend/pallas_call | solution.py:95
  137.0 2.6 convert_reduce_fusion.1
  144.1 8.2 %attend_back.3 = (bf16[512,512]{1,0:T(8,128)(2,1)}, bf16[512,512]{1,0:T(8,128)(2,1)}, bf16[512,512]{1,0:T(8,128)(2,1)}) custom-call(bf16[512,512]{1,0:T(8,128)(2,1)} %fusion.4.q, bf16[512,512]{1,0:T(8,128)(2,1)} %convolution_convert_fusion.13.k, bf16[512,512]{1,0:T(8,128)(2,1)} %fusion.5.v, bf16[8,512,512]{2,1,0:T(8,128)(2,1)} %get-tuple-element.260.weights, ...), custom_call_target="tpu_custom_call" | custom-call | flops 4294967296 | bytes 4194304 | tf_op jit(solution)/shard_map/attend_back/pallas_call | solution.py:95
  152.3 2.5 multiply_reduce_fusion.2
  157.6 2.8 convolution_convert_fusion.1
  160.3 2.6 convolution_convert_fusion
  172.3 7.7 %split_second.1 = (bf16[4,40,1664]{2,1,0:T(8,128)(2,1)}, bf16[4,32,1664]{2,1,0:T(8,128)(2,1)}, bf16[4,40,1664]{2,1,0:T(8,128)(2,1)}, bf16[4,32,1664]{2,1,0:T(8,1...) custom-call(bf16[4,2,64,512]{3,2,1,0:T(8,128)(2,1)} %bitcast.164, ...), custom_call_target="tpu_custom_call" | custom-call | tf_op jit(solution)/shard_map/split_second/pallas_call | solution.py:204
  186.6 2.3 maximum_select_fusion
  189.9 6.0 %add_many.4 = (bf16[4,40,1664]{2,1,0:T(8,128)(2,1)}, bf16[4,32,1664]{2,1,0:T(8,128)(2,1)}, bf16[4,40,1664]{2,1,0:T(8,128)(2,1)}, bf16[4,32,1664]{2,1,0:T(8,128)(...) custom-call(bf16[4,40,1664]{2,1,0:T(8,128)(2,1)} %get-tuple-element., ...), custom_call_target="tpu_custom_call" | custom-call | tf_op jit(solution)/shard_map/add_many/pallas_call | solution.py:312
  198.1 12.7 %attend_back.4 = (bf16[512,512]{1,0:T(8,128)(2,1)}, bf16[2048,512]{1,0:T(8,128)(2,1)}, bf16[2048,512]{1,0:T(8,128)(2,1)}) custom-call(bf16[512,512]{1,0:T(8,128)(2,1)} %fusion.3.q, bf16[2048,512]{1,0:T(8,128)(2,1)} %convolution_convert_fusion.2.k, bf16[2048,512]{1,0:T(8,128)(2,1)} %add_convert_fusion.v, bf16[8,2048,512]{2,1,0:T(8,128)(2,1)} %get-tuple-element.264.weights, ...), custom_call_target="tpu_custom_call" | custom-call | flops 8589934592 | bytes 8388608 | tf_op jit(solution)/shard_map/attend_back/pallas_call | solution.py:95
  211.7 2.5 add_many.5
  218.3 12.5 %attend_back.5 = (bf16[512,512]{1,0:T(8,128)(2,1)}, bf16[2048,512]{1,0:T(8,128)(2,1)}, bf16[2048,512]{1,0:T(8,128)(2,1)}) custom-call(bf16[512,512]{1,0:T(8,128)(2,1)} %fusion.3.q, bf16[2048,512]{1,0:T(8,128)(2,1)} %convolution_convert_fusion.2.k, bf16[2048,512]{1,0:T(8,128)(2,1)} %add_convert_fusion.v, ...), custom_call_target="tpu_custom_call", output_to_operand_aliasing={{0}: (7, {}), {1}: (8, {}), {2}: (9, {})} | custom-call | flops 8589934592 | bytes 8388608 | tf_op jit(solution)/shard_map/attend_back/pallas_call | solution.py:95
  230.8 7.8 %row_grads.1 = (f32[512,512]{1,0:T(8,128)}, f32[128,512]{1,0:T(8,128)}, bf16[320,512]{1,0:T(8,128)(2,1)}, bf16[320,512]{1,0:T(8,128)(2,1)}, bf16[320,512]{1,0:T(...) custom-call(bf16[2048,512]{1,0:T(8,128)(2,1)} %get-tuple-element.342.dk, ...), custom_call_target="tpu_custom_call" | custom-call | tf_op jit(solution)/shard_map/row_grads/pallas_call | solution.py:593
  241.7 3.7 %convolution_convert_fusion.4 = bf16[512,512]{1,0:T(8,128)(2,1)} fusion(bf16[2048,512]{1,0:T(8,128)(2,1)S(1)} %copy-done.2, bf16[2048,512]{1,0:T(8,128)(2,1)} %get-tuple-element.342.dk), kind=kOutput, calls=%fused_computation.25 | convolution fusion | flops 1074003968 | bytes 4718592 | tf_op jit(solution)/shard_map/dot_general | solution.py:20
  263.4 3.1 split_first.1
  266.6 3.6 %collective-permute-done.53 = bf16[320,512]{1,0:T(8,128)(2,1)} collective-permute-done((bf16[320,512]{1,0:T(8,128)(2,1)}, bf16[320,512]{1,0:T(8,128)(2,1)}, u32[]{:S(2)}, u32[]{:S(2)}) %collective-permute-start.53) | collective-permute-done | bytes 327712 | tf_op jit(solution)/shard_map/ppermute | solution.py:235
  277.7 3.3 %collective-permute-start.67 = (bf16[72,1664]{1,0:T(8,128)(2,1)}, bf16[72,1664]{1,0:T(8,128)(2,1)S(1)}, u32[]{:S(2)}, u32[]{:S(2)}) collective-permute-start(bf16[72,1664]{1,0:T(8,128)(2,1)} %get-tuple-element.416), channel_id=1, source_target_pairs={{0,24},{8,0},{16,8},{24,16},{1,25},{9,1},{17,9},{25,17},{2,26},{10... | collective-permute-start | bytes 718856 | tf_op jit(solution)/shard_map/ppermute | solution.py:240
  280.9 2.6 add_many.7
  287.0 2.5 fusion.11
  292.0 4.7 %collective-permute-done.63 = bf16[4,72,384]{2,1,0:T(8,128)(2,1)S(1)} collective-permute-done((bf16[4,72,384]{2,1,0:T(8,128)(2,1)}, bf16[4,72,384]{2,1,0:T(8,128)(2,1)S(1)}, u32[]{:S(2)}, u32[]{:S(2)}) %collective-permute-start.63) | collective-permute-done | bytes 221216 | tf_op jit(solution)/shard_map/ppermute | solution.py:260
  (438 shorter events, 140.1 us)
Async XLA Ops:
  2.9 18.8 %collective-permute-start.1 = (bf16[320,512]{1,0:T(8,128)(2,1)}, bf16[320,512]{1,0:T(8,128)(2,1)S(1)}, u32[]{:S(2)}, u32[]{:S(2)}) collective-permute-start(bf16[320,512]{1,0:T(8,128)(2,1)} %get-tuple-element.210.refs_0_), channel_id=1, source_target_pairs={{0,2},{1,3},{2,0},{3,1},{4,6},{5,7},{6,4},{7,5},{8,10},{9,11},{10,... | collective-permute-start | bytes 983048 | tf_op jit(solution)/shard_map/ppermute | solution.py:235
  5.8 20.7 %collective-permute-start.3 = (bf16[320,512]{1,0:T(8,128)(2,1)}, bf16[320,512]{1,0:T(8,128)(2,1)S(1)}, u32[]{:S(2)}, u32[]{:S(2)}) collective-permute-start(bf16[320,512]{1,0:T(8,128)(2,1)} %get-tuple-element.210.refs_0_), channel_id=1, source_target_pairs={{0,4},{4,0},{1,5},{5,1},{2,6},{6,2},{3,7},{7,3},{8,12},{12,8},{9,1... | collective-permute-start | bytes 983048 | tf_op jit(solution)/shard_map/ppermute | solution.py:240
  21.6 16.9 %collective-permute-start.11 = (bf16[64,1664]{1,0:T(8,128)(2,1)}, bf16[64,1664]{1,0:T(8,128)(2,1)S(1)}, u32[]{:S(2)}, u32[]{:S(2)}) collective-permute-start(bf16[64,1664]{1,0:T(8,128)(2,1)} %get-tuple-element.219.refs_0_), channel_id=1, source_target_pairs={{0,16},{8,24},{16,0},{24,8},{1,17},{9,25},{17,1},{25,9},{2,18},{10... | collective-permute-start | bytes 638984 | tf_op jit(solution)/shard_map/ppermute | solution.py:240
  28.4 12.3 %collective-permute-start.17 = (bf16[4,64,384]{2,1,0:T(8,128)(2,1)}, bf16[4,64,384]{2,1,0:T(8,128)(2,1)}, u32[]{:S(2)}, u32[]{:S(2)}) collective-permute-start(bf16[4,64,384]{2,1,0:T(8,128)(2,1)} %stack_first.1.refs_0_), channel_id=1, source_target_pairs={{0,2},{1,3},{2,0},{3,1},{4,6},{5,7},{6,4},{7,5},{8,10},{9,11},{10,... | collective-permute-start | bytes 589832 | tf_op jit(solution)/shard_map/ppermute | solution.py:260
  29.0 12.2 %collective-permute-start.18 = (bf16[4,64,384]{2,1,0:T(8,128)(2,1)}, bf16[4,64,384]{2,1,0:T(8,128)(2,1)}, u32[]{:S(2)}, u32[]{:S(2)}) collective-permute-start(bf16[4,64,384]{2,1,0:T(8,128)(2,1)} %stack_first.1.refs_0_), channel_id=1, source_target_pairs={{0,4},{1,5},{2,6},{3,7},{4,0},{5,1},{6,2},{7,3},{8,12},{9,13},{10,... | collective-permute-start | bytes 589832 | tf_op jit(solution)/shard_map/ppermute | solution.py:260
  31.9 14.1 %collective-permute-start.8 = (bf16[320,512]{1,0:T(8,128)(2,1)S(1)}, bf16[320,512]{1,0:T(8,128)(2,1)S(1)}, u32[]{:S(2)}, u32[]{:S(2)}) collective-permute-start(bf16[320,512]{1,0:T(8,128)(2,1)S(1)} %collective-permute-done.1.refs_2_), channel_id=1, source_target_pairs={{0,4},{4,0},{1,5},{5,1},{2,6},{6,2},{3,7},{7,3},{8,12},{12,8},{9,1... | collective-permute-start | bytes 983048 | tf_op jit(solution)/shard_map/ppermute | solution.py:240
  41.2 14.9 %collective-permute-start.20 = (bf16[4,64,384]{2,1,0:T(8,128)(2,1)}, bf16[4,64,384]{2,1,0:T(8,128)(2,1)S(1)}, u32[]{:S(2)}, u32[]{:S(2)}) collective-permute-start(bf16[4,64,384]{2,1,0:T(8,128)(2,1)} %stack_first.1.refs_0_), channel_id=1, source_target_pairs={{0,1},{1,0},{2,3},{3,2},{4,5},{5,4},{6,7},{7,6},{8,9},{9,8},{10,11... | collective-permute-start | bytes 589832 | tf_op jit(solution)/shard_map/ppermute | solution.py:230
  41.2 16.4 %collective-permute-start.21 = (bf16[4,64,384]{2,1,0:T(8,128)(2,1)}, bf16[4,64,384]{2,1,0:T(8,128)(2,1)S(1)}, u32[]{:S(2)}, u32[]{:S(2)}) collective-permute-start(bf16[4,64,384]{2,1,0:T(8,128)(2,1)} %collective-permute-done.17.refs_1_), channel_id=1, source_target_pairs={{0,1},{1,0},{2,3},{3,2},{4,5},{5,4},{6,7},{7,6},{8,9},{9,8},{10,11... | collective-permute-start | bytes 589832 | tf_op jit(solution)/shard_map/ppermute | solution.py:230
  46.0 13.1 %collective-permute-start.22 = (bf16[4,64,384]{2,1,0:T(8,128)(2,1)}, bf16[4,64,384]{2,1,0:T(8,128)(2,1)S(1)}, u32[]{:S(2)}, u32[]{:S(2)}) collective-permute-start(bf16[4,64,384]{2,1,0:T(8,128)(2,1)} %collective-permute-done.18.refs_2_), channel_id=1, source_target_pairs={{0,1},{1,0},{2,3},{3,2},{4,5},{5,4},{6,7},{7,6},{8,9},{9,8},{10,11... | collective-permute-start | bytes 589832 | tf_op jit(solution)/shard_map/ppermute | solution.py:230
  47.6 12.1 %collective-permute-start.23 = (bf16[4,64,384]{2,1,0:T(8,128)(2,1)}, bf16[4,64,384]{2,1,0:T(8,128)(2,1)S(1)}, u32[]{:S(2)}, u32[]{:S(2)}) collective-permute-start(bf16[4,64,384]{2,1,0:T(8,128)(2,1)} %collective-permute-done.19.refs_3_), channel_id=1, source_target_pairs={{0,1},{1,0},{2,3},{3,2},{4,5},{5,4},{6,7},{7,6},{8,9},{9,8},{10,11... | collective-permute-start | bytes 589832 | tf_op jit(solution)/shard_map/ppermute | solution.py:230
  55.5 28.6 %collective-permute-start.13 = (bf16[4,32,1664]{2,1,0:T(8,128)(2,1)}, bf16[4,32,1664]{2,1,0:T(8,128)(2,1)}, u32[]{:S(2)}, u32[]{:S(2)}) collective-permute-start(bf16[4,32,1664]{2,1,0:T(8,128)(2,1)} %get-tuple-element.243.refs_0_), channel_id=1, source_target_pairs={{0,2},{1,3},{2,0},{3,1},{4,6},{5,7},{6,4},{7,5},{8,10},{9,11},{10,... | collective-permute-start | bytes 1277960 | tf_op jit(solution)/shard_map/ppermute | solution.py:235
  56.1 28.1 %collective-permute-start.15 = (bf16[4,32,1664]{2,1,0:T(8,128)(2,1)}, bf16[4,32,1664]{2,1,0:T(8,128)(2,1)S(1)}, u32[]{:S(2)}, u32[]{:S(2)}) collective-permute-start(bf16[4,32,1664]{2,1,0:T(8,128)(2,1)} %get-tuple-element.243.refs_0_), channel_id=1, source_target_pairs={{0,4},{4,0},{1,5},{5,1},{2,6},{6,2},{3,7},{7,3},{8,12},{12,8},{9,1... | collective-permute-start | bytes 1277960 | tf_op jit(solution)/shard_map/ppermute | solution.py:240
  57.6 26.5 %collective-permute-start.14 = (bf16[4,32,1664]{2,1,0:T(8,128)(2,1)}, bf16[4,32,1664]{2,1,0:T(8,128)(2,1)S(1)}, u32[]{:S(2)}, u32[]{:S(2)}) collective-permute-start(bf16[4,32,1664]{2,1,0:T(8,128)(2,1)} %get-tuple-element.244.refs_1_), channel_id=1, source_target_pairs={{0,2},{1,3},{2,0},{3,1},{4,6},{5,7},{6,4},{7,5},{8,10},{9,11},{10,... | collective-permute-start | bytes 1277960 | tf_op jit(solution)/shard_map/ppermute | solution.py:235
  59.1 25.1 %collective-permute-start.16 = (bf16[4,32,1664]{2,1,0:T(8,128)(2,1)}, bf16[4,32,1664]{2,1,0:T(8,128)(2,1)S(1)}, u32[]{:S(2)}, u32[]{:S(2)}) collective-permute-start(bf16[4,32,1664]{2,1,0:T(8,128)(2,1)} %get-tuple-element.244.refs_1_), channel_id=1, source_target_pairs={{0,4},{4,0},{1,5},{5,1},{2,6},{6,2},{3,7},{7,3},{8,12},{12,8},{9,1... | collective-permute-start | bytes 1277960 | tf_op jit(solution)/shard_map/ppermute | solution.py:240
  84.2 15.0 %collective-permute-start.24 = (bf16[4,32,1664]{2,1,0:T(8,128)(2,1)}, bf16[4,32,1664]{2,1,0:T(8,128)(2,1)S(1)}, u32[]{:S(2)}, u32[]{:S(2)}) collective-permute-start(bf16[4,32,1664]{2,1,0:T(8,128)(2,1)} %collective-permute-done.13.refs_2_), channel_id=1, source_target_pairs={{0,4},{4,0},{1,5},{5,1},{2,6},{6,2},{3,7},{7,3},{8,12},{12,8},{9,1... | collective-permute-start | bytes 1277960 | tf_op jit(solution)/shard_map/ppermute | solution.py:240
  85.7 13.5 %collective-permute-start.25 = (bf16[4,32,1664]{2,1,0:T(8,128)(2,1)S(1)}, bf16[4,32,1664]{2,1,0:T(8,128)(2,1)S(1)}, u32[]{:S(2)}, u32[]{:S(2)}) collective-permute-start(bf16[4,32,1664]{2,1,0:T(8,128)(2,1)S(1)} %collective-permute-done.16.refs_5_), channel_id=1, source_target_pairs={{0,2},{1,3},{2,0},{3,1},{4,6},{5,7},{6,4},{7,5},{8,10},{9,11},{10,... | collective-permute-start | bytes 1277960 | tf_op jit(solution)/shard_map/ppermute | solution.py:235
  105.6 29.2 %collective-permute-start.35 = (bf16[256,512]{1,0:T(8,128)(2,1)}, bf16[256,512]{1,0:T(8,128)(2,1)S(1)}, u32[]{:S(2)}, u32[]{:S(2)}) collective-permute-start(bf16[256,512]{1,0:T(8,128)(2,1)} %get-tuple-element.420), channel_id=1, source_target_pairs={{0,1},{1,0},{2,3},{3,2},{4,5},{5,4},{6,7},{7,6},{8,9},{9,8},{10,11... | collective-permute-start | bytes 786440 | tf_op jit(solution)/shard_map/ppermute | solution.py:230
  164.6 19.2 %collective-permute-start.34 = (f32[256,512]{1,0:T(8,128)}, f32[256,512]{1,0:T(8,128)}, u32[]{:S(2)}, u32[]{:S(2)}) collective-permute-start(f32[256,512]{1,0:T(8,128)} %get-tuple-element.415), channel_id=1, source_target_pairs={{0,1},{1,0},{2,3},{3,2},{4,5},{5,4},{6,7},{7,6},{8,9},{9,8},{10,11... | collective-permute-start | bytes 1572872 | tf_op jit(solution)/shard_map/ppermute | solution.py:230
  195.9 14.9 %collective-permute-start.44 = (bf16[4,40,1664]{2,1,0:T(8,128)(2,1)}, bf16[4,40,1664]{2,1,0:T(8,128)(2,1)S(1)}, u32[]{:S(2)}, u32[]{:S(2)}) collective-permute-start(bf16[4,40,1664]{2,1,0:T(8,128)(2,1)} %get-tuple-element.299), channel_id=1, source_target_pairs={{0,4},{4,0},{1,5},{5,1},{2,6},{6,2},{3,7},{7,3},{8,12},{12,8},{9,1... | collective-permute-start | bytes 1597448 | tf_op jit(solution)/shard_map/ppermute | solution.py:240
  196.6 14.2 %collective-permute-start.45 = (bf16[4,32,1664]{2,1,0:T(8,128)(2,1)}, bf16[4,32,1664]{2,1,0:T(8,128)(2,1)S(1)}, u32[]{:S(2)}, u32[]{:S(2)}) collective-permute-start(bf16[4,32,1664]{2,1,0:T(8,128)(2,1)} %get-tuple-element.300), channel_id=1, source_target_pairs={{0,2},{1,3},{2,0},{3,1},{4,6},{5,7},{6,4},{7,5},{8,10},{9,11},{10,... | collective-permute-start | bytes 1277960 | tf_op jit(solution)/shard_map/ppermute | solution.py:235
  214.3 24.4 %collective-permute-start.46 = (bf16[4,40,1664]{2,1,0:T(8,128)(2,1)}, bf16[4,40,1664]{2,1,0:T(8,128)(2,1)S(1)}, u32[]{:S(2)}, u32[]{:S(2)}) collective-permute-start(bf16[4,40,1664]{2,1,0:T(8,128)(2,1)} %get-tuple-element.327), channel_id=1, source_target_pairs={{0,2},{1,3},{2,0},{3,1},{4,6},{5,7},{6,4},{7,5},{8,10},{9,11},{10,... | collective-permute-start | bytes 1597448 | tf_op jit(solution)/shard_map/ppermute | solution.py:235
  215.4 23.3 %collective-permute-start.47 = (bf16[4,32,1664]{2,1,0:T(8,128)(2,1)S(1)}, bf16[4,32,1664]{2,1,0:T(8,128)(2,1)S(1)}, u32[]{:S(2)}, u32[]{:S(2)}) collective-permute-start(bf16[4,32,1664]{2,1,0:T(8,128)(2,1)S(1)} %copy-done.87), channel_id=1, source_target_pairs={{0,2},{1,3},{2,0},{3,1},{4,6},{5,7},{6,4},{7,5},{8,10},{9,11},{10,... | collective-permute-start | bytes 1277960 | tf_op jit(solution)/shard_map/ppermute | solution.py:235
  216.3 22.4 %collective-permute-start.48 = (bf16[4,40,1664]{2,1,0:T(8,128)(2,1)S(1)}, bf16[4,40,1664]{2,1,0:T(8,128)(2,1)S(1)}, u32[]{:S(2)}, u32[]{:S(2)}) collective-permute-start(bf16[4,40,1664]{2,1,0:T(8,128)(2,1)S(1)} %copy-done.85), channel_id=1, source_target_pairs={{0,4},{4,0},{1,5},{5,1},{2,6},{6,2},{3,7},{7,3},{8,12},{12,8},{9,1... | collective-permute-start | bytes 1597448 | tf_op jit(solution)/shard_map/ppermute | solution.py:240
  217.7 21.0 %collective-permute-start.49 = (bf16[4,32,1664]{2,1,0:T(8,128)(2,1)}, bf16[4,32,1664]{2,1,0:T(8,128)(2,1)S(1)}, u32[]{:S(2)}, u32[]{:S(2)}) collective-permute-start(bf16[4,32,1664]{2,1,0:T(8,128)(2,1)} %get-tuple-element.330), channel_id=1, source_target_pairs={{0,4},{4,0},{1,5},{5,1},{2,6},{6,2},{3,7},{7,3},{8,12},{12,8},{9,1... | collective-permute-start | bytes 1277960 | tf_op jit(solution)/shard_map/ppermute | solution.py:240
  239.8 12.7 %collective-permute-start.50 = (bf16[320,512]{1,0:T(8,128)(2,1)}, bf16[320,512]{1,0:T(8,128)(2,1)S(1)}, u32[]{:S(2)}, u32[]{:S(2)}) collective-permute-start(bf16[320,512]{1,0:T(8,128)(2,1)} %get-tuple-element.336), channel_id=1, source_target_pairs={{0,4},{4,0},{1,5},{5,1},{2,6},{6,2},{3,7},{7,3},{8,12},{12,8},{9,1... | collective-permute-start | bytes 983048 | tf_op jit(solution)/shard_map/ppermute | solution.py:240
  250.6 34.4 %collective-permute-start.65 = (bf16[72,1664]{1,0:T(8,128)(2,1)}, bf16[72,1664]{1,0:T(8,128)(2,1)}, u32[]{:S(2)}, u32[]{:S(2)}) collective-permute-start(bf16[72,1664]{1,0:T(8,128)(2,1)} %get-tuple-element.418), channel_id=1, source_target_pairs={{0,8},{8,16},{16,24},{24,0},{1,9},{9,17},{17,25},{25,1},{2,10},{10... | collective-permute-start | bytes 718856 | tf_op jit(solution)/shard_map/ppermute | solution.py:240
  256.3 13.9 %collective-permute-start.53 = (bf16[320,512]{1,0:T(8,128)(2,1)}, bf16[320,512]{1,0:T(8,128)(2,1)}, u32[]{:S(2)}, u32[]{:S(2)}) collective-permute-start(bf16[320,512]{1,0:T(8,128)(2,1)} %get-tuple-element.345), channel_id=1, source_target_pairs={{0,2},{1,3},{2,0},{3,1},{4,6},{5,7},{6,4},{7,5},{8,10},{9,11},{10,... | collective-permute-start | bytes 983048 | tf_op jit(solution)/shard_map/ppermute | solution.py:235
  257.4 12.8 %collective-permute-start.54 = (bf16[320,512]{1,0:T(8,128)(2,1)}, bf16[320,512]{1,0:T(8,128)(2,1)}, u32[]{:S(2)}, u32[]{:S(2)}) collective-permute-start(bf16[320,512]{1,0:T(8,128)(2,1)} %get-tuple-element.346), channel_id=1, source_target_pairs={{0,4},{4,0},{1,5},{5,1},{2,6},{6,2},{3,7},{7,3},{8,12},{12,8},{9,1... | collective-permute-start | bytes 983048 | tf_op jit(solution)/shard_map/ppermute | solution.py:240
  258.1 13.6 %collective-permute-start.55 = (bf16[320,512]{1,0:T(8,128)(2,1)}, bf16[320,512]{1,0:T(8,128)(2,1)}, u32[]{:S(2)}, u32[]{:S(2)}) collective-permute-start(bf16[320,512]{1,0:T(8,128)(2,1)} %get-tuple-element.347), channel_id=1, source_target_pairs={{0,4},{4,0},{1,5},{5,1},{2,6},{6,2},{3,7},{7,3},{8,12},{12,8},{9,1... | collective-permute-start | bytes 983048 | tf_op jit(solution)/shard_map/ppermute | solution.py:240
  276.3 14.9 %collective-permute-start.66 = (bf16[72,1664]{1,0:T(8,128)(2,1)}, bf16[72,1664]{1,0:T(8,128)(2,1)S(1)}, u32[]{:S(2)}, u32[]{:S(2)}) collective-permute-start(bf16[72,1664]{1,0:T(8,128)(2,1)} %get-tuple-element.417), channel_id=1, source_target_pairs={{0,16},{8,24},{16,0},{24,8},{1,17},{9,25},{17,1},{25,9},{2,18},{10... | collective-permute-start | bytes 718856 | tf_op jit(solution)/shard_map/ppermute | solution.py:240
  277.7 13.6 %collective-permute-start.67 = (bf16[72,1664]{1,0:T(8,128)(2,1)}, bf16[72,1664]{1,0:T(8,128)(2,1)S(1)}, u32[]{:S(2)}, u32[]{:S(2)}) collective-permute-start(bf16[72,1664]{1,0:T(8,128)(2,1)} %get-tuple-element.416), channel_id=1, source_target_pairs={{0,24},{8,0},{16,8},{24,16},{1,25},{9,1},{17,9},{25,17},{2,26},{10... | collective-permute-start | bytes 718856 | tf_op jit(solution)/shard_map/ppermute | solution.py:240
  291.2 15.5 %collective-permute-start.56 = (f32[256,512]{1,0:T(8,128)}, f32[256,512]{1,0:T(8,128)S(1)}, u32[]{:S(2)}, u32[]{:S(2)}) collective-permute-start(f32[256,512]{1,0:T(8,128)} %get-tuple-element.412), channel_id=1, source_target_pairs={{0,1},{1,0},{2,3},{3,2},{4,5},{5,4},{6,7},{7,6},{8,9},{9,8},{10,11... | collective-permute-start | bytes 1572872 | tf_op jit(solution)/shard_map/ppermute | solution.py:230
  (141 other events, 837.8 us)

commit v4 on v3

--- a/solution.py
+++ b/solution.py
@@ -73,7 +73,7 @@
 
 
 def attend_back_kernel(heads, q, k, v, weights, inverse, exact, grad, *refs):
-    dq, dk, dv = refs[-3:]
+    dq, dk, dv, dq_sum, dv_sum = refs[-5:]
     for head in range(heads):
         cols = slice(head * HEAD_DIM, (head + 1) * HEAD_DIM)
         grads = grad[:, cols].astype(F32).T
@@ -82,18 +82,22 @@
         weight = weights[head]
         grad_weight = contract(v[:, cols], scaled, 1, 0)
         grad_scores = (weight.astype(F32) * (grad_weight - inner)).astype(BF16)
-        dq[:, cols] = (contract(k[:, cols], grad_scores, 0, 0) * SCALE).T.astype(BF16)
-        dv[:, cols] = contract(weight, scaled, 1, 1).astype(BF16)
+        low = (contract(k[:, cols], grad_scores, 0, 0) * SCALE).T.astype(BF16)
+        dq[:, cols] = low
+        dq_sum[:, cols] = jnp.sum(low.astype(F32), axis=0, keepdims=True)
+        low = contract(weight, scaled, 1, 1).astype(BF16)
+        dv[:, cols] = low
+        dv_sum[:, cols] = jnp.sum(low.astype(F32), axis=0, keepdims=True)
         dk[:, cols] = (contract(grad_scores, q[:, cols], 1, 0) * SCALE).astype(BF16)
 
 
 HEADS_PER_STEP = 2
 
 
-def attend_call(body, arrays, specs, shapes, out_specs, earlier, steps, cost, name):
+def attend_call(body, arrays, specs, shapes, out_specs, earlier, each, steps, cost, name):
     given = [] if earlier is None else list(earlier)
     return pl.pallas_call(
-        functools.partial(body, HEADS_PER_STEP),
+        functools.partial(body, each),
         grid=(steps,),
         in_specs=specs + [pl.BlockSpec(memory_space=pl.ANY)] * len(given),
         out_specs=out_specs,
@@ -105,15 +109,15 @@
     )(*arrays, *given)
 
 
-def head_specs(first):
+def head_specs(first, each):
     def columns(rows):
-        return pl.BlockSpec((rows, HEADS_PER_STEP * HEAD_DIM), lambda i: (0, i + first))
+        return pl.BlockSpec((rows, each * HEAD_DIM), lambda i: (0, i + first))
 
     def lines(rows):
-        return pl.BlockSpec((HEADS_PER_STEP * HEAD_DIM, rows), lambda i: (i + first, 0))
+        return pl.BlockSpec((each * HEAD_DIM, rows), lambda i: (i + first, 0))
 
     def heads(*dims):
-        return pl.BlockSpec((HEADS_PER_STEP,) + dims, lambda i: (i + first, 0, 0))
+        return pl.BlockSpec((each,) + dims, lambda i: (i + first, 0, 0))
 
     return columns, lines, heads
 
@@ -122,8 +126,9 @@
     rows, width = q.shape
     keys = k.shape[0]
     heads = width // HEAD_DIM
-    steps = heads // HEADS_PER_STEP // parts
-    columns, lines, by_head = head_specs(part * steps)
+    each = HEADS_PER_STEP
+    steps = heads // each // parts
+    columns, lines, by_head = head_specs(part * steps, each)
     return attend_call(
         attend_kernel,
         (q, k, v, qp, kp),
@@ -142,6 +147,7 @@
         ],
         [columns(rows), lines(rows), by_head(keys, rows), by_head(1, rows)],
         earlier,
+        each,
         steps,
         pl.CostEstimate(
             flops=16 * rows * keys * width // parts,
@@ -156,8 +162,9 @@
     rows, width = q.shape
     keys = k.shape[0]
     heads = width // HEAD_DIM
-    steps = heads // HEADS_PER_STEP // parts
-    columns, lines, by_head = head_specs(part * steps)
+    each = HEADS_PER_STEP
+    steps = heads // each // parts
+    columns, lines, by_head = head_specs(part * steps, each)
     return attend_call(
         attend_back_kernel,
         (q, k, v, weights, inverse, exact, grad),
@@ -174,9 +181,12 @@
             jax.ShapeDtypeStruct((rows, width), BF16),
             jax.ShapeDtypeStruct((keys, width), BF16),
             jax.ShapeDtypeStruct((keys, width), BF16),
+            jax.ShapeDtypeStruct((1, width), F32),
+            jax.ShapeDtypeStruct((1, width), F32),
         ],
-        [columns(rows), columns(keys), columns(keys)],
+        [columns(rows), columns(keys), columns(keys), columns(1), columns(1)],
         earlier,
+        each,
         steps,
         pl.CostEstimate(
             flops=32 * rows * keys * width // parts,
@@ -793,8 +803,8 @@
         "rows_together",
     )
     rows_in = wide_rows[:rows]
-    second_half = plane_one(
-        *depth_blocks([after(p, wide_rows) for p in second_pieces], 2, "stack_second")
+    second_blocks = plane_direct(
+        depth_blocks([after(p, wide_rows) for p in second_pieces], 1, "stack_second")[0]
     )
 
     slots = lax.dynamic_index_in_dim(positions, core, 0, keepdims=False)
@@ -820,12 +830,8 @@
     query_low = (product(rows_in, full_query) + query_bias).astype(BF16)
     keys = product(wide_rows, full_key).astype(BF16)
     values = (product(wide_rows, full_value) + value_bias).astype(BF16)
-    early = list(attend(query_low, keys, values, query_positions, key_positions, 0, 2))
-    second_half, late_query, ready = gated(second_half, query_low, early[1])
-    early[1] = ready
-    second_blocks = plane_two(second_half)
     attended, attended_exact, weights, inverse = attend(
-        late_query, keys, values, query_positions, key_positions, 1, 2, early
+        query_low, keys, values, query_positions, key_positions
     )
     second_blocks, attended = gated(second_blocks, attended)
     (
@@ -872,7 +878,7 @@
     )
     second_grad_low = second_in_grad.astype(BF16)
     cross_attended_grad = product(second_grad_low, full_cross_output).astype(BF16)
-    cross_query_grad, memory_key_grad, memory_value_grad = attend_back(
+    cross_query_grad, memory_key_grad, memory_value_grad, *cross_sums = attend_back(
         cross_query,
         memory_key,
         memory_value,
@@ -896,8 +902,8 @@
         jnp.sum(first_in_grad, axis=0),
         first_gain_part,
         first_shift_part,
-        jnp.sum(cross_query_grad.astype(F32), axis=0),
-        jnp.sum(memory_value_grad.astype(F32), axis=0),
+        cross_sums[0].reshape(-1),
+        cross_sums[1].reshape(-1),
         jnp.sum(second_in_grad, axis=0),
         second_gain_part,
         second_shift_part,
@@ -928,7 +934,7 @@
     second_blocks = sum_adds(second_blocks)
     second_blocks, late_grad = gated(second_blocks, attended_grad)
     second_left = sum_two(second_blocks)
-    query_grad, key_grad, value_grad = attend_back(
+    query_grad, key_grad, value_grad, *self_sums = attend_back(
         query_low, keys, values, weights, inverse, attended_exact, late_grad, 1, 2, early
     )
     input_part, memory_own, low_blocks = row_grads(
@@ -945,10 +951,7 @@
         product_left(wide_rows, key_late).astype(BF16),
         product_left(wide_rows, value_late).astype(BF16),
     ]
-    late_vectors = [
-        jnp.sum(query_late.astype(F32), axis=0),
-        jnp.sum(value_late.astype(F32), axis=0),
-    ]
+    late_vectors = [self_sums[0].reshape(-1), self_sums[1].reshape(-1)]
     low_blocks = sum_adds(low_blocks)
     low_blocks, unused, first_part = regroup(low_blocks, [], [tuple(first_part)])
     left = sum_two(low_blocks)[1:]

time: 314 us -> 303 us (0.965)
  starting transfers between devices: 54 us -> 47.9 us
  waiting for transfers between devices: 28.4 us -> 33.7 us
  Pallas kernels: 122 us -> 117 us
  local copies, waits for them, and re-layouts: 26.3 us -> 22.1 us
    ppermute x24 -> x21, starting transfers between devices: 27.9 us -> 21.5 us  [shift(): lax.ppermute(value, axis, [(i, (i + step) % total) for i in range(total)])]
    unnamed x211 -> x163, local copies, waits for them, and re-layouts: 15.7 us -> 10.3 us
    reduce_sum x4 -> x0, other arithmetic: 4.03 us -> none  [the longest x1 1.73 us: per_device(): jnp.sum(query_late.astype(F32), axis=0)]
    pallas_call x6 -> x5, Pallas kernels: 67.8 us -> 64.2 us  [attend_call(): pl.pallas_call(functools.partial(body, each), grid=(steps,), in_specs=spe...]
    ppermute x6 -> x9, starting transfers between devices: 6.98 us -> 10.5 us  [shift_plane(): return lax.ppermute(value, ('ctx', 'tp'), pairs)]
    ppermute x24 -> x21, waiting for transfers between devices: 15.8 us -> 18.7 us  [shift(): lax.ppermute(value, axis, [(i, (i + step) % total) for i in range(total)])]
    ppermute x6 -> x9, waiting for transfers between devices: 5.88 us -> 7.84 us  [shift_plane(): return lax.ppermute(value, ('ctx', 'tp'), pairs)]
    ppermute x12 -> x9, starting transfers between devices: 12.8 us -> 10.8 us  [shift_x(): lax.ppermute(value, 'tp', [(i, (i + 2 * step) % total) for i in range(tot...]
  transfers between devices with their start and end apart: 71 -> 64, of which waited for: 16 -> 18; matrix products, arithmetic and copies ran while one was open for 22% -> 23% of each run, Pallas kernels for 33% -> 32%
where the time goes in v4:
time: 303 us; the launch traced here: 299 us
  Pallas kernels  117 us (39%)
  matrix products  49.1 us (16%)
  starting transfers between devices  47.9 us (16%)
  waiting for transfers between devices  33.7 us (11%)
  other arithmetic  26.3 us (9%)
  local copies, waits for them, and re-layouts  22.1 us (7%)
    pallas_call x5, Pallas kernels, attend_call(): pl.pallas_call(functools.partial(body, each), grid=(steps,), in_specs=spe...  64.2 us
    dot_general x28, matrix products, contract(): lax.dot_general(left, right, (((left_dim,), (right_dim,)), ((), ())), pre...  49.1 us
    pallas_call x7, Pallas kernels, move(): pl.pallas_call(body, in_specs=[pl.BlockSpec(memory_space=pl.ANY)] * len(s...  27 us
    ppermute x21, starting transfers between devices, shift(): lax.ppermute(value, axis, [(i, (i + step) % total) for i in range(total)])  21.5 us
    ppermute x21, waiting for transfers between devices, shift(): lax.ppermute(value, axis, [(i, (i + step) % total) for i in range(total)])  18.7 us
    pallas_call x4, Pallas kernels, add_many(): pl.pallas_call(add_kernel, grid=(steps,), in_specs=[spec(part) for part i...  12.9 us
    ppermute x9, starting transfers between devices, shift_x(): lax.ppermute(value, 'tp', [(i, (i + 2 * step) % total) for i in range(tot...  10.8 us
    ppermute x9, starting transfers between devices, shift_plane(): return lax.ppermute(value, ('ctx', 'tp'), pairs)  10.5 us
  transfers between devices with their start and end apart: 64, of which 18 were waited for; matrix products, arithmetic and copies ran while one was open for 23% of the time, Pallas kernels for 32%

profile of v4, /device:TPU:0, one launch (start us, length us, event | category | flops | bytes accessed | tf_op | source)
XLA Modules:
  0.0 298.6 jit_solution(15920517249471270751)
XLA Ops:
  2.9 3.0 collective-permute-start.1
  12.0 2.6 collective-permute-start.6
  29.5 2.4 collective-permute-start.18
  33.1 5.4 %collective-permute-done.11.refs_2_ = bf16[64,1664]{1,0:T(8,128)(2,1)S(1)} collective-permute-done((bf16[64,1664]{1,0:T(8,128)(2,1)}, bf16[64,1664]{1,0:T(8,128)(2,1)S(1)}, u32[]{:S(2)}, u32[]{:S(2)}) %collective-permute-start.11) | collective-permute-done | bytes 213024 | tf_op jit(solution)/shard_map/ppermute | solution.py:250
  41.7 4.3 %collective-permute-done.8.refs_6_ = bf16[320,512]{1,0:T(8,128)(2,1)S(1)} collective-permute-done((bf16[320,512]{1,0:T(8,128)(2,1)S(1)}, bf16[320,512]{1,0:T(8,128)(2,1)S(1)}, u32[]{:S(2)}, u32[]{:S(2)}) %collective-permute-start.8) | collective-permute-done | bytes 327712 | tf_op jit(solution)/shard_map/ppermute | solution.py:250
  49.3 3.3 %rows_together.1 = (bf16[2048,512]{1,0:T(8,128)(2,1)}, bf16[512,512]{1,0:T(8,128)(2,1)}) custom-call(bf16[320,512]{1,0:T(8,128)(2,1)} %get-tuple-element.198.refs_0_, bf16[320,512]{1,0:T(8,128)(2,1)} %copy-done.36, bf16[320,512]{1,0:T(8,128)(2,1)} %copy-done.34, bf16[320,512]{1,0:T(8,128)(2,1)} %copy-done.37, bf16[320,512]{1,0:T(8,128)(2,1)} %copy-done.35, ...), custom_call_target="tpu_custom_call" | custom-call | tf_op jit(solution)/shard_map/rows_together/pallas_call | solution.py:214
  60.4 2.8 place_first.1
  63.2 3.7 %convolution_convert_fusion.2.k = bf16[2048,512]{1,0:T(8,128)(2,1)} fusion(bf16[2048,512]{1,0:T(8,128)(2,1)S(1)} %copy-done, bf16[512,512]{1,0:T(8,128)(2,1)} %bitcast.145), kind=kOutput, calls=%fused_computation.7 | convolution fusion | flops 1074790400 | bytes 4718592 | tf_op jit(solution)/shard_map/dot_general | solution.py:20
  66.9 2.6 add_convert_fusion.v
  70.8 21.7 %attend.2 = (bf16[512,512]{1,0:T(8,128)(2,1)}, f32[512,512]{1,0:T(8,128)}, bf16[8,2048,512]{2,1,0:T(8,128)(2,1)}, f32[8,1,512]{2,1,0:T(1,128)}) custom-call(bf16[512,512]{1,0:T(8,128)(2,1)} %fusion.3.q, bf16[2048,512]{1,0:T(8,128)(2,1)} %convolution_convert_fusion.2.k, bf16[2048,512]{1,0:T(8,128)(2,1)} %add_convert_fusion.v, s32[1,512]{1,0:T(1,128)} %bitcast.179, ...), custom_call_target="tpu_custom_call" | custom-call | flops 8589934592 | bytes 16777216 | tf_op jit(solution)/shard_map/attend/pallas_call | solution.py:99
  102.6 6.4 %place_second.1 = (bf16[4,2,64,512]{3,2,1,0:T(8,128)(2,1)}, bf16[4,2,64,512]{3,2,1,0:T(8,128)(2,1)}, bf16[4,2,64,512]{3,2,1,0:T(8,128)(2,1)}, bf16[4,2,64,512]{3...) custom-call(bf16[4,64,1664]{2,1,0:T(8,128)(2,1)} %stack_second.1.ref, ...), custom_call_target="tpu_custom_call" | custom-call | tf_op jit(solution)/shard_map/place_second/pallas_call | solution.py:214
  115.6 8.6 %attend.3 = (bf16[512,512]{1,0:T(8,128)(2,1)}, f32[512,512]{1,0:T(8,128)}, bf16[8,512,512]{2,1,0:T(8,128)(2,1)}, f32[8,1,512]{2,1,0:T(1,128)}) custom-call(bf16[512,512]{1,0:T(8,128)(2,1)} %fusion.4.q, bf16[512,512]{1,0:T(8,128)(2,1)} %convolution_convert_fusion.13.k, bf16[512,512]{1,0:T(8,128)(2,1)} %fusion.5.v, s32[1,512]{1,0:T(1,128)} %broadcast_in_dim.20.qp, ...), custom_call_target="tpu_custom_call" | custom-call | flops 2147483648 | bytes 4194304 | tf_op jit(solution)/shard_map/attend/pallas_call | solution.py:99
  133.3 2.4 convert_reduce_fusion
  140.1 8.7 %attend_back.3 = (bf16[512,512]{1,0:T(8,128)(2,1)}, bf16[512,512]{1,0:T(8,128)(2,1)}, bf16[512,512]{1,0:T(8,128)(2,1)}, f32[1,512]{1,0:T(1,128)}, f32[1,512]{1,0:T(1,128)}) custom-call(bf16[512,512]{1,0:T(8,128)(2,1)} %fusion.4.q, bf16[512,512]{1,0:T(8,128)(2,1)} %convolution_convert_fusion.13.k, bf16[512,512]{1,0:T(8,128)(2,1)} %fusion.5.v, ...), custom_call_target="tpu_custom_call" | custom-call | flops 4294967296 | bytes 4194304 | tf_op jit(solution)/shard_map/attend_back/pallas_call | solution.py:99
  148.9 2.7 multiply_reduce_fusion.2
  154.3 2.7 convolution_convert_fusion.1
  157.1 2.7 convolution_convert_fusion
  168.2 7.6 %split_second.1 = (bf16[4,40,1664]{2,1,0:T(8,128)(2,1)}, bf16[4,32,1664]{2,1,0:T(8,128)(2,1)}, bf16[4,40,1664]{2,1,0:T(8,128)(2,1)}, bf16[4,32,1664]{2,1,0:T(8,1...) custom-call(bf16[4,2,64,512]{3,2,1,0:T(8,128)(2,1)} %bitcast.160, ...), custom_call_target="tpu_custom_call" | custom-call | tf_op jit(solution)/shard_map/split_second/pallas_call | solution.py:214
  182.7 2.3 maximum_select_fusion
  185.1 5.6 %add_many.4 = (bf16[4,40,1664]{2,1,0:T(8,128)(2,1)}, bf16[4,32,1664]{2,1,0:T(8,128)(2,1)}, bf16[4,40,1664]{2,1,0:T(8,128)(2,1)}, bf16[4,32,1664]{2,1,0:T(8,128)(...) custom-call(bf16[4,40,1664]{2,1,0:T(8,128)(2,1)} %get-tuple-element., ...), custom_call_target="tpu_custom_call" | custom-call | tf_op jit(solution)/shard_map/add_many/pallas_call | solution.py:322
  193.1 12.7 %attend_back.4 = (bf16[512,512]{1,0:T(8,128)(2,1)}, bf16[2048,512]{1,0:T(8,128)(2,1)}, bf16[2048,512]{1,0:T(8,128)(2,1)}, f32[1,512]{1,0:T(1,128)}, f32[1,512]{1,0:T(1,128)}) custom-call(bf16[512,512]{1,0:T(8,128)(2,1)} %fusion.3.q, bf16[2048,512]{1,0:T(8,128)(2,1)} %convolution_convert_fusion.2.k, bf16[2048,512]{1,0:T(8,128)(2,1)} %add_convert_fusion.v, ...), custom_call_target="tpu_custom_call" | custom-call | flops 8589934592 | bytes 8388608 | tf_op jit(solution)/shard_map/attend_back/pallas_call | solution.py:99
  205.8 2.5 add_many.5
  212.4 12.6 %attend_back.5 = (bf16[512,512]{1,0:T(8,128)(2,1)}, bf16[2048,512]{1,0:T(8,128)(2,1)}, bf16[2048,512]{1,0:T(8,128)(2,1)}, f32[1,512]{1,0:T(1,128)}, f32[1,512]{1,0:T(1,128)}) custom-call(bf16[512,512]{1,0:T(8,128)(2,1)} %fusion.3.q, ...), custom_call_target="tpu_custom_call", output_to_operand_aliasing={{0}: (7, {}), {1}: (8, {}), {2}: (9, {}), {3}: (10, {}), {4... | custom-call | flops 8589934592 | bytes 8388608 | tf_op jit(solution)/shard_map/attend_back/pallas_call | solution.py:99
  226.3 7.8 %row_grads.1 = (f32[512,512]{1,0:T(8,128)}, f32[128,512]{1,0:T(8,128)}, bf16[320,512]{1,0:T(8,128)(2,1)}, bf16[320,512]{1,0:T(8,128)(2,1)}, bf16[320,512]{1,0:T(...) custom-call(bf16[2048,512]{1,0:T(8,128)(2,1)} %get-tuple-element.316.dk, ...), custom_call_target="tpu_custom_call" | custom-call | tf_op jit(solution)/shard_map/row_grads/pallas_call | solution.py:603
  238.0 2.3 convert_add_fusion.1
  240.4 2.4 convert_add_fusion
  255.5 3.1 %split_first.1 = (bf16[4,72,384]{2,1,0:T(8,128)(2,1)}, bf16[4,72,384]{2,1,0:T(8,128)(2,1)}, bf16[4,72,384]{2,1,0:T(8,128)(2,1)}, bf16[4,72,384]{2,1,0:T(8,128)(2...) custom-call(bf16[4,2,64,512]{3,2,1,0:T(8,128)(2,1)} %bitcast.152, ...), custom_call_target="tpu_custom_call" | custom-call | tf_op jit(solution)/shard_map/split_first/pallas_call | solution.py:214
  259.8 3.9 %collective-permute-done.46 = bf16[320,512]{1,0:T(8,128)(2,1)S(1)} collective-permute-done((bf16[320,512]{1,0:T(8,128)(2,1)}, bf16[320,512]{1,0:T(8,128)(2,1)S(1)}, u32[]{:S(2)}, u32[]{:S(2)}) %collective-permute-start.46) | collective-permute-done | bytes 327712 | tf_op jit(solution)/shard_map/ppermute | solution.py:245
  270.3 2.5 add_many.7
  276.4 2.5 fusion.11
  281.7 2.3 collective-permute-done.56
  292.7 2.5 collective-permute-done.62
  (371 shorter events, 137.4 us)
Async XLA Ops:
  2.9 18.8 %collective-permute-start.1 = (bf16[320,512]{1,0:T(8,128)(2,1)}, bf16[320,512]{1,0:T(8,128)(2,1)S(1)}, u32[]{:S(2)}, u32[]{:S(2)}) collective-permute-start(bf16[320,512]{1,0:T(8,128)(2,1)} %get-tuple-element.198.refs_0_), channel_id=1, source_target_pairs={{0,2},{1,3},{2,0},{3,1},{4,6},{5,7},{6,4},{7,5},{8,10},{9,11},{10,... | collective-permute-start | bytes 983048 | tf_op jit(solution)/shard_map/ppermute | solution.py:245
  5.8 20.7 %collective-permute-start.3 = (bf16[320,512]{1,0:T(8,128)(2,1)}, bf16[320,512]{1,0:T(8,128)(2,1)S(1)}, u32[]{:S(2)}, u32[]{:S(2)}) collective-permute-start(bf16[320,512]{1,0:T(8,128)(2,1)} %get-tuple-element.198.refs_0_), channel_id=1, source_target_pairs={{0,4},{4,0},{1,5},{5,1},{2,6},{6,2},{3,7},{7,3},{8,12},{12,8},{9,1... | collective-permute-start | bytes 983048 | tf_op jit(solution)/shard_map/ppermute | solution.py:250
  21.6 16.9 %collective-permute-start.11 = (bf16[64,1664]{1,0:T(8,128)(2,1)}, bf16[64,1664]{1,0:T(8,128)(2,1)S(1)}, u32[]{:S(2)}, u32[]{:S(2)}) collective-permute-start(bf16[64,1664]{1,0:T(8,128)(2,1)} %get-tuple-element.207.refs_0_), channel_id=1, source_target_pairs={{0,16},{8,24},{16,0},{24,8},{1,17},{9,25},{17,1},{25,9},{2,18},{10... | collective-permute-start | bytes 638984 | tf_op jit(solution)/shard_map/ppermute | solution.py:250
  28.4 12.3 %collective-permute-start.16 = (bf16[4,64,384]{2,1,0:T(8,128)(2,1)}, bf16[4,64,384]{2,1,0:T(8,128)(2,1)}, u32[]{:S(2)}, u32[]{:S(2)}) collective-permute-start(bf16[4,64,384]{2,1,0:T(8,128)(2,1)} %stack_first.1.refs_0_), channel_id=1, source_target_pairs={{0,2},{1,3},{2,0},{3,1},{4,6},{5,7},{6,4},{7,5},{8,10},{9,11},{10,... | collective-permute-start | bytes 589832 | tf_op jit(solution)/shard_map/ppermute | solution.py:270
  29.0 12.2 %collective-permute-start.17 = (bf16[4,64,384]{2,1,0:T(8,128)(2,1)}, bf16[4,64,384]{2,1,0:T(8,128)(2,1)}, u32[]{:S(2)}, u32[]{:S(2)}) collective-permute-start(bf16[4,64,384]{2,1,0:T(8,128)(2,1)} %stack_first.1.refs_0_), channel_id=1, source_target_pairs={{0,4},{1,5},{2,6},{3,7},{4,0},{5,1},{6,2},{7,3},{8,12},{9,13},{10,... | collective-permute-start | bytes 589832 | tf_op jit(solution)/shard_map/ppermute | solution.py:270
  29.5 11.7 %collective-permute-start.18 = (bf16[4,64,384]{2,1,0:T(8,128)(2,1)}, bf16[4,64,384]{2,1,0:T(8,128)(2,1)}, u32[]{:S(2)}, u32[]{:S(2)}) collective-permute-start(bf16[4,64,384]{2,1,0:T(8,128)(2,1)} %stack_first.1.refs_0_), channel_id=1, source_target_pairs={{0,6},{1,7},{2,4},{3,5},{4,2},{5,3},{6,0},{7,1},{8,14},{9,15},{10,... | collective-permute-start | bytes 589832 | tf_op jit(solution)/shard_map/ppermute | solution.py:270
  31.9 14.1 %collective-permute-start.8 = (bf16[320,512]{1,0:T(8,128)(2,1)S(1)}, bf16[320,512]{1,0:T(8,128)(2,1)S(1)}, u32[]{:S(2)}, u32[]{:S(2)}) collective-permute-start(bf16[320,512]{1,0:T(8,128)(2,1)S(1)} %collective-permute-done.1.refs_2_), channel_id=1, source_target_pairs={{0,4},{4,0},{1,5},{5,1},{2,6},{6,2},{3,7},{7,3},{8,12},{12,8},{9,1... | collective-permute-start | bytes 983048 | tf_op jit(solution)/shard_map/ppermute | solution.py:250
  40.8 11.8 %collective-permute-start.12 = (bf16[64,1664]{1,0:T(8,128)(2,1)}, bf16[64,1664]{1,0:T(8,128)(2,1)S(1)}, u32[]{:S(2)}, u32[]{:S(2)}) collective-permute-start(bf16[64,1664]{1,0:T(8,128)(2,1)} %get-tuple-element.207.refs_0_), channel_id=1, source_target_pairs={{0,24},{8,0},{16,8},{24,16},{1,25},{9,1},{17,9},{25,17},{2,26},{10... | collective-permute-start | bytes 638984 | tf_op jit(solution)/shard_map/ppermute | solution.py:250
  41.2 14.9 %collective-permute-start.19 = (bf16[4,64,384]{2,1,0:T(8,128)(2,1)}, bf16[4,64,384]{2,1,0:T(8,128)(2,1)S(1)}, u32[]{:S(2)}, u32[]{:S(2)}) collective-permute-start(bf16[4,64,384]{2,1,0:T(8,128)(2,1)} %stack_first.1.refs_0_), channel_id=1, source_target_pairs={{0,1},{1,0},{2,3},{3,2},{4,5},{5,4},{6,7},{7,6},{8,9},{9,8},{10,11... | collective-permute-start | bytes 589832 | tf_op jit(solution)/shard_map/ppermute | solution.py:240
  41.2 16.4 %collective-permute-start.20 = (bf16[4,64,384]{2,1,0:T(8,128)(2,1)}, bf16[4,64,384]{2,1,0:T(8,128)(2,1)S(1)}, u32[]{:S(2)}, u32[]{:S(2)}) collective-permute-start(bf16[4,64,384]{2,1,0:T(8,128)(2,1)} %collective-permute-done.16.refs_1_), channel_id=1, source_target_pairs={{0,1},{1,0},{2,3},{3,2},{4,5},{5,4},{6,7},{7,6},{8,9},{9,8},{10,11... | collective-permute-start | bytes 589832 | tf_op jit(solution)/shard_map/ppermute | solution.py:240
  46.0 13.0 %collective-permute-start.21 = (bf16[4,64,384]{2,1,0:T(8,128)(2,1)}, bf16[4,64,384]{2,1,0:T(8,128)(2,1)S(1)}, u32[]{:S(2)}, u32[]{:S(2)}) collective-permute-start(bf16[4,64,384]{2,1,0:T(8,128)(2,1)} %collective-permute-done.17.refs_2_), channel_id=1, source_target_pairs={{0,1},{1,0},{2,3},{3,2},{4,5},{5,4},{6,7},{7,6},{8,9},{9,8},{10,11... | collective-permute-start | bytes 589832 | tf_op jit(solution)/shard_map/ppermute | solution.py:240
  47.6 11.5 %collective-permute-start.22 = (bf16[4,64,384]{2,1,0:T(8,128)(2,1)}, bf16[4,64,384]{2,1,0:T(8,128)(2,1)S(1)}, u32[]{:S(2)}, u32[]{:S(2)}) collective-permute-start(bf16[4,64,384]{2,1,0:T(8,128)(2,1)} %collective-permute-done.18.refs_3_), channel_id=1, source_target_pairs={{0,1},{1,0},{2,3},{3,2},{4,5},{5,4},{6,7},{7,6},{8,9},{9,8},{10,11... | collective-permute-start | bytes 589832 | tf_op jit(solution)/shard_map/ppermute | solution.py:240
  55.5 37.1 %collective-permute-start.13 = (bf16[4,64,1664]{2,1,0:T(8,128)(2,1)}, bf16[4,64,1664]{2,1,0:T(8,128)(2,1)}, u32[]{:S(2)}, u32[]{:S(2)}) collective-permute-start(bf16[4,64,1664]{2,1,0:T(8,128)(2,1)} %stack_second.1.refs_0_), channel_id=1, source_target_pairs={{0,2},{1,3},{2,0},{3,1},{4,6},{5,7},{6,4},{7,5},{8,10},{9,11},{10,... | collective-permute-start | bytes 2555912 | tf_op jit(solution)/shard_map/ppermute | solution.py:270
  56.1 38.7 %collective-permute-start.14 = (bf16[4,64,1664]{2,1,0:T(8,128)(2,1)}, bf16[4,64,1664]{2,1,0:T(8,128)(2,1)}, u32[]{:S(2)}, u32[]{:S(2)}) collective-permute-start(bf16[4,64,1664]{2,1,0:T(8,128)(2,1)} %stack_second.1.refs_0_), channel_id=1, source_target_pairs={{0,4},{1,5},{2,6},{3,7},{4,0},{5,1},{6,2},{7,3},{8,12},{9,13},{10,... | collective-permute-start | bytes 2555912 | tf_op jit(solution)/shard_map/ppermute | solution.py:270
  57.6 38.8 %collective-permute-start.15 = (bf16[4,64,1664]{2,1,0:T(8,128)(2,1)}, bf16[4,64,1664]{2,1,0:T(8,128)(2,1)}, u32[]{:S(2)}, u32[]{:S(2)}) collective-permute-start(bf16[4,64,1664]{2,1,0:T(8,128)(2,1)} %stack_second.1.refs_0_), channel_id=1, source_target_pairs={{0,6},{1,7},{2,4},{3,5},{4,2},{5,3},{6,0},{7,1},{8,14},{9,15},{10,... | collective-permute-start | bytes 2555912 | tf_op jit(solution)/shard_map/ppermute | solution.py:270
  99.2 30.8 %collective-permute-start.28 = (bf16[256,512]{1,0:T(8,128)(2,1)}, bf16[256,512]{1,0:T(8,128)(2,1)S(1)}, u32[]{:S(2)}, u32[]{:S(2)}) collective-permute-start(bf16[256,512]{1,0:T(8,128)(2,1)} %get-tuple-element.396), channel_id=1, source_target_pairs={{0,1},{1,0},{2,3},{3,2},{4,5},{5,4},{6,7},{7,6},{8,9},{9,8},{10,11... | collective-permute-start | bytes 786440 | tf_op jit(solution)/shard_map/ppermute | solution.py:240
  160.8 18.8 %collective-permute-start.27 = (f32[256,512]{1,0:T(8,128)}, f32[256,512]{1,0:T(8,128)}, u32[]{:S(2)}, u32[]{:S(2)}) collective-permute-start(f32[256,512]{1,0:T(8,128)} %get-tuple-element.391), channel_id=1, source_target_pairs={{0,1},{1,0},{2,3},{3,2},{4,5},{5,4},{6,7},{7,6},{8,9},{9,8},{10,11... | collective-permute-start | bytes 1572872 | tf_op jit(solution)/shard_map/ppermute | solution.py:240
  190.7 15.1 %collective-permute-start.37 = (bf16[4,40,1664]{2,1,0:T(8,128)(2,1)}, bf16[4,40,1664]{2,1,0:T(8,128)(2,1)}, u32[]{:S(2)}, u32[]{:S(2)}) collective-permute-start(bf16[4,40,1664]{2,1,0:T(8,128)(2,1)} %get-tuple-element.271), channel_id=1, source_target_pairs={{0,4},{4,0},{1,5},{5,1},{2,6},{6,2},{3,7},{7,3},{8,12},{12,8},{9,1... | collective-permute-start | bytes 1597448 | tf_op jit(solution)/shard_map/ppermute | solution.py:250
  191.6 14.2 %collective-permute-start.38 = (bf16[4,32,1664]{2,1,0:T(8,128)(2,1)}, bf16[4,32,1664]{2,1,0:T(8,128)(2,1)}, u32[]{:S(2)}, u32[]{:S(2)}) collective-permute-start(bf16[4,32,1664]{2,1,0:T(8,128)(2,1)} %get-tuple-element.272), channel_id=1, source_target_pairs={{0,2},{1,3},{2,0},{3,1},{4,6},{5,7},{6,4},{7,5},{8,10},{9,11},{10,... | collective-permute-start | bytes 1277960 | tf_op jit(solution)/shard_map/ppermute | solution.py:245
  208.3 25.8 %collective-permute-start.39 = (bf16[4,40,1664]{2,1,0:T(8,128)(2,1)}, bf16[4,40,1664]{2,1,0:T(8,128)(2,1)}, u32[]{:S(2)}, u32[]{:S(2)}) collective-permute-start(bf16[4,40,1664]{2,1,0:T(8,128)(2,1)} %get-tuple-element.301), channel_id=1, source_target_pairs={{0,2},{1,3},{2,0},{3,1},{4,6},{5,7},{6,4},{7,5},{8,10},{9,11},{10,... | collective-permute-start | bytes 1597448 | tf_op jit(solution)/shard_map/ppermute | solution.py:245
  208.9 25.2 %collective-permute-start.40 = (bf16[4,32,1664]{2,1,0:T(8,128)(2,1)}, bf16[4,32,1664]{2,1,0:T(8,128)(2,1)}, u32[]{:S(2)}, u32[]{:S(2)}) collective-permute-start(bf16[4,32,1664]{2,1,0:T(8,128)(2,1)} %get-tuple-element.302), channel_id=1, source_target_pairs={{0,2},{1,3},{2,0},{3,1},{4,6},{5,7},{6,4},{7,5},{8,10},{9,11},{10,... | collective-permute-start | bytes 1277960 | tf_op jit(solution)/shard_map/ppermute | solution.py:245
  210.4 23.7 %collective-permute-start.41 = (bf16[4,40,1664]{2,1,0:T(8,128)(2,1)}, bf16[4,40,1664]{2,1,0:T(8,128)(2,1)}, u32[]{:S(2)}, u32[]{:S(2)}) collective-permute-start(bf16[4,40,1664]{2,1,0:T(8,128)(2,1)} %get-tuple-element.303), channel_id=1, source_target_pairs={{0,4},{4,0},{1,5},{5,1},{2,6},{6,2},{3,7},{7,3},{8,12},{12,8},{9,1... | collective-permute-start | bytes 1597448 | tf_op jit(solution)/shard_map/ppermute | solution.py:250
  210.9 23.2 %collective-permute-start.42 = (bf16[4,32,1664]{2,1,0:T(8,128)(2,1)}, bf16[4,32,1664]{2,1,0:T(8,128)(2,1)}, u32[]{:S(2)}, u32[]{:S(2)}) collective-permute-start(bf16[4,32,1664]{2,1,0:T(8,128)(2,1)} %get-tuple-element.304), channel_id=1, source_target_pairs={{0,4},{4,0},{1,5},{5,1},{2,6},{6,2},{3,7},{7,3},{8,12},{12,8},{9,1... | collective-permute-start | bytes 1277960 | tf_op jit(solution)/shard_map/ppermute | solution.py:250
  234.1 11.9 %collective-permute-start.43 = (bf16[320,512]{1,0:T(8,128)(2,1)}, bf16[320,512]{1,0:T(8,128)(2,1)S(1)}, u32[]{:S(2)}, u32[]{:S(2)}) collective-permute-start(bf16[320,512]{1,0:T(8,128)(2,1)} %get-tuple-element.310), channel_id=1, source_target_pairs={{0,4},{4,0},{1,5},{5,1},{2,6},{6,2},{3,7},{7,3},{8,12},{12,8},{9,1... | collective-permute-start | bytes 983048 | tf_op jit(solution)/shard_map/ppermute | solution.py:250
  234.7 11.4 %collective-permute-start.44 = (bf16[320,512]{1,0:T(8,128)(2,1)}, bf16[320,512]{1,0:T(8,128)(2,1)}, u32[]{:S(2)}, u32[]{:S(2)}) collective-permute-start(bf16[320,512]{1,0:T(8,128)(2,1)} %get-tuple-element.311), channel_id=1, source_target_pairs={{0,2},{1,3},{2,0},{3,1},{4,6},{5,7},{6,4},{7,5},{8,10},{9,11},{10,... | collective-permute-start | bytes 983048 | tf_op jit(solution)/shard_map/ppermute | solution.py:245
  249.8 13.9 %collective-permute-start.46 = (bf16[320,512]{1,0:T(8,128)(2,1)}, bf16[320,512]{1,0:T(8,128)(2,1)S(1)}, u32[]{:S(2)}, u32[]{:S(2)}) collective-permute-start(bf16[320,512]{1,0:T(8,128)(2,1)} %get-tuple-element.319), channel_id=1, source_target_pairs={{0,2},{1,3},{2,0},{3,1},{4,6},{5,7},{6,4},{7,5},{8,10},{9,11},{10,... | collective-permute-start | bytes 983048 | tf_op jit(solution)/shard_map/ppermute | solution.py:245
  251.0 12.7 %collective-permute-start.47 = (bf16[320,512]{1,0:T(8,128)(2,1)}, bf16[320,512]{1,0:T(8,128)(2,1)S(1)}, u32[]{:S(2)}, u32[]{:S(2)}) collective-permute-start(bf16[320,512]{1,0:T(8,128)(2,1)} %get-tuple-element.320), channel_id=1, source_target_pairs={{0,4},{4,0},{1,5},{5,1},{2,6},{6,2},{3,7},{7,3},{8,12},{12,8},{9,1... | collective-permute-start | bytes 983048 | tf_op jit(solution)/shard_map/ppermute | solution.py:250
  251.8 13.3 %collective-permute-start.48 = (bf16[320,512]{1,0:T(8,128)(2,1)}, bf16[320,512]{1,0:T(8,128)(2,1)S(1)}, u32[]{:S(2)}, u32[]{:S(2)}) collective-permute-start(bf16[320,512]{1,0:T(8,128)(2,1)} %get-tuple-element.321), channel_id=1, source_target_pairs={{0,4},{4,0},{1,5},{5,1},{2,6},{6,2},{3,7},{7,3},{8,12},{12,8},{9,1... | collective-permute-start | bytes 983048 | tf_op jit(solution)/shard_map/ppermute | solution.py:250
  255.5 18.5 %collective-permute-start.58 = (bf16[72,1664]{1,0:T(8,128)(2,1)}, bf16[72,1664]{1,0:T(8,128)(2,1)S(1)}, u32[]{:S(2)}, u32[]{:S(2)}) collective-permute-start(bf16[72,1664]{1,0:T(8,128)(2,1)} %get-tuple-element.394), channel_id=1, source_target_pairs={{0,8},{8,16},{16,24},{24,0},{1,9},{9,17},{17,25},{25,1},{2,10},{10... | collective-permute-start | bytes 718856 | tf_op jit(solution)/shard_map/ppermute | solution.py:250
  268.6 13.0 %collective-permute-start.59 = (bf16[72,1664]{1,0:T(8,128)(2,1)}, bf16[72,1664]{1,0:T(8,128)(2,1)S(1)}, u32[]{:S(2)}, u32[]{:S(2)}) collective-permute-start(bf16[72,1664]{1,0:T(8,128)(2,1)} %get-tuple-element.393), channel_id=1, source_target_pairs={{0,16},{8,24},{16,0},{24,8},{1,17},{9,25},{17,1},{25,9},{2,18},{10... | collective-permute-start | bytes 718856 | tf_op jit(solution)/shard_map/ppermute | solution.py:250
  268.6 13.2 %collective-permute-start.60 = (bf16[72,1664]{1,0:T(8,128)(2,1)}, bf16[72,1664]{1,0:T(8,128)(2,1)}, u32[]{:S(2)}, u32[]{:S(2)}) collective-permute-start(bf16[72,1664]{1,0:T(8,128)(2,1)} %get-tuple-element.392), channel_id=1, source_target_pairs={{0,24},{8,0},{16,8},{24,16},{1,25},{9,1},{17,9},{25,17},{2,26},{10... | collective-permute-start | bytes 718856 | tf_op jit(solution)/shard_map/ppermute | solution.py:250
  281.5 15.8 %collective-permute-start.49 = (f32[256,512]{1,0:T(8,128)}, f32[256,512]{1,0:T(8,128)S(1)}, u32[]{:S(2)}, u32[]{:S(2)}) collective-permute-start(f32[256,512]{1,0:T(8,128)} %get-tuple-element.388), channel_id=1, source_target_pairs={{0,1},{1,0},{2,3},{3,2},{4,5},{5,4},{6,7},{7,6},{8,9},{9,8},{10,11... | collective-permute-start | bytes 1572872 | tf_op jit(solution)/shard_map/ppermute | solution.py:240
  (110 other events, 672.5 us)

commit v5 on v4

--- a/solution.py
+++ b/solution.py
@@ -55,7 +55,7 @@
 
 
 def attend_kernel(heads, q, k, v, qp, kp, *refs):
-    out, exact, weights, inverse = refs[-4:]
+    out, exact, weights = refs[-3:]
     allowed = kp[...] <= qp[...]
     for head in range(heads):
         cols = slice(head * HEAD_DIM, (head + 1) * HEAD_DIM)
@@ -64,28 +64,26 @@
         largest = jnp.max(scores, axis=0, keepdims=True)
         power = jnp.exp(scores - largest)
         rate = 1.0 / jnp.sum(power, axis=0, keepdims=True)
-        low = power.astype(BF16)
+        low = (power * rate).astype(BF16)
         weights[head] = low
-        inverse[head] = rate
-        mixed = contract(v[:, cols], low, 0, 0) * rate
+        mixed = contract(v[:, cols], low, 0, 0)
         exact[cols, :] = mixed
         out[:, cols] = mixed.T.astype(BF16)
 
 
-def attend_back_kernel(heads, q, k, v, weights, inverse, exact, grad, *refs):
+def attend_back_kernel(heads, q, k, v, weights, exact, grad, *refs):
     dq, dk, dv, dq_sum, dv_sum = refs[-5:]
     for head in range(heads):
         cols = slice(head * HEAD_DIM, (head + 1) * HEAD_DIM)
         grads = grad[:, cols].astype(F32).T
-        inner = jnp.sum(grads * exact[cols, :], axis=0, keepdims=True) * inverse[head]
-        scaled = (grads * inverse[head]).astype(BF16)
+        inner = jnp.sum(grads * exact[cols, :], axis=0, keepdims=True)
         weight = weights[head]
-        grad_weight = contract(v[:, cols], scaled, 1, 0)
+        grad_weight = contract(v[:, cols], grad[:, cols], 1, 1)
         grad_scores = (weight.astype(F32) * (grad_weight - inner)).astype(BF16)
         low = (contract(k[:, cols], grad_scores, 0, 0) * SCALE).T.astype(BF16)
         dq[:, cols] = low
         dq_sum[:, cols] = jnp.sum(low.astype(F32), axis=0, keepdims=True)
-        low = contract(weight, scaled, 1, 1).astype(BF16)
+        low = contract(weight, grad[:, cols], 1, 0).astype(BF16)
         dv[:, cols] = low
         dv_sum[:, cols] = jnp.sum(low.astype(F32), axis=0, keepdims=True)
         dk[:, cols] = (contract(grad_scores, q[:, cols], 1, 0) * SCALE).astype(BF16)
@@ -143,9 +141,8 @@
             jax.ShapeDtypeStruct((rows, width), BF16),
             jax.ShapeDtypeStruct((width, rows), F32),
             jax.ShapeDtypeStruct((heads, keys, rows), BF16),
-            jax.ShapeDtypeStruct((heads, 1, rows), F32),
         ],
-        [columns(rows), lines(rows), by_head(keys, rows), by_head(1, rows)],
+        [columns(rows), lines(rows), by_head(keys, rows)],
         earlier,
         each,
         steps,
@@ -158,7 +155,7 @@
     )
 
 
-def attend_back(q, k, v, weights, inverse, exact, grad, part=0, parts=1, earlier=None):
+def attend_back(q, k, v, weights, exact, grad, part=0, parts=1, earlier=None):
     rows, width = q.shape
     keys = k.shape[0]
     heads = width // HEAD_DIM
@@ -167,13 +164,12 @@
     columns, lines, by_head = head_specs(part * steps, each)
     return attend_call(
         attend_back_kernel,
-        (q, k, v, weights, inverse, exact, grad),
+        (q, k, v, weights, exact, grad),
         [
             columns(rows),
             columns(keys),
             columns(keys),
             by_head(keys, rows),
-            by_head(1, rows),
             lines(rows),
             columns(rows),
         ],
@@ -532,7 +528,7 @@
     own = jnp.concatenate(own, axis=1) if len(own) > 1 else own[0]
     low = own.astype(BF16)
     at = lax.axis_index("fsdp")
-    result = lax.dynamic_index_in_dim(own, at, 0, keepdims=False)
+    result = lax.dynamic_index_in_dim(low, at, 0, keepdims=False).astype(F32)
     moved = []
     for k in range(1, deep):
         piece = lax.dynamic_index_in_dim(low, (at + k) % deep, 0, keepdims=False)
@@ -774,6 +770,7 @@
     first_pieces = spread(after(first_pack, got))
     blocks = plane_one(keep, got)
     first_depth = depth_blocks(first_pieces, 1, "stack_first")[0]
+    positions = after(positions, first_depth)
     *blocks, (first_depth,) = gated(blocks + [(first_depth,)])[0]
     blocks = plane_two(blocks)
     first_blocks = plane_direct(first_depth)
@@ -830,7 +827,7 @@
     query_low = (product(rows_in, full_query) + query_bias).astype(BF16)
     keys = product(wide_rows, full_key).astype(BF16)
     values = (product(wide_rows, full_value) + value_bias).astype(BF16)
-    attended, attended_exact, weights, inverse = attend(
+    attended, attended_exact, weights = attend(
         query_low, keys, values, query_positions, key_positions
     )
     second_blocks, attended = gated(second_blocks, attended)
@@ -850,7 +847,7 @@
     first_out = layer_norm(first_in, first_gain, first_shift)
     first_low = first_out.astype(BF16)
     cross_query = (product(first_low, full_cross_query) + cross_query_bias).astype(BF16)
-    cross_attended, cross_exact, cross_weights, cross_inverse = attend(
+    cross_attended, cross_exact, cross_weights = attend(
         cross_query, memory_key, memory_value, memory_limit, memory_slots
     )
     second_in = first_out + product_right(cross_attended, full_cross_output) + cross_output_bias
@@ -883,7 +880,6 @@
         memory_key,
         memory_value,
         cross_weights,
-        cross_inverse,
         cross_exact,
         cross_attended_grad,
     )
@@ -928,14 +924,14 @@
     second_blocks, early_grad = gated(second_blocks, attended_grad)
     second_blocks = sum_one(second_blocks)
     early = list(
-        attend_back(query_low, keys, values, weights, inverse, attended_exact, early_grad, 0, 2)
+        attend_back(query_low, keys, values, weights, attended_exact, early_grad, 0, 2)
     )
     second_blocks, early[0] = gated(second_blocks, early[0])
     second_blocks = sum_adds(second_blocks)
     second_blocks, late_grad = gated(second_blocks, attended_grad)
     second_left = sum_two(second_blocks)
     query_grad, key_grad, value_grad, *self_sums = attend_back(
-        query_low, keys, values, weights, inverse, attended_exact, late_grad, 1, 2, early
+        query_low, keys, values, weights, attended_exact, late_grad, 1, 2, early
     )
     input_part, memory_own, low_blocks = row_grads(
         key_grad, value_grad, full_key, full_value, memory_part, own_rows

time: 303 us -> 300 us (0.990)
  starting transfers between devices: 47.9 us -> 53.5 us
  waiting for transfers between devices: 33.7 us -> 28.8 us
    ppermute x21, waiting for transfers between devices: 18.7 us -> 10.9 us  [shift(): lax.ppermute(value, axis, [(i, (i + step) % total) for i in range(total)])]
    ppermute x21, starting transfers between devices: 21.5 us -> 28 us  [shift(): lax.ppermute(value, axis, [(i, (i + step) % total) for i in range(total)])]
    add x4 -> x2, other arithmetic: 4.87 us -> 0.18 us  [summed(): return sum((part.astype(F32) for part in parts))]
    another operation x0 -> x2, other arithmetic: none -> 3.76 us
    unnamed x163 -> x165, local copies, waits for them, and re-layouts: 10.3 us -> 9.18 us
  transfers between devices with their start and end apart: 64 -> 64, of which waited for: 18 -> 16; matrix products, arithmetic and copies ran while one was open for 23% -> 23% of each run, Pallas kernels for 32% -> 32%
where the time goes in v5:
time: 300 us; the launch traced here: 296 us
  Pallas kernels  117 us (39%)
  starting transfers between devices  53.5 us (18%)
  matrix products  49 us (16%)
  waiting for transfers between devices  28.8 us (10%)
  other arithmetic  25.1 us (8%)
  local copies, waits for them, and re-layouts  20.1 us (7%)
    pallas_call x5, Pallas kernels, attend_call(): pl.pallas_call(functools.partial(body, each), grid=(steps,), in_specs=spe...  64 us
    dot_general x28, matrix products, contract(): lax.dot_general(left, right, (((left_dim,), (right_dim,)), ((), ())), pre...  49 us
    ppermute x21, starting transfers between devices, shift(): lax.ppermute(value, axis, [(i, (i + step) % total) for i in range(total)])  28 us
    pallas_call x7, Pallas kernels, move(): pl.pallas_call(body, in_specs=[pl.BlockSpec(memory_space=pl.ANY)] * len(s...  27 us
    pallas_call x4, Pallas kernels, add_many(): pl.pallas_call(add_kernel, grid=(steps,), in_specs=[spec(part) for part i...  13 us
    ppermute x21, waiting for transfers between devices, shift(): lax.ppermute(value, axis, [(i, (i + step) % total) for i in range(total)])  10.9 us
    ppermute x9, starting transfers between devices, shift_plane(): return lax.ppermute(value, ('ctx', 'tp'), pairs)  10.5 us
    ppermute x9, waiting for transfers between devices, shift_plane(): return lax.ppermute(value, ('ctx', 'tp'), pairs)  9.58 us
  transfers between devices with their start and end apart: 64, of which 16 were waited for; matrix products, arithmetic and copies ran while one was open for 23% of the time, Pallas kernels for 32%

profile of v5, /device:TPU:0, one launch (start us, length us, event | category | flops | bytes accessed | tf_op | source)
XLA Modules:
  0.0 295.8 jit_solution(1890961306464483866)
XLA Ops:
  4.8 2.9 collective-permute-start.5
  7.8 2.6 collective-permute-start.6
  37.9 2.4 collective-permute-start.12
  42.2 3.6 %collective-permute-done.8.refs_6_ = bf16[320,512]{1,0:T(8,128)(2,1)S(1)} collective-permute-done((bf16[320,512]{1,0:T(8,128)(2,1)S(1)}, bf16[320,512]{1,0:T(8,128)(2,1)S(1)}, u32[]{:S(2)}, u32[]{:S(2)}) %collective-permute-start.8) | collective-permute-done | bytes 327712 | tf_op jit(solution)/shard_map/ppermute | solution.py:246
  48.0 3.3 %rows_together.1 = (bf16[2048,512]{1,0:T(8,128)(2,1)}, bf16[512,512]{1,0:T(8,128)(2,1)}) custom-call(bf16[320,512]{1,0:T(8,128)(2,1)} %get-tuple-element.197.refs_0_, bf16[320,512]{1,0:T(8,128)(2,1)} %copy-done.36, bf16[320,512]{1,0:T(8,128)(2,1)} %copy-done.37, bf16[320,512]{1,0:T(8,128)(2,1)} %copy-done.39, bf16[320,512]{1,0:T(8,128)(2,1)} %copy-done.38, ...), custom_call_target="tpu_custom_call" | custom-call | tf_op jit(solution)/shard_map/rows_together/pallas_call | solution.py:210
  59.1 2.8 place_first.1
  62.0 3.7 %convolution_convert_fusion.2.k = bf16[2048,512]{1,0:T(8,128)(2,1)} fusion(bf16[2048,512]{1,0:T(8,128)(2,1)S(1)} %copy-done, bf16[512,512]{1,0:T(8,128)(2,1)} %bitcast.147), kind=kOutput, calls=%fused_computation.7 | convolution fusion | flops 1074790400 | bytes 4718592 | tf_op jit(solution)/shard_map/dot_general | solution.py:20
  65.7 2.6 add_convert_fusion.v
  69.5 21.2 %attend.2 = (bf16[512,512]{1,0:T(8,128)(2,1)}, f32[512,512]{1,0:T(8,128)}, bf16[8,2048,512]{2,1,0:T(8,128)(2,1)}) custom-call(bf16[512,512]{1,0:T(8,128)(2,1)} %fusion.2.q, bf16[2048,512]{1,0:T(8,128)(2,1)} %convolution_convert_fusion.2.k, bf16[2048,512]{1,0:T(8,128)(2,1)} %add_convert_fusion.v, s32[1,512]{1,0:T(1,128)} %bitcast.181, ...), custom_call_target="tpu_custom_call" | custom-call | flops 8589934592 | bytes 16777216 | tf_op jit(solution)/shard_map/attend/pallas_call | solution.py:97
  90.7 4.1 %collective-permute-done.14.refs_2_ = bf16[4,64,1664]{2,1,0:T(8,128)(2,1)} collective-permute-done((bf16[4,64,1664]{2,1,0:T(8,128)(2,1)}, bf16[4,64,1664]{2,1,0:T(8,128)(2,1)}, u32[]{:S(2)}, u32[]{:S(2)}) %collective-permute-start.14) | collective-permute-done | bytes 852000 | tf_op jit(solution)/shard_map/ppermute | solution.py:266
  101.1 6.4 %place_second.1 = (bf16[4,2,64,512]{3,2,1,0:T(8,128)(2,1)}, bf16[4,2,64,512]{3,2,1,0:T(8,128)(2,1)}, bf16[4,2,64,512]{3,2,1,0:T(8,128)(2,1)}, bf16[4,2,64,512]{3...) custom-call(bf16[4,64,1664]{2,1,0:T(8,128)(2,1)} %stack_second.1.ref, ...), custom_call_target="tpu_custom_call" | custom-call | tf_op jit(solution)/shard_map/place_second/pallas_call | solution.py:210
  114.0 8.9 %attend.3 = (bf16[512,512]{1,0:T(8,128)(2,1)}, f32[512,512]{1,0:T(8,128)}, bf16[8,512,512]{2,1,0:T(8,128)(2,1)}) custom-call(bf16[512,512]{1,0:T(8,128)(2,1)} %fusion.3.q, bf16[512,512]{1,0:T(8,128)(2,1)} %convolution_convert_fusion.13.k, bf16[512,512]{1,0:T(8,128)(2,1)} %fusion.4.v, s32[1,512]{1,0:T(1,128)} %broadcast_in_dim.20.qp, s32[512,1]{1,0:T(8,128)} %copy.84.kp), custom_call_target="tpu_custom_call" | custom-call | flops 2147483648 | bytes 4194304 | tf_op jit(solution)/shard_map/attend/pallas_call | solution.py:97
  132.0 2.4 convert_reduce_fusion
  138.9 8.7 %attend_back.3 = (bf16[512,512]{1,0:T(8,128)(2,1)}, bf16[512,512]{1,0:T(8,128)(2,1)}, bf16[512,512]{1,0:T(8,128)(2,1)}, f32[1,512]{1,0:T(1,128)}, f32[1,512]{1,0:T(1,128)}) custom-call(bf16[512,512]{1,0:T(8,128)(2,1)} %fusion.3.q, bf16[512,512]{1,0:T(8,128)(2,1)} %convolution_convert_fusion.13.k, bf16[512,512]{1,0:T(8,128)(2,1)} %fusion.4.v, ...), custom_call_target="tpu_custom_call" | custom-call | flops 4294967296 | bytes 4194304 | tf_op jit(solution)/shard_map/attend_back/pallas_call | solution.py:97
  147.6 2.7 multiply_reduce_fusion.2
  153.0 2.7 convolution_convert_fusion.1
  155.7 2.7 convolution_convert_fusion
  166.5 7.6 %split_second.1 = (bf16[4,40,1664]{2,1,0:T(8,128)(2,1)}, bf16[4,32,1664]{2,1,0:T(8,128)(2,1)}, bf16[4,40,1664]{2,1,0:T(8,128)(2,1)}, bf16[4,32,1664]{2,1,0:T(8,1...) custom-call(bf16[4,2,64,512]{3,2,1,0:T(8,128)(2,1)} %bitcast.162, ...), custom_call_target="tpu_custom_call" | custom-call | tf_op jit(solution)/shard_map/split_second/pallas_call | solution.py:210
  181.0 2.3 maximum_select_fusion
  183.4 5.7 %add_many.4 = (bf16[4,40,1664]{2,1,0:T(8,128)(2,1)}, bf16[4,32,1664]{2,1,0:T(8,128)(2,1)}, bf16[4,40,1664]{2,1,0:T(8,128)(2,1)}, bf16[4,32,1664]{2,1,0:T(8,128)(...) custom-call(bf16[4,40,1664]{2,1,0:T(8,128)(2,1)} %get-tuple-element., ...), custom_call_target="tpu_custom_call" | custom-call | tf_op jit(solution)/shard_map/add_many/pallas_call | solution.py:318
  191.3 12.7 %attend_back.4 = (bf16[512,512]{1,0:T(8,128)(2,1)}, bf16[2048,512]{1,0:T(8,128)(2,1)}, bf16[2048,512]{1,0:T(8,128)(2,1)}, f32[1,512]{1,0:T(1,128)}, f32[1,512]{1,0:T(1,128)}) custom-call(bf16[512,512]{1,0:T(8,128)(2,1)} %fusion.2.q, bf16[2048,512]{1,0:T(8,128)(2,1)} %convolution_convert_fusion.2.k, bf16[2048,512]{1,0:T(8,128)(2,1)} %add_convert_fusion.v, ...), custom_call_target="tpu_custom_call" | custom-call | flops 8589934592 | bytes 8388608 | tf_op jit(solution)/shard_map/attend_back/pallas_call | solution.py:97
  204.0 2.6 add_many.5
  210.7 12.6 %attend_back.5 = (bf16[512,512]{1,0:T(8,128)(2,1)}, bf16[2048,512]{1,0:T(8,128)(2,1)}, bf16[2048,512]{1,0:T(8,128)(2,1)}, f32[1,512]{1,0:T(1,128)}, f32[1,512]{1,0:T(1,128)}) custom-call(bf16[512,512]{1,0:T(8,128)(2,1)} %fusion.2.q, ...), custom_call_target="tpu_custom_call", output_to_operand_aliasing={{0}: (6, {}), {1}: (7, {}), {2}: (8, {}), {3}: (9, {}), {4}... | custom-call | flops 8589934592 | bytes 8388608 | tf_op jit(solution)/shard_map/attend_back/pallas_call | solution.py:97
  224.6 7.8 %row_grads.1 = (f32[512,512]{1,0:T(8,128)}, f32[128,512]{1,0:T(8,128)}, bf16[320,512]{1,0:T(8,128)(2,1)}, bf16[320,512]{1,0:T(8,128)(2,1)}, bf16[320,512]{1,0:T(...) custom-call(bf16[2048,512]{1,0:T(8,128)(2,1)} %get-tuple-element.314.dk, ...), custom_call_target="tpu_custom_call" | custom-call | tf_op jit(solution)/shard_map/row_grads/pallas_call | solution.py:599
  236.5 2.3 add_convert_fusion.1
  252.3 3.1 %split_first.1 = (bf16[4,72,384]{2,1,0:T(8,128)(2,1)}, bf16[4,72,384]{2,1,0:T(8,128)(2,1)}, bf16[4,72,384]{2,1,0:T(8,128)(2,1)}, bf16[4,72,384]{2,1,0:T(8,128)(2...) custom-call(bf16[4,2,64,512]{3,2,1,0:T(8,128)(2,1)} %bitcast.154, ...), custom_call_target="tpu_custom_call" | custom-call | tf_op jit(solution)/shard_map/split_first/pallas_call | solution.py:210
  256.0 4.2 %collective-permute-done.46 = bf16[320,512]{1,0:T(8,128)(2,1)S(1)} collective-permute-done((bf16[320,512]{1,0:T(8,128)(2,1)}, bf16[320,512]{1,0:T(8,128)(2,1)S(1)}, u32[]{:S(2)}, u32[]{:S(2)}) %collective-permute-start.46) | collective-permute-done | bytes 327712 | tf_op jit(solution)/shard_map/ppermute | solution.py:241
  264.9 2.6 collective-permute-start.60
  267.5 2.5 add_many.7
  273.5 2.5 fusion.10
  278.8 2.5 collective-permute-done.56
  289.9 2.4 collective-permute-done.62
  (372 shorter events, 136.3 us)
Async XLA Ops:
  4.8 11.1 %collective-permute-start.5 = (bf16[64,384]{1,0:T(8,128)(2,1)}, bf16[64,384]{1,0:T(8,128)(2,1)S(1)}, u32[]{:S(2)}, u32[]{:S(2)}) collective-permute-start(bf16[64,384]{1,0:T(8,128)(2,1)} %get-tuple-element.196.refs_0_), channel_id=1, source_target_pairs={{0,8},{8,16},{16,24},{24,0},{1,9},{9,17},{17,25},{25,1},{2,10},{10... | collective-permute-start | bytes 147464 | tf_op jit(solution)/shard_map/ppermute | solution.py:246
  11.7 12.2 %collective-permute-start.1 = (bf16[320,512]{1,0:T(8,128)(2,1)}, bf16[320,512]{1,0:T(8,128)(2,1)S(1)}, u32[]{:S(2)}, u32[]{:S(2)}) collective-permute-start(bf16[320,512]{1,0:T(8,128)(2,1)} %get-tuple-element.197.refs_0_), channel_id=1, source_target_pairs={{0,2},{1,3},{2,0},{3,1},{4,6},{5,7},{6,4},{7,5},{8,10},{9,11},{10,... | collective-permute-start | bytes 983048 | tf_op jit(solution)/shard_map/ppermute | solution.py:241
  13.2 13.0 %collective-permute-start.3 = (bf16[320,512]{1,0:T(8,128)(2,1)}, bf16[320,512]{1,0:T(8,128)(2,1)S(1)}, u32[]{:S(2)}, u32[]{:S(2)}) collective-permute-start(bf16[320,512]{1,0:T(8,128)(2,1)} %get-tuple-element.197.refs_0_), channel_id=1, source_target_pairs={{0,4},{4,0},{1,5},{5,1},{2,6},{6,2},{3,7},{7,3},{8,12},{12,8},{9,1... | collective-permute-start | bytes 983048 | tf_op jit(solution)/shard_map/ppermute | solution.py:246
  15.9 11.9 %collective-permute-start.2 = (bf16[320,512]{1,0:T(8,128)(2,1)S(1)}, bf16[320,512]{1,0:T(8,128)(2,1)S(1)}, u32[]{:S(2)}, u32[]{:S(2)}) collective-permute-start(bf16[320,512]{1,0:T(8,128)(2,1)S(1)} %collective-permute-done.refs_1_), channel_id=1, source_target_pairs={{0,2},{1,3},{2,0},{3,1},{4,6},{5,7},{6,4},{7,5},{8,10},{9,11},{10,... | collective-permute-start | bytes 983048 | tf_op jit(solution)/shard_map/ppermute | solution.py:241
  16.5 12.6 %collective-permute-start.4 = (bf16[320,512]{1,0:T(8,128)(2,1)S(1)}, bf16[320,512]{1,0:T(8,128)(2,1)S(1)}, u32[]{:S(2)}, u32[]{:S(2)}) collective-permute-start(bf16[320,512]{1,0:T(8,128)(2,1)S(1)} %collective-permute-done.refs_1_), channel_id=1, source_target_pairs={{0,4},{4,0},{1,5},{5,1},{2,6},{6,2},{3,7},{7,3},{8,12},{12,8},{9,1... | collective-permute-start | bytes 983048 | tf_op jit(solution)/shard_map/ppermute | solution.py:246
  17.0 15.5 %collective-permute-start.10 = (bf16[64,1664]{1,0:T(8,128)(2,1)}, bf16[64,1664]{1,0:T(8,128)(2,1)S(1)}, u32[]{:S(2)}, u32[]{:S(2)}) collective-permute-start(bf16[64,1664]{1,0:T(8,128)(2,1)} %get-tuple-element.206.refs_0_), channel_id=1, source_target_pairs={{0,8},{8,16},{16,24},{24,0},{1,9},{9,17},{17,25},{25,1},{2,10},{10... | collective-permute-start | bytes 638984 | tf_op jit(solution)/shard_map/ppermute | solution.py:246
  29.6 12.1 %collective-permute-start.17 = (bf16[4,64,384]{2,1,0:T(8,128)(2,1)}, bf16[4,64,384]{2,1,0:T(8,128)(2,1)}, u32[]{:S(2)}, u32[]{:S(2)}) collective-permute-start(bf16[4,64,384]{2,1,0:T(8,128)(2,1)} %stack_first.1.refs_0_), channel_id=1, source_target_pairs={{0,4},{1,5},{2,6},{3,7},{4,0},{5,1},{6,2},{7,3},{8,12},{9,13},{10,... | collective-permute-start | bytes 589832 | tf_op jit(solution)/shard_map/ppermute | solution.py:266
  32.5 13.3 %collective-permute-start.8 = (bf16[320,512]{1,0:T(8,128)(2,1)S(1)}, bf16[320,512]{1,0:T(8,128)(2,1)S(1)}, u32[]{:S(2)}, u32[]{:S(2)}) collective-permute-start(bf16[320,512]{1,0:T(8,128)(2,1)S(1)} %collective-permute-done.1.refs_2_), channel_id=1, source_target_pairs={{0,4},{4,0},{1,5},{5,1},{2,6},{6,2},{3,7},{7,3},{8,12},{12,8},{9,1... | collective-permute-start | bytes 983048 | tf_op jit(solution)/shard_map/ppermute | solution.py:246
  34.9 11.0 %collective-permute-start.9 = (bf16[320,512]{1,0:T(8,128)(2,1)S(1)}, bf16[320,512]{1,0:T(8,128)(2,1)}, u32[]{:S(2)}, u32[]{:S(2)}) collective-permute-start(bf16[320,512]{1,0:T(8,128)(2,1)S(1)} %collective-permute-done.4.refs_5_), channel_id=1, source_target_pairs={{0,2},{1,3},{2,0},{3,1},{4,6},{5,7},{6,4},{7,5},{8,10},{9,11},{10,... | collective-permute-start | bytes 983048 | tf_op jit(solution)/shard_map/ppermute | solution.py:241
  37.9 13.4 %collective-permute-start.12 = (bf16[64,1664]{1,0:T(8,128)(2,1)}, bf16[64,1664]{1,0:T(8,128)(2,1)S(1)}, u32[]{:S(2)}, u32[]{:S(2)}) collective-permute-start(bf16[64,1664]{1,0:T(8,128)(2,1)} %get-tuple-element.206.refs_0_), channel_id=1, source_target_pairs={{0,24},{8,0},{16,8},{24,16},{1,25},{9,1},{17,9},{25,17},{2,26},{10... | collective-permute-start | bytes 638984 | tf_op jit(solution)/shard_map/ppermute | solution.py:246
  41.7 14.0 %collective-permute-start.19 = (bf16[4,64,384]{2,1,0:T(8,128)(2,1)}, bf16[4,64,384]{2,1,0:T(8,128)(2,1)S(1)}, u32[]{:S(2)}, u32[]{:S(2)}) collective-permute-start(bf16[4,64,384]{2,1,0:T(8,128)(2,1)} %stack_first.1.refs_0_), channel_id=1, source_target_pairs={{0,1},{1,0},{2,3},{3,2},{4,5},{5,4},{6,7},{7,6},{8,9},{9,8},{10,11... | collective-permute-start | bytes 589832 | tf_op jit(solution)/shard_map/ppermute | solution.py:236
  41.7 15.5 %collective-permute-start.20 = (bf16[4,64,384]{2,1,0:T(8,128)(2,1)}, bf16[4,64,384]{2,1,0:T(8,128)(2,1)S(1)}, u32[]{:S(2)}, u32[]{:S(2)}) collective-permute-start(bf16[4,64,384]{2,1,0:T(8,128)(2,1)} %collective-permute-done.16.refs_1_), channel_id=1, source_target_pairs={{0,1},{1,0},{2,3},{3,2},{4,5},{5,4},{6,7},{7,6},{8,9},{9,8},{10,11... | collective-permute-start | bytes 589832 | tf_op jit(solution)/shard_map/ppermute | solution.py:236
  45.8 12.0 %collective-permute-start.21 = (bf16[4,64,384]{2,1,0:T(8,128)(2,1)}, bf16[4,64,384]{2,1,0:T(8,128)(2,1)S(1)}, u32[]{:S(2)}, u32[]{:S(2)}) collective-permute-start(bf16[4,64,384]{2,1,0:T(8,128)(2,1)} %collective-permute-done.17.refs_2_), channel_id=1, source_target_pairs={{0,1},{1,0},{2,3},{3,2},{4,5},{5,4},{6,7},{7,6},{8,9},{9,8},{10,11... | collective-permute-start | bytes 589832 | tf_op jit(solution)/shard_map/ppermute | solution.py:236
  45.8 12.0 %collective-permute-start.22 = (bf16[4,64,384]{2,1,0:T(8,128)(2,1)}, bf16[4,64,384]{2,1,0:T(8,128)(2,1)S(1)}, u32[]{:S(2)}, u32[]{:S(2)}) collective-permute-start(bf16[4,64,384]{2,1,0:T(8,128)(2,1)} %collective-permute-done.18.refs_3_), channel_id=1, source_target_pairs={{0,1},{1,0},{2,3},{3,2},{4,5},{5,4},{6,7},{7,6},{8,9},{9,8},{10,11... | collective-permute-start | bytes 589832 | tf_op jit(solution)/shard_map/ppermute | solution.py:236
  54.2 36.5 %collective-permute-start.13 = (bf16[4,64,1664]{2,1,0:T(8,128)(2,1)}, bf16[4,64,1664]{2,1,0:T(8,128)(2,1)}, u32[]{:S(2)}, u32[]{:S(2)}) collective-permute-start(bf16[4,64,1664]{2,1,0:T(8,128)(2,1)} %stack_second.1.refs_0_), channel_id=1, source_target_pairs={{0,2},{1,3},{2,0},{3,1},{4,6},{5,7},{6,4},{7,5},{8,10},{9,11},{10,... | collective-permute-start | bytes 2555912 | tf_op jit(solution)/shard_map/ppermute | solution.py:266
  55.7 39.2 %collective-permute-start.14 = (bf16[4,64,1664]{2,1,0:T(8,128)(2,1)}, bf16[4,64,1664]{2,1,0:T(8,128)(2,1)}, u32[]{:S(2)}, u32[]{:S(2)}) collective-permute-start(bf16[4,64,1664]{2,1,0:T(8,128)(2,1)} %stack_second.1.refs_0_), channel_id=1, source_target_pairs={{0,4},{1,5},{2,6},{3,7},{4,0},{5,1},{6,2},{7,3},{8,12},{9,13},{10,... | collective-permute-start | bytes 2555912 | tf_op jit(solution)/shard_map/ppermute | solution.py:266
  57.2 37.7 %collective-permute-start.15 = (bf16[4,64,1664]{2,1,0:T(8,128)(2,1)}, bf16[4,64,1664]{2,1,0:T(8,128)(2,1)}, u32[]{:S(2)}, u32[]{:S(2)}) collective-permute-start(bf16[4,64,1664]{2,1,0:T(8,128)(2,1)} %stack_second.1.refs_0_), channel_id=1, source_target_pairs={{0,6},{1,7},{2,4},{3,5},{4,2},{5,3},{6,0},{7,1},{8,14},{9,15},{10,... | collective-permute-start | bytes 2555912 | tf_op jit(solution)/shard_map/ppermute | solution.py:266
  97.7 31.1 %collective-permute-start.28 = (bf16[256,512]{1,0:T(8,128)(2,1)}, bf16[256,512]{1,0:T(8,128)(2,1)S(1)}, u32[]{:S(2)}, u32[]{:S(2)}) collective-permute-start(bf16[256,512]{1,0:T(8,128)(2,1)} %get-tuple-element.392), channel_id=1, source_target_pairs={{0,1},{1,0},{2,3},{3,2},{4,5},{5,4},{6,7},{7,6},{8,9},{9,8},{10,11... | collective-permute-start | bytes 786440 | tf_op jit(solution)/shard_map/ppermute | solution.py:236
  159.5 18.7 %collective-permute-start.27 = (f32[256,512]{1,0:T(8,128)}, f32[256,512]{1,0:T(8,128)}, u32[]{:S(2)}, u32[]{:S(2)}) collective-permute-start(f32[256,512]{1,0:T(8,128)} %get-tuple-element.387), channel_id=1, source_target_pairs={{0,1},{1,0},{2,3},{3,2},{4,5},{5,4},{6,7},{7,6},{8,9},{9,8},{10,11... | collective-permute-start | bytes 1572872 | tf_op jit(solution)/shard_map/ppermute | solution.py:236
  189.0 15.0 %collective-permute-start.37 = (bf16[4,40,1664]{2,1,0:T(8,128)(2,1)}, bf16[4,40,1664]{2,1,0:T(8,128)(2,1)}, u32[]{:S(2)}, u32[]{:S(2)}) collective-permute-start(bf16[4,40,1664]{2,1,0:T(8,128)(2,1)} %get-tuple-element.269), channel_id=1, source_target_pairs={{0,4},{4,0},{1,5},{5,1},{2,6},{6,2},{3,7},{7,3},{8,12},{12,8},{9,1... | collective-permute-start | bytes 1597448 | tf_op jit(solution)/shard_map/ppermute | solution.py:246
  190.6 13.4 %collective-permute-start.38 = (bf16[4,32,1664]{2,1,0:T(8,128)(2,1)}, bf16[4,32,1664]{2,1,0:T(8,128)(2,1)}, u32[]{:S(2)}, u32[]{:S(2)}) collective-permute-start(bf16[4,32,1664]{2,1,0:T(8,128)(2,1)} %get-tuple-element.270), channel_id=1, source_target_pairs={{0,2},{1,3},{2,0},{3,1},{4,6},{5,7},{6,4},{7,5},{8,10},{9,11},{10,... | collective-permute-start | bytes 1277960 | tf_op jit(solution)/shard_map/ppermute | solution.py:241
  206.6 25.8 %collective-permute-start.39 = (bf16[4,40,1664]{2,1,0:T(8,128)(2,1)}, bf16[4,40,1664]{2,1,0:T(8,128)(2,1)}, u32[]{:S(2)}, u32[]{:S(2)}) collective-permute-start(bf16[4,40,1664]{2,1,0:T(8,128)(2,1)} %get-tuple-element.299), channel_id=1, source_target_pairs={{0,2},{1,3},{2,0},{3,1},{4,6},{5,7},{6,4},{7,5},{8,10},{9,11},{10,... | collective-permute-start | bytes 1597448 | tf_op jit(solution)/shard_map/ppermute | solution.py:241
  208.0 24.4 %collective-permute-start.40 = (bf16[4,32,1664]{2,1,0:T(8,128)(2,1)}, bf16[4,32,1664]{2,1,0:T(8,128)(2,1)}, u32[]{:S(2)}, u32[]{:S(2)}) collective-permute-start(bf16[4,32,1664]{2,1,0:T(8,128)(2,1)} %get-tuple-element.300), channel_id=1, source_target_pairs={{0,2},{1,3},{2,0},{3,1},{4,6},{5,7},{6,4},{7,5},{8,10},{9,11},{10,... | collective-permute-start | bytes 1277960 | tf_op jit(solution)/shard_map/ppermute | solution.py:241
  208.6 23.8 %collective-permute-start.41 = (bf16[4,40,1664]{2,1,0:T(8,128)(2,1)}, bf16[4,40,1664]{2,1,0:T(8,128)(2,1)}, u32[]{:S(2)}, u32[]{:S(2)}) collective-permute-start(bf16[4,40,1664]{2,1,0:T(8,128)(2,1)} %get-tuple-element.301), channel_id=1, source_target_pairs={{0,4},{4,0},{1,5},{5,1},{2,6},{6,2},{3,7},{7,3},{8,12},{12,8},{9,1... | collective-permute-start | bytes 1597448 | tf_op jit(solution)/shard_map/ppermute | solution.py:246
  209.9 22.5 %collective-permute-start.42 = (bf16[4,32,1664]{2,1,0:T(8,128)(2,1)}, bf16[4,32,1664]{2,1,0:T(8,128)(2,1)}, u32[]{:S(2)}, u32[]{:S(2)}) collective-permute-start(bf16[4,32,1664]{2,1,0:T(8,128)(2,1)} %get-tuple-element.302), channel_id=1, source_target_pairs={{0,4},{4,0},{1,5},{5,1},{2,6},{6,2},{3,7},{7,3},{8,12},{12,8},{9,1... | collective-permute-start | bytes 1277960 | tf_op jit(solution)/shard_map/ppermute | solution.py:246
  246.6 13.5 %collective-permute-start.46 = (bf16[320,512]{1,0:T(8,128)(2,1)}, bf16[320,512]{1,0:T(8,128)(2,1)S(1)}, u32[]{:S(2)}, u32[]{:S(2)}) collective-permute-start(bf16[320,512]{1,0:T(8,128)(2,1)} %get-tuple-element.317), channel_id=1, source_target_pairs={{0,2},{1,3},{2,0},{3,1},{4,6},{5,7},{6,4},{7,5},{8,10},{9,11},{10,... | collective-permute-start | bytes 983048 | tf_op jit(solution)/shard_map/ppermute | solution.py:241
  247.2 12.9 %collective-permute-start.47 = (bf16[320,512]{1,0:T(8,128)(2,1)}, bf16[320,512]{1,0:T(8,128)(2,1)S(1)}, u32[]{:S(2)}, u32[]{:S(2)}) collective-permute-start(bf16[320,512]{1,0:T(8,128)(2,1)} %get-tuple-element.318), channel_id=1, source_target_pairs={{0,4},{4,0},{1,5},{5,1},{2,6},{6,2},{3,7},{7,3},{8,12},{12,8},{9,1... | collective-permute-start | bytes 983048 | tf_op jit(solution)/shard_map/ppermute | solution.py:246
  248.7 12.9 %collective-permute-start.48 = (bf16[320,512]{1,0:T(8,128)(2,1)}, bf16[320,512]{1,0:T(8,128)(2,1)S(1)}, u32[]{:S(2)}, u32[]{:S(2)}) collective-permute-start(bf16[320,512]{1,0:T(8,128)(2,1)} %get-tuple-element.319), channel_id=1, source_target_pairs={{0,4},{4,0},{1,5},{5,1},{2,6},{6,2},{3,7},{7,3},{8,12},{12,8},{9,1... | collective-permute-start | bytes 983048 | tf_op jit(solution)/shard_map/ppermute | solution.py:246
  251.6 19.7 %collective-permute-start.58 = (bf16[72,1664]{1,0:T(8,128)(2,1)}, bf16[72,1664]{1,0:T(8,128)(2,1)}, u32[]{:S(2)}, u32[]{:S(2)}) collective-permute-start(bf16[72,1664]{1,0:T(8,128)(2,1)} %get-tuple-element.389), channel_id=1, source_target_pairs={{0,8},{8,16},{16,24},{24,0},{1,9},{9,17},{17,25},{25,1},{2,10},{10... | collective-permute-start | bytes 718856 | tf_op jit(solution)/shard_map/ppermute | solution.py:246
  264.4 14.3 %collective-permute-start.59 = (bf16[72,1664]{1,0:T(8,128)(2,1)}, bf16[72,1664]{1,0:T(8,128)(2,1)}, u32[]{:S(2)}, u32[]{:S(2)}) collective-permute-start(bf16[72,1664]{1,0:T(8,128)(2,1)} %get-tuple-element.390), channel_id=1, source_target_pairs={{0,16},{8,24},{16,0},{24,8},{1,17},{9,25},{17,1},{25,9},{2,18},{10... | collective-permute-start | bytes 718856 | tf_op jit(solution)/shard_map/ppermute | solution.py:246
  264.9 13.8 %collective-permute-start.60 = (bf16[72,1664]{1,0:T(8,128)(2,1)}, bf16[72,1664]{1,0:T(8,128)(2,1)}, u32[]{:S(2)}, u32[]{:S(2)}) collective-permute-start(bf16[72,1664]{1,0:T(8,128)(2,1)} %get-tuple-element.388), channel_id=1, source_target_pairs={{0,24},{8,0},{16,8},{24,16},{1,25},{9,1},{17,9},{25,17},{2,26},{10... | collective-permute-start | bytes 718856 | tf_op jit(solution)/shard_map/ppermute | solution.py:246
  278.7 15.8 %collective-permute-start.49 = (f32[256,512]{1,0:T(8,128)}, f32[256,512]{1,0:T(8,128)S(1)}, u32[]{:S(2)}, u32[]{:S(2)}) collective-permute-start(f32[256,512]{1,0:T(8,128)} %get-tuple-element.384), channel_id=1, source_target_pairs={{0,1},{1,0},{2,3},{3,2},{4,5},{5,4},{6,7},{7,6},{8,9},{9,8},{10,11... | collective-permute-start | bytes 1572872 | tf_op jit(solution)/shard_map/ppermute | solution.py:236
  (111 other events, 648.0 us)

commit v6 on v5

--- a/solution.py
+++ b/solution.py
@@ -307,7 +307,7 @@
 
 
 def add_many(left, right):
-    steps = left[0].shape[0]
+    steps = max(1, left[0].shape[0] // 2)
     if sum(part.size for part in left) < 2**20:
         steps = 1
 

time: 300 us -> 299 us (level)
  no operation moved by 1% of the time
where the time goes in v6:
time: 299 us; the launch traced here: 295 us
  Pallas kernels  116 us (39%)
  starting transfers between devices  53.5 us (18%)
  matrix products  49 us (16%)
  waiting for transfers between devices  28.8 us (10%)
  other arithmetic  25.1 us (8%)
  local copies, waits for them, and re-layouts  20.1 us (7%)
    pallas_call x5, Pallas kernels, attend_call(): pl.pallas_call(functools.partial(body, each), grid=(steps,), in_specs=spe...  64 us
    dot_general x28, matrix products, contract(): lax.dot_general(left, right, (((left_dim,), (right_dim,)), ((), ())), pre...  49 us
    ppermute x21, starting transfers between devices, shift(): lax.ppermute(value, axis, [(i, (i + step) % total) for i in range(total)])  28 us
    pallas_call x7, Pallas kernels, move(): pl.pallas_call(body, in_specs=[pl.BlockSpec(memory_space=pl.ANY)] * len(s...  27 us
    pallas_call x4, Pallas kernels, add_many(): pl.pallas_call(add_kernel, grid=(steps,), in_specs=[spec(part) for part i...  12.2 us
    ppermute x21, waiting for transfers between devices, shift(): lax.ppermute(value, axis, [(i, (i + step) % total) for i in range(total)])  10.9 us
    ppermute x9, starting transfers between devices, shift_plane(): return lax.ppermute(value, ('ctx', 'tp'), pairs)  10.5 us
    ppermute x9, waiting for transfers between devices, shift_plane(): return lax.ppermute(value, ('ctx', 'tp'), pairs)  9.58 us
  transfers between devices with their start and end apart: 64, of which 16 were waited for; matrix products, arithmetic and copies ran while one was open for 23% of the time, Pallas kernels for 32%

profile of v6, /device:TPU:0, one launch (start us, length us, event | category | flops | bytes accessed | tf_op | source)
XLA Modules:
  0.0 295.1 jit_solution(17946759220941291983)
XLA Ops:
  4.8 2.9 collective-permute-start.5
  7.8 2.6 collective-permute-start.6
  37.9 2.4 collective-permute-start.12
  42.2 3.6 %collective-permute-done.8.refs_6_ = bf16[320,512]{1,0:T(8,128)(2,1)S(1)} collective-permute-done((bf16[320,512]{1,0:T(8,128)(2,1)S(1)}, bf16[320,512]{1,0:T(8,128)(2,1)S(1)}, u32[]{:S(2)}, u32[]{:S(2)}) %collective-permute-start.8) | collective-permute-done | bytes 327712 | tf_op jit(solution)/shard_map/ppermute | solution.py:246
  48.0 3.3 %rows_together.1 = (bf16[2048,512]{1,0:T(8,128)(2,1)}, bf16[512,512]{1,0:T(8,128)(2,1)}) custom-call(bf16[320,512]{1,0:T(8,128)(2,1)} %get-tuple-element.197.refs_0_, bf16[320,512]{1,0:T(8,128)(2,1)} %copy-done.36, bf16[320,512]{1,0:T(8,128)(2,1)} %copy-done.37, bf16[320,512]{1,0:T(8,128)(2,1)} %copy-done.39, bf16[320,512]{1,0:T(8,128)(2,1)} %copy-done.38, ...), custom_call_target="tpu_custom_call" | custom-call | tf_op jit(solution)/shard_map/rows_together/pallas_call | solution.py:210
  59.1 2.8 place_first.1
  62.0 3.7 %convolution_convert_fusion.2.k = bf16[2048,512]{1,0:T(8,128)(2,1)} fusion(bf16[2048,512]{1,0:T(8,128)(2,1)S(1)} %copy-done, bf16[512,512]{1,0:T(8,128)(2,1)} %bitcast.147), kind=kOutput, calls=%fused_computation.7 | convolution fusion | flops 1074790400 | bytes 4718592 | tf_op jit(solution)/shard_map/dot_general | solution.py:20
  65.7 2.6 add_convert_fusion.v
  69.5 21.2 %attend.2 = (bf16[512,512]{1,0:T(8,128)(2,1)}, f32[512,512]{1,0:T(8,128)}, bf16[8,2048,512]{2,1,0:T(8,128)(2,1)}) custom-call(bf16[512,512]{1,0:T(8,128)(2,1)} %fusion.2.q, bf16[2048,512]{1,0:T(8,128)(2,1)} %convolution_convert_fusion.2.k, bf16[2048,512]{1,0:T(8,128)(2,1)} %add_convert_fusion.v, s32[1,512]{1,0:T(1,128)} %bitcast.181, ...), custom_call_target="tpu_custom_call" | custom-call | flops 8589934592 | bytes 16777216 | tf_op jit(solution)/shard_map/attend/pallas_call | solution.py:97
  90.7 4.1 %collective-permute-done.14.refs_2_ = bf16[4,64,1664]{2,1,0:T(8,128)(2,1)} collective-permute-done((bf16[4,64,1664]{2,1,0:T(8,128)(2,1)}, bf16[4,64,1664]{2,1,0:T(8,128)(2,1)}, u32[]{:S(2)}, u32[]{:S(2)}) %collective-permute-start.14) | collective-permute-done | bytes 852000 | tf_op jit(solution)/shard_map/ppermute | solution.py:266
  101.1 6.4 %place_second.1 = (bf16[4,2,64,512]{3,2,1,0:T(8,128)(2,1)}, bf16[4,2,64,512]{3,2,1,0:T(8,128)(2,1)}, bf16[4,2,64,512]{3,2,1,0:T(8,128)(2,1)}, bf16[4,2,64,512]{3...) custom-call(bf16[4,64,1664]{2,1,0:T(8,128)(2,1)} %stack_second.1.ref, ...), custom_call_target="tpu_custom_call" | custom-call | tf_op jit(solution)/shard_map/place_second/pallas_call | solution.py:210
  114.0 8.9 %attend.3 = (bf16[512,512]{1,0:T(8,128)(2,1)}, f32[512,512]{1,0:T(8,128)}, bf16[8,512,512]{2,1,0:T(8,128)(2,1)}) custom-call(bf16[512,512]{1,0:T(8,128)(2,1)} %fusion.3.q, bf16[512,512]{1,0:T(8,128)(2,1)} %convolution_convert_fusion.13.k, bf16[512,512]{1,0:T(8,128)(2,1)} %fusion.4.v, s32[1,512]{1,0:T(1,128)} %broadcast_in_dim.20.qp, s32[512,1]{1,0:T(8,128)} %copy.84.kp), custom_call_target="tpu_custom_call" | custom-call | flops 2147483648 | bytes 4194304 | tf_op jit(solution)/shard_map/attend/pallas_call | solution.py:97
  132.0 2.4 convert_reduce_fusion
  138.9 8.7 %attend_back.3 = (bf16[512,512]{1,0:T(8,128)(2,1)}, bf16[512,512]{1,0:T(8,128)(2,1)}, bf16[512,512]{1,0:T(8,128)(2,1)}, f32[1,512]{1,0:T(1,128)}, f32[1,512]{1,0:T(1,128)}) custom-call(bf16[512,512]{1,0:T(8,128)(2,1)} %fusion.3.q, bf16[512,512]{1,0:T(8,128)(2,1)} %convolution_convert_fusion.13.k, bf16[512,512]{1,0:T(8,128)(2,1)} %fusion.4.v, ...), custom_call_target="tpu_custom_call" | custom-call | flops 4294967296 | bytes 4194304 | tf_op jit(solution)/shard_map/attend_back/pallas_call | solution.py:97
  147.6 2.7 multiply_reduce_fusion.2
  153.0 2.7 convolution_convert_fusion.1
  155.7 2.7 convolution_convert_fusion
  166.5 7.6 %split_second.1 = (bf16[4,40,1664]{2,1,0:T(8,128)(2,1)}, bf16[4,32,1664]{2,1,0:T(8,128)(2,1)}, bf16[4,40,1664]{2,1,0:T(8,128)(2,1)}, bf16[4,32,1664]{2,1,0:T(8,1...) custom-call(bf16[4,2,64,512]{3,2,1,0:T(8,128)(2,1)} %bitcast.162, ...), custom_call_target="tpu_custom_call" | custom-call | tf_op jit(solution)/shard_map/split_second/pallas_call | solution.py:210
  181.0 2.3 maximum_select_fusion
  183.4 4.9 %add_many.4 = (bf16[4,40,1664]{2,1,0:T(8,128)(2,1)}, bf16[4,32,1664]{2,1,0:T(8,128)(2,1)}, bf16[4,40,1664]{2,1,0:T(8,128)(2,1)}, bf16[4,32,1664]{2,1,0:T(8,128)(...) custom-call(bf16[4,40,1664]{2,1,0:T(8,128)(2,1)} %get-tuple-element., ...), custom_call_target="tpu_custom_call" | custom-call | tf_op jit(solution)/shard_map/add_many/pallas_call | solution.py:318
  190.5 12.7 %attend_back.4 = (bf16[512,512]{1,0:T(8,128)(2,1)}, bf16[2048,512]{1,0:T(8,128)(2,1)}, bf16[2048,512]{1,0:T(8,128)(2,1)}, f32[1,512]{1,0:T(1,128)}, f32[1,512]{1,0:T(1,128)}) custom-call(bf16[512,512]{1,0:T(8,128)(2,1)} %fusion.2.q, bf16[2048,512]{1,0:T(8,128)(2,1)} %convolution_convert_fusion.2.k, bf16[2048,512]{1,0:T(8,128)(2,1)} %add_convert_fusion.v, ...), custom_call_target="tpu_custom_call" | custom-call | flops 8589934592 | bytes 8388608 | tf_op jit(solution)/shard_map/attend_back/pallas_call | solution.py:97
  203.3 2.6 add_many.5
  209.9 12.6 %attend_back.5 = (bf16[512,512]{1,0:T(8,128)(2,1)}, bf16[2048,512]{1,0:T(8,128)(2,1)}, bf16[2048,512]{1,0:T(8,128)(2,1)}, f32[1,512]{1,0:T(1,128)}, f32[1,512]{1,0:T(1,128)}) custom-call(bf16[512,512]{1,0:T(8,128)(2,1)} %fusion.2.q, ...), custom_call_target="tpu_custom_call", output_to_operand_aliasing={{0}: (6, {}), {1}: (7, {}), {2}: (8, {}), {3}: (9, {}), {4}... | custom-call | flops 8589934592 | bytes 8388608 | tf_op jit(solution)/shard_map/attend_back/pallas_call | solution.py:97
  223.8 7.8 %row_grads.1 = (f32[512,512]{1,0:T(8,128)}, f32[128,512]{1,0:T(8,128)}, bf16[320,512]{1,0:T(8,128)(2,1)}, bf16[320,512]{1,0:T(8,128)(2,1)}, bf16[320,512]{1,0:T(...) custom-call(bf16[2048,512]{1,0:T(8,128)(2,1)} %get-tuple-element.314.dk, ...), custom_call_target="tpu_custom_call" | custom-call | tf_op jit(solution)/shard_map/row_grads/pallas_call | solution.py:599
  235.8 2.3 add_convert_fusion.1
  251.5 3.1 %split_first.1 = (bf16[4,72,384]{2,1,0:T(8,128)(2,1)}, bf16[4,72,384]{2,1,0:T(8,128)(2,1)}, bf16[4,72,384]{2,1,0:T(8,128)(2,1)}, bf16[4,72,384]{2,1,0:T(8,128)(2...) custom-call(bf16[4,2,64,512]{3,2,1,0:T(8,128)(2,1)} %bitcast.154, ...), custom_call_target="tpu_custom_call" | custom-call | tf_op jit(solution)/shard_map/split_first/pallas_call | solution.py:210
  255.3 4.2 %collective-permute-done.46 = bf16[320,512]{1,0:T(8,128)(2,1)S(1)} collective-permute-done((bf16[320,512]{1,0:T(8,128)(2,1)}, bf16[320,512]{1,0:T(8,128)(2,1)S(1)}, u32[]{:S(2)}, u32[]{:S(2)}) %collective-permute-start.46) | collective-permute-done | bytes 327712 | tf_op jit(solution)/shard_map/ppermute | solution.py:241
  264.2 2.6 collective-permute-start.60
  266.8 2.5 add_many.7
  272.8 2.5 fusion.10
  278.0 2.5 collective-permute-done.56
  289.2 2.4 collective-permute-done.62
  (372 shorter events, 136.3 us)
Async XLA Ops:
  4.8 11.1 %collective-permute-start.5 = (bf16[64,384]{1,0:T(8,128)(2,1)}, bf16[64,384]{1,0:T(8,128)(2,1)S(1)}, u32[]{:S(2)}, u32[]{:S(2)}) collective-permute-start(bf16[64,384]{1,0:T(8,128)(2,1)} %get-tuple-element.196.refs_0_), channel_id=1, source_target_pairs={{0,8},{8,16},{16,24},{24,0},{1,9},{9,17},{17,25},{25,1},{2,10},{10... | collective-permute-start | bytes 147464 | tf_op jit(solution)/shard_map/ppermute | solution.py:246
  11.7 12.2 %collective-permute-start.1 = (bf16[320,512]{1,0:T(8,128)(2,1)}, bf16[320,512]{1,0:T(8,128)(2,1)S(1)}, u32[]{:S(2)}, u32[]{:S(2)}) collective-permute-start(bf16[320,512]{1,0:T(8,128)(2,1)} %get-tuple-element.197.refs_0_), channel_id=1, source_target_pairs={{0,2},{1,3},{2,0},{3,1},{4,6},{5,7},{6,4},{7,5},{8,10},{9,11},{10,... | collective-permute-start | bytes 983048 | tf_op jit(solution)/shard_map/ppermute | solution.py:241
  13.2 13.0 %collective-permute-start.3 = (bf16[320,512]{1,0:T(8,128)(2,1)}, bf16[320,512]{1,0:T(8,128)(2,1)S(1)}, u32[]{:S(2)}, u32[]{:S(2)}) collective-permute-start(bf16[320,512]{1,0:T(8,128)(2,1)} %get-tuple-element.197.refs_0_), channel_id=1, source_target_pairs={{0,4},{4,0},{1,5},{5,1},{2,6},{6,2},{3,7},{7,3},{8,12},{12,8},{9,1... | collective-permute-start | bytes 983048 | tf_op jit(solution)/shard_map/ppermute | solution.py:246
  15.9 11.9 %collective-permute-start.2 = (bf16[320,512]{1,0:T(8,128)(2,1)S(1)}, bf16[320,512]{1,0:T(8,128)(2,1)S(1)}, u32[]{:S(2)}, u32[]{:S(2)}) collective-permute-start(bf16[320,512]{1,0:T(8,128)(2,1)S(1)} %collective-permute-done.refs_1_), channel_id=1, source_target_pairs={{0,2},{1,3},{2,0},{3,1},{4,6},{5,7},{6,4},{7,5},{8,10},{9,11},{10,... | collective-permute-start | bytes 983048 | tf_op jit(solution)/shard_map/ppermute | solution.py:241
  16.5 12.6 %collective-permute-start.4 = (bf16[320,512]{1,0:T(8,128)(2,1)S(1)}, bf16[320,512]{1,0:T(8,128)(2,1)S(1)}, u32[]{:S(2)}, u32[]{:S(2)}) collective-permute-start(bf16[320,512]{1,0:T(8,128)(2,1)S(1)} %collective-permute-done.refs_1_), channel_id=1, source_target_pairs={{0,4},{4,0},{1,5},{5,1},{2,6},{6,2},{3,7},{7,3},{8,12},{12,8},{9,1... | collective-permute-start | bytes 983048 | tf_op jit(solution)/shard_map/ppermute | solution.py:246
  17.0 15.5 %collective-permute-start.10 = (bf16[64,1664]{1,0:T(8,128)(2,1)}, bf16[64,1664]{1,0:T(8,128)(2,1)S(1)}, u32[]{:S(2)}, u32[]{:S(2)}) collective-permute-start(bf16[64,1664]{1,0:T(8,128)(2,1)} %get-tuple-element.206.refs_0_), channel_id=1, source_target_pairs={{0,8},{8,16},{16,24},{24,0},{1,9},{9,17},{17,25},{25,1},{2,10},{10... | collective-permute-start | bytes 638984 | tf_op jit(solution)/shard_map/ppermute | solution.py:246
  29.6 12.1 %collective-permute-start.17 = (bf16[4,64,384]{2,1,0:T(8,128)(2,1)}, bf16[4,64,384]{2,1,0:T(8,128)(2,1)}, u32[]{:S(2)}, u32[]{:S(2)}) collective-permute-start(bf16[4,64,384]{2,1,0:T(8,128)(2,1)} %stack_first.1.refs_0_), channel_id=1, source_target_pairs={{0,4},{1,5},{2,6},{3,7},{4,0},{5,1},{6,2},{7,3},{8,12},{9,13},{10,... | collective-permute-start | bytes 589832 | tf_op jit(solution)/shard_map/ppermute | solution.py:266
  32.5 13.3 %collective-permute-start.8 = (bf16[320,512]{1,0:T(8,128)(2,1)S(1)}, bf16[320,512]{1,0:T(8,128)(2,1)S(1)}, u32[]{:S(2)}, u32[]{:S(2)}) collective-permute-start(bf16[320,512]{1,0:T(8,128)(2,1)S(1)} %collective-permute-done.1.refs_2_), channel_id=1, source_target_pairs={{0,4},{4,0},{1,5},{5,1},{2,6},{6,2},{3,7},{7,3},{8,12},{12,8},{9,1... | collective-permute-start | bytes 983048 | tf_op jit(solution)/shard_map/ppermute | solution.py:246
  34.9 11.0 %collective-permute-start.9 = (bf16[320,512]{1,0:T(8,128)(2,1)S(1)}, bf16[320,512]{1,0:T(8,128)(2,1)}, u32[]{:S(2)}, u32[]{:S(2)}) collective-permute-start(bf16[320,512]{1,0:T(8,128)(2,1)S(1)} %collective-permute-done.4.refs_5_), channel_id=1, source_target_pairs={{0,2},{1,3},{2,0},{3,1},{4,6},{5,7},{6,4},{7,5},{8,10},{9,11},{10,... | collective-permute-start | bytes 983048 | tf_op jit(solution)/shard_map/ppermute | solution.py:241
  37.9 13.4 %collective-permute-start.12 = (bf16[64,1664]{1,0:T(8,128)(2,1)}, bf16[64,1664]{1,0:T(8,128)(2,1)S(1)}, u32[]{:S(2)}, u32[]{:S(2)}) collective-permute-start(bf16[64,1664]{1,0:T(8,128)(2,1)} %get-tuple-element.206.refs_0_), channel_id=1, source_target_pairs={{0,24},{8,0},{16,8},{24,16},{1,25},{9,1},{17,9},{25,17},{2,26},{10... | collective-permute-start | bytes 638984 | tf_op jit(solution)/shard_map/ppermute | solution.py:246
  41.7 14.0 %collective-permute-start.19 = (bf16[4,64,384]{2,1,0:T(8,128)(2,1)}, bf16[4,64,384]{2,1,0:T(8,128)(2,1)S(1)}, u32[]{:S(2)}, u32[]{:S(2)}) collective-permute-start(bf16[4,64,384]{2,1,0:T(8,128)(2,1)} %stack_first.1.refs_0_), channel_id=1, source_target_pairs={{0,1},{1,0},{2,3},{3,2},{4,5},{5,4},{6,7},{7,6},{8,9},{9,8},{10,11... | collective-permute-start | bytes 589832 | tf_op jit(solution)/shard_map/ppermute | solution.py:236
  41.7 15.5 %collective-permute-start.20 = (bf16[4,64,384]{2,1,0:T(8,128)(2,1)}, bf16[4,64,384]{2,1,0:T(8,128)(2,1)S(1)}, u32[]{:S(2)}, u32[]{:S(2)}) collective-permute-start(bf16[4,64,384]{2,1,0:T(8,128)(2,1)} %collective-permute-done.16.refs_1_), channel_id=1, source_target_pairs={{0,1},{1,0},{2,3},{3,2},{4,5},{5,4},{6,7},{7,6},{8,9},{9,8},{10,11... | collective-permute-start | bytes 589832 | tf_op jit(solution)/shard_map/ppermute | solution.py:236
  45.8 12.0 %collective-permute-start.21 = (bf16[4,64,384]{2,1,0:T(8,128)(2,1)}, bf16[4,64,384]{2,1,0:T(8,128)(2,1)S(1)}, u32[]{:S(2)}, u32[]{:S(2)}) collective-permute-start(bf16[4,64,384]{2,1,0:T(8,128)(2,1)} %collective-permute-done.17.refs_2_), channel_id=1, source_target_pairs={{0,1},{1,0},{2,3},{3,2},{4,5},{5,4},{6,7},{7,6},{8,9},{9,8},{10,11... | collective-permute-start | bytes 589832 | tf_op jit(solution)/shard_map/ppermute | solution.py:236
  45.8 12.0 %collective-permute-start.22 = (bf16[4,64,384]{2,1,0:T(8,128)(2,1)}, bf16[4,64,384]{2,1,0:T(8,128)(2,1)S(1)}, u32[]{:S(2)}, u32[]{:S(2)}) collective-permute-start(bf16[4,64,384]{2,1,0:T(8,128)(2,1)} %collective-permute-done.18.refs_3_), channel_id=1, source_target_pairs={{0,1},{1,0},{2,3},{3,2},{4,5},{5,4},{6,7},{7,6},{8,9},{9,8},{10,11... | collective-permute-start | bytes 589832 | tf_op jit(solution)/shard_map/ppermute | solution.py:236
  54.2 36.5 %collective-permute-start.13 = (bf16[4,64,1664]{2,1,0:T(8,128)(2,1)}, bf16[4,64,1664]{2,1,0:T(8,128)(2,1)}, u32[]{:S(2)}, u32[]{:S(2)}) collective-permute-start(bf16[4,64,1664]{2,1,0:T(8,128)(2,1)} %stack_second.1.refs_0_), channel_id=1, source_target_pairs={{0,2},{1,3},{2,0},{3,1},{4,6},{5,7},{6,4},{7,5},{8,10},{9,11},{10,... | collective-permute-start | bytes 2555912 | tf_op jit(solution)/shard_map/ppermute | solution.py:266
  55.7 39.2 %collective-permute-start.14 = (bf16[4,64,1664]{2,1,0:T(8,128)(2,1)}, bf16[4,64,1664]{2,1,0:T(8,128)(2,1)}, u32[]{:S(2)}, u32[]{:S(2)}) collective-permute-start(bf16[4,64,1664]{2,1,0:T(8,128)(2,1)} %stack_second.1.refs_0_), channel_id=1, source_target_pairs={{0,4},{1,5},{2,6},{3,7},{4,0},{5,1},{6,2},{7,3},{8,12},{9,13},{10,... | collective-permute-start | bytes 2555912 | tf_op jit(solution)/shard_map/ppermute | solution.py:266
  57.2 37.7 %collective-permute-start.15 = (bf16[4,64,1664]{2,1,0:T(8,128)(2,1)}, bf16[4,64,1664]{2,1,0:T(8,128)(2,1)}, u32[]{:S(2)}, u32[]{:S(2)}) collective-permute-start(bf16[4,64,1664]{2,1,0:T(8,128)(2,1)} %stack_second.1.refs_0_), channel_id=1, source_target_pairs={{0,6},{1,7},{2,4},{3,5},{4,2},{5,3},{6,0},{7,1},{8,14},{9,15},{10,... | collective-permute-start | bytes 2555912 | tf_op jit(solution)/shard_map/ppermute | solution.py:266
  97.7 31.1 %collective-permute-start.28 = (bf16[256,512]{1,0:T(8,128)(2,1)}, bf16[256,512]{1,0:T(8,128)(2,1)S(1)}, u32[]{:S(2)}, u32[]{:S(2)}) collective-permute-start(bf16[256,512]{1,0:T(8,128)(2,1)} %get-tuple-element.392), channel_id=1, source_target_pairs={{0,1},{1,0},{2,3},{3,2},{4,5},{5,4},{6,7},{7,6},{8,9},{9,8},{10,11... | collective-permute-start | bytes 786440 | tf_op jit(solution)/shard_map/ppermute | solution.py:236
  159.5 18.7 %collective-permute-start.27 = (f32[256,512]{1,0:T(8,128)}, f32[256,512]{1,0:T(8,128)}, u32[]{:S(2)}, u32[]{:S(2)}) collective-permute-start(f32[256,512]{1,0:T(8,128)} %get-tuple-element.387), channel_id=1, source_target_pairs={{0,1},{1,0},{2,3},{3,2},{4,5},{5,4},{6,7},{7,6},{8,9},{9,8},{10,11... | collective-permute-start | bytes 1572872 | tf_op jit(solution)/shard_map/ppermute | solution.py:236
  188.3 15.0 %collective-permute-start.37 = (bf16[4,40,1664]{2,1,0:T(8,128)(2,1)}, bf16[4,40,1664]{2,1,0:T(8,128)(2,1)}, u32[]{:S(2)}, u32[]{:S(2)}) collective-permute-start(bf16[4,40,1664]{2,1,0:T(8,128)(2,1)} %get-tuple-element.269), channel_id=1, source_target_pairs={{0,4},{4,0},{1,5},{5,1},{2,6},{6,2},{3,7},{7,3},{8,12},{12,8},{9,1... | collective-permute-start | bytes 1597448 | tf_op jit(solution)/shard_map/ppermute | solution.py:246
  189.9 13.4 %collective-permute-start.38 = (bf16[4,32,1664]{2,1,0:T(8,128)(2,1)}, bf16[4,32,1664]{2,1,0:T(8,128)(2,1)}, u32[]{:S(2)}, u32[]{:S(2)}) collective-permute-start(bf16[4,32,1664]{2,1,0:T(8,128)(2,1)} %get-tuple-element.270), channel_id=1, source_target_pairs={{0,2},{1,3},{2,0},{3,1},{4,6},{5,7},{6,4},{7,5},{8,10},{9,11},{10,... | collective-permute-start | bytes 1277960 | tf_op jit(solution)/shard_map/ppermute | solution.py:241
  205.9 25.8 %collective-permute-start.39 = (bf16[4,40,1664]{2,1,0:T(8,128)(2,1)}, bf16[4,40,1664]{2,1,0:T(8,128)(2,1)}, u32[]{:S(2)}, u32[]{:S(2)}) collective-permute-start(bf16[4,40,1664]{2,1,0:T(8,128)(2,1)} %get-tuple-element.299), channel_id=1, source_target_pairs={{0,2},{1,3},{2,0},{3,1},{4,6},{5,7},{6,4},{7,5},{8,10},{9,11},{10,... | collective-permute-start | bytes 1597448 | tf_op jit(solution)/shard_map/ppermute | solution.py:241
  207.2 24.4 %collective-permute-start.40 = (bf16[4,32,1664]{2,1,0:T(8,128)(2,1)}, bf16[4,32,1664]{2,1,0:T(8,128)(2,1)}, u32[]{:S(2)}, u32[]{:S(2)}) collective-permute-start(bf16[4,32,1664]{2,1,0:T(8,128)(2,1)} %get-tuple-element.300), channel_id=1, source_target_pairs={{0,2},{1,3},{2,0},{3,1},{4,6},{5,7},{6,4},{7,5},{8,10},{9,11},{10,... | collective-permute-start | bytes 1277960 | tf_op jit(solution)/shard_map/ppermute | solution.py:241
  207.9 23.8 %collective-permute-start.41 = (bf16[4,40,1664]{2,1,0:T(8,128)(2,1)}, bf16[4,40,1664]{2,1,0:T(8,128)(2,1)}, u32[]{:S(2)}, u32[]{:S(2)}) collective-permute-start(bf16[4,40,1664]{2,1,0:T(8,128)(2,1)} %get-tuple-element.301), channel_id=1, source_target_pairs={{0,4},{4,0},{1,5},{5,1},{2,6},{6,2},{3,7},{7,3},{8,12},{12,8},{9,1... | collective-permute-start | bytes 1597448 | tf_op jit(solution)/shard_map/ppermute | solution.py:246
  209.2 22.5 %collective-permute-start.42 = (bf16[4,32,1664]{2,1,0:T(8,128)(2,1)}, bf16[4,32,1664]{2,1,0:T(8,128)(2,1)}, u32[]{:S(2)}, u32[]{:S(2)}) collective-permute-start(bf16[4,32,1664]{2,1,0:T(8,128)(2,1)} %get-tuple-element.302), channel_id=1, source_target_pairs={{0,4},{4,0},{1,5},{5,1},{2,6},{6,2},{3,7},{7,3},{8,12},{12,8},{9,1... | collective-permute-start | bytes 1277960 | tf_op jit(solution)/shard_map/ppermute | solution.py:246
  245.9 13.5 %collective-permute-start.46 = (bf16[320,512]{1,0:T(8,128)(2,1)}, bf16[320,512]{1,0:T(8,128)(2,1)S(1)}, u32[]{:S(2)}, u32[]{:S(2)}) collective-permute-start(bf16[320,512]{1,0:T(8,128)(2,1)} %get-tuple-element.317), channel_id=1, source_target_pairs={{0,2},{1,3},{2,0},{3,1},{4,6},{5,7},{6,4},{7,5},{8,10},{9,11},{10,... | collective-permute-start | bytes 983048 | tf_op jit(solution)/shard_map/ppermute | solution.py:241
  246.5 12.9 %collective-permute-start.47 = (bf16[320,512]{1,0:T(8,128)(2,1)}, bf16[320,512]{1,0:T(8,128)(2,1)S(1)}, u32[]{:S(2)}, u32[]{:S(2)}) collective-permute-start(bf16[320,512]{1,0:T(8,128)(2,1)} %get-tuple-element.318), channel_id=1, source_target_pairs={{0,4},{4,0},{1,5},{5,1},{2,6},{6,2},{3,7},{7,3},{8,12},{12,8},{9,1... | collective-permute-start | bytes 983048 | tf_op jit(solution)/shard_map/ppermute | solution.py:246
  248.0 12.9 %collective-permute-start.48 = (bf16[320,512]{1,0:T(8,128)(2,1)}, bf16[320,512]{1,0:T(8,128)(2,1)S(1)}, u32[]{:S(2)}, u32[]{:S(2)}) collective-permute-start(bf16[320,512]{1,0:T(8,128)(2,1)} %get-tuple-element.319), channel_id=1, source_target_pairs={{0,4},{4,0},{1,5},{5,1},{2,6},{6,2},{3,7},{7,3},{8,12},{12,8},{9,1... | collective-permute-start | bytes 983048 | tf_op jit(solution)/shard_map/ppermute | solution.py:246
  250.8 19.7 %collective-permute-start.58 = (bf16[72,1664]{1,0:T(8,128)(2,1)}, bf16[72,1664]{1,0:T(8,128)(2,1)}, u32[]{:S(2)}, u32[]{:S(2)}) collective-permute-start(bf16[72,1664]{1,0:T(8,128)(2,1)} %get-tuple-element.389), channel_id=1, source_target_pairs={{0,8},{8,16},{16,24},{24,0},{1,9},{9,17},{17,25},{25,1},{2,10},{10... | collective-permute-start | bytes 718856 | tf_op jit(solution)/shard_map/ppermute | solution.py:246
  263.7 14.3 %collective-permute-start.59 = (bf16[72,1664]{1,0:T(8,128)(2,1)}, bf16[72,1664]{1,0:T(8,128)(2,1)}, u32[]{:S(2)}, u32[]{:S(2)}) collective-permute-start(bf16[72,1664]{1,0:T(8,128)(2,1)} %get-tuple-element.390), channel_id=1, source_target_pairs={{0,16},{8,24},{16,0},{24,8},{1,17},{9,25},{17,1},{25,9},{2,18},{10... | collective-permute-start | bytes 718856 | tf_op jit(solution)/shard_map/ppermute | solution.py:246
  264.2 13.8 %collective-permute-start.60 = (bf16[72,1664]{1,0:T(8,128)(2,1)}, bf16[72,1664]{1,0:T(8,128)(2,1)}, u32[]{:S(2)}, u32[]{:S(2)}) collective-permute-start(bf16[72,1664]{1,0:T(8,128)(2,1)} %get-tuple-element.388), channel_id=1, source_target_pairs={{0,24},{8,0},{16,8},{24,16},{1,25},{9,1},{17,9},{25,17},{2,26},{10... | collective-permute-start | bytes 718856 | tf_op jit(solution)/shard_map/ppermute | solution.py:246
  278.0 15.8 %collective-permute-start.49 = (f32[256,512]{1,0:T(8,128)}, f32[256,512]{1,0:T(8,128)S(1)}, u32[]{:S(2)}, u32[]{:S(2)}) collective-permute-start(f32[256,512]{1,0:T(8,128)} %get-tuple-element.384), channel_id=1, source_target_pairs={{0,1},{1,0},{2,3},{3,2},{4,5},{5,4},{6,7},{7,6},{8,9},{9,8},{10,11... | collective-permute-start | bytes 1572872 | tf_op jit(solution)/shard_map/ppermute | solution.py:236
  (111 other events, 648.0 us)
